TPU v7x, 256 devices: a whole 4x4x8 slice. The times are simulated.
256 devices in a mesh: segment: 4 (over x), shard: 64 (over y, z, core).
Axes of the slice: x: 4, y: 4, z: 8, core: 2. Of those that a mesh axis runs over, the one named last changes fastest.
Arguments:
- tokens: bfloat16 [3, 128, 3072], P(None, 'shard'), may hold values from -6 to 6
- norm_gain: float32 [4, 3072], P('segment'), may hold values from 0.5 to 1.5
- w_gate: bfloat16 [4, 3072, 32768], P('segment', None, 'shard'), may hold values from -0.109375 to 0.109375
- w_up: bfloat16 [4, 3072, 32768], P('segment', None, 'shard'), may hold values from -0.109375 to 0.109375
- w_down: bfloat16 [4, 32768, 3072], P('segment', 'shard'), may hold values from -0.046875 to 0.046875
- block_counts: int32 [4], P('segment'), may hold values from 1 to 2
- gate_prob: float32 [4, 3, 128], P('segment', None, 'shard'), may hold values from 0.1 to 1
Outputs:
- section_outputs: bfloat16 [4, 3, 128, 3072], P('segment', None, 'shard')
All inputs are finite; a program needn't handle non-finite values.
Results may differ from a plain program's by a relative error of at most 0.009.
Values may be sent and summed in bfloat16 or wider, within the bound.
A program may use at most 64 MiB of HBM per device.

v0:
```python
import jax
import jax.numpy as jnp
from jax import lax
from jax.sharding import PartitionSpec as P

FF = 16384


def shifted(value, axis, steps):
    count = lax.axis_size(axis)
    initial, last = (max(0, -steps), min(count, count - steps))
    return lax.ppermute(value, axis, [(source, source + steps) for source in range(initial, last)])


def normalize(rows, row_gain):
    values = rows.astype(jnp.float32)
    scale = lax.rsqrt(jnp.mean(values * values, axis=-1, keepdims=True) + 1e-05)
    return (values * scale * row_gain).astype(jnp.bfloat16)


def expert_rows(normed, gate_part, up_part, down_part):
    gate_val = jnp.dot(normed, gate_part, preferred_element_type=jnp.float32)
    up_val = jnp.dot(normed, up_part, preferred_element_type=jnp.float32)
    hidden = (jax.nn.silu(gate_val) * up_val).astype(jnp.bfloat16)
    return jnp.dot(hidden, down_part, preferred_element_type=jnp.float32)


def shards(tokens, norm_gain, w_gate, w_up, w_down, block_counts, gate_prob):
    segment_index = lax.axis_index("segment")
    segment_count = lax.axis_size("segment")
    shard_count = lax.axis_size("shard")
    hidden_count = w_gate.shape[2]
    own_expert = lax.axis_index("shard") // (FF // hidden_count)
    zero_blocks = block_counts[0]
    row_gain = norm_gain[0]
    gate_part = w_gate[0]
    up_part = w_up[0]
    down_part = w_down[0]
    probs = gate_prob[0]
    block_total = tokens.shape[0]
    local_rows = tokens.shape[1]
    width = tokens.shape[2]
    first_block = jnp.where(own_expert == 0, 0, zero_blocks)
    last_block = jnp.where(own_expert == 0, zero_blocks, block_total)
    carried = tokens
    stored = jnp.zeros_like(tokens)
    for tick in range(segment_count):
        normed = normalize(carried, row_gain)
        gathered = lax.all_gather(normed, "shard", axis=1, tiled=True)
        partial_sum = jnp.zeros(gathered.shape, jnp.float32)

        def add_block(block_id, acc):
            block_rows = lax.dynamic_index_in_dim(gathered, block_id, 0, keepdims=False)
            result = expert_rows(block_rows, gate_part, up_part, down_part)
            return lax.dynamic_update_index_in_dim(acc, result, block_id, 0)

        partial_sum = lax.fori_loop(first_block, last_block, add_block, partial_sum)
        split_terms = partial_sum.reshape(block_total, shard_count, local_rows, width)
        received = lax.all_to_all(split_terms, "shard", split_axis=1, concat_axis=1, tiled=True)
        mixed = jnp.sum(received, axis=1)
        updated = (carried.astype(jnp.float32) + probs[:, :, None] * mixed).astype(jnp.bfloat16)
        stored = jnp.where(segment_index == tick, updated, stored)
        if tick + 1 < segment_count:
            carried = shifted(updated, "segment", 1)
    return stored[None]


def solution(mesh):
    placed = (
        P(None, "shard", None),
        P("segment", None),
        P("segment", None, "shard"),
        P("segment", None, "shard"),
        P("segment", "shard", None),
        P("segment"),
        P("segment", None, "shard"),
    )
    return jax.shard_map(
        shards,
        mesh=mesh,
        in_specs=placed,
        out_specs=P("segment", None, "shard", None),
        check_vma=False,
    )
```

profile of v0, /device:TPU:1, one launch (start us, length us, event | category | flops | bytes accessed | tf_op | source)
XLA Modules:
  0.0 946.6 jit_solution(11908347532508689451)
XLA Ops:
  9.6 83.1 %all-gather.5.cloned.1.call-done = bf16[3,128,3072]{2,0,1:T(4,128)(2,1)} async-done(((bf16[3,2,3072]{2,0,1:T(4,128)(2,1)}), bf16[3,128,3072]{2,0,1:T(4,128)(2,1)}) %all-gather.5.cloned.1.call-update) | async-done | bytes 2359312 | tf_op jit(solution)/shard_map/all_gather | solution.py:49
  92.7 4.2 copy.27
  99.7 14.2 %while.40 = (s32[]{:T(128)}, f32[3,128,3072]{2,1,0:T(8,128)}, s32[]{:T(128)}, bf16[3,128,3072]{2,1,0:T(8,128)(2,1)}, bf16[3072,512]{1,0:T(8,128)(2,1)S(1)}, /*in...) while((s32[]{:T(128)}, f32[3,128,3072]{2,1,0:T(8,128)}, ...), condition=%wide.region_2.3_spmd, body=%wide.region_1.2_spmd.sunk | while | flops 1208352768 | bytes 13108363 | solution.py:57
  101.5 5.4 fusion.139
  108.6 5.4 fusion.139
  113.9 6.6 reshape.46
  120.5 6.1 copy.28
  126.6 5.5 all-to-all-start
  132.3 107.0 %all-to-all-done = f32[3,64,2,3072]{3,2,0,1:T(2,128)} async-done(((f32[3,64,2,3072]{3,2,0,1:T(2,128)}), f32[3,64,2,3072]{3,2,0,1:T(2,128)}, u32[]{:S(2)}, u32[]{:S(2)}) %all-to-all-start) | async-done | bytes 4718624 | tf_op jit(solution)/shard_map/all_to_all | solution.py:59
  243.0 4.3 collective-permute-start
  249.3 77.1 %all-gather.7.cloned.1.call-done = bf16[3,128,3072]{2,0,1:T(4,128)(2,1)} async-done(((bf16[3,2,3072]{2,0,1:T(4,128)(2,1)}), bf16[3,128,3072]{2,0,1:T(4,128)(2,1)}) %all-gather.7.cloned.1.call-update) | async-done | bytes 2359312 | tf_op jit(solution)/shard_map/all_gather | solution.py:49
  333.3 14.2 %while.41 = (s32[]{:T(128)}, f32[3,128,3072]{2,1,0:T(8,128)}, s32[]{:T(128)}, bf16[3,128,3072]{2,1,0:T(8,128)(2,1)}, bf16[3072,512]{1,0:T(8,128)(2,1)S(1)}, /*in...) while((s32[]{:T(128)}, f32[3,128,3072]{2,1,0:T(8,128)}, ...), condition=%wide.region_6.7_spmd, body=%wide.region_5.6_spmd.sunk | while | flops 1208352768 | bytes 13108363 | solution.py:57
  335.0 5.4 fusion.146
  342.1 5.4 fusion.146
  347.5 6.6 reshape.47
  358.0 112.3 %all_to_all.20 = f32[3,64,2,3072]{3,2,0,1:T(2,128)} all-to-all(f32[3,64,2,3072]{3,2,0,1:T(2,128)S(1)} %copy.31), channel_id=1, replica_groups=mesh['segment'=4,'shard'=64] {'shard'}, dimensions={1} | all-to-all | bytes 9437184 | tf_op jit(solution)/shard_map/all_to_all | solution.py:59
  474.1 4.3 collective-permute-start.1
  480.4 77.5 %all-gather.9.cloned.1.call-done = bf16[3,128,3072]{2,0,1:T(4,128)(2,1)} async-done(((bf16[3,2,3072]{2,0,1:T(4,128)(2,1)}), bf16[3,128,3072]{2,0,1:T(4,128)(2,1)}) %all-gather.9.cloned.1.call-update) | async-done | bytes 2359312 | tf_op jit(solution)/shard_map/all_gather | solution.py:49
  564.8 14.2 %while.42 = (s32[]{:T(128)}, f32[3,128,3072]{2,1,0:T(8,128)}, s32[]{:T(128)}, bf16[3,128,3072]{2,1,0:T(8,128)(2,1)}, bf16[3072,512]{1,0:T(8,128)(2,1)S(1)}, /*in...) while((s32[]{:T(128)}, f32[3,128,3072]{2,1,0:T(8,128)}, ...), condition=%wide.region_10.11_spmd, body=%wide.region_9.10_spmd.sunk | while | flops 1208352768 | bytes 13108363 | solution.py:57
  566.5 5.4 fusion.153
  573.6 5.4 fusion.153
  579.0 6.6 reshape.48
  589.5 112.3 %all_to_all.21 = f32[3,64,2,3072]{3,2,0,1:T(2,128)} all-to-all(f32[3,64,2,3072]{3,2,0,1:T(2,128)S(1)} %copy.34), channel_id=1, replica_groups=mesh['segment'=4,'shard'=64] {'shard'}, dimensions={1} | all-to-all | bytes 9437184 | tf_op jit(solution)/shard_map/all_to_all | solution.py:59
  705.6 4.3 collective-permute-start.2
  711.9 77.5 %all-gather.11.cloned.1.call-done = bf16[3,128,3072]{2,0,1:T(4,128)(2,1)} async-done(((bf16[3,2,3072]{2,0,1:T(4,128)(2,1)}), bf16[3,128,3072]{2,0,1:T(4,128)(2,1)}) %all-gather.11.cloned.1.call-update) | async-done | bytes 2359312 | tf_op jit(solution)/shard_map/all_gather | solution.py:49
  796.3 14.2 %while.43 = (s32[]{:T(128)}, f32[3,128,3072]{2,1,0:T(8,128)}, s32[]{:T(128)}, bf16[3,128,3072]{2,1,0:T(8,128)(2,1)}, bf16[3072,512]{1,0:T(8,128)(2,1)S(1)}, /*in...) while((s32[]{:T(128)}, f32[3,128,3072]{2,1,0:T(8,128)}, ...), condition=%wide.region_14.15_spmd, body=%wide.region_13.14_spmd.sunk | while | flops 1208352768 | bytes 13108363 | solution.py:57
  798.0 5.4 fusion.160
  805.1 5.4 fusion.160
  810.5 6.6 reshape.49
  817.1 6.1 copy.37
  823.1 5.4 all-to-all-start.3
  828.5 107.1 %all-to-all-done.3 = f32[3,64,2,3072]{3,2,0,1:T(2,128)} async-done(((f32[3,64,2,3072]{3,2,0,1:T(2,128)}), f32[3,64,2,3072]{3,2,0,1:T(2,128)}, u32[]{:S(2)}, u32[]{:S(2)}) %all-to-all-start.3) | async-done | bytes 4718624 | tf_op jit(solution)/shard_map/all_to_all | solution.py:59
  (65 shorter events, 69.3 us)
Async XLA Ops:
  6.5 86.2 %all-gather.5.cloned.1.call-start = ((), (), s32[]{:S(2)}) async-start(), calls=%async_computation.4 | async-start | bytes 3194880 | tf_op jit(solution)/shard_map/all_gather | solution.py:49
  97.0 2.8 copy-start
  126.6 5.6 copy-start.5
  126.6 112.7 %all-to-all-start = ((f32[3,64,2,3072]{3,2,0,1:T(2,128)}), f32[3,64,2,3072]{3,2,0,1:T(2,128)}, u32[]{:S(2)}, u32[]{:S(2)}) async-start(f32[3,64,2,3072]{3,2,0,1:T(2,128)} %copy.28), calls=%async_computation | async-start | bytes 9437184 | tf_op jit(solution)/shard_map/all_to_all | solution.py:59
  132.1 110.8 %copy-start.1 = (bf16[3,2,3072]{2,1,0:T(2,128)(2,1)S(1)}, bf16[3,2,3072]{2,1,0:T(2,128)(2,1)}, u32[]{:S(2)}) copy-start(bf16[3,2,3072]{2,1,0:T(2,128)(2,1)} %param.15) | copy-start | bytes 110596
  132.1 116.4 %copy-start.2 = (f32[1,3072]{1,0:T(1,128)S(1)}, f32[1,3072]{1,0:T(1,128)}, u32[]{:S(2)}) copy-start(f32[1,3072]{1,0:T(1,128)} %param.16) | copy-start | bytes 36868
  132.1 194.3 %all-gather.7.cloned.1.call-start = ((), (), s32[]{:S(2)}) async-start(), calls=%async_computation.5 | async-start | bytes 3194880 | tf_op jit(solution)/shard_map/all_gather | solution.py:49
  243.0 5.3 collective-permute-start
  249.3 308.6 %all-gather.9.cloned.1.call-start = ((), (), s32[]{:S(2)}) async-start(), calls=%async_computation.6 | async-start | bytes 3194880 | tf_op jit(solution)/shard_map/all_gather | solution.py:49
  474.1 5.3 collective-permute-start.1
  480.3 309.0 %all-gather.11.cloned.1.call-start = ((), (), s32[]{:S(2)}) async-start(), calls=%async_computation.7 | async-start | bytes 3194880 | tf_op jit(solution)/shard_map/all_gather | solution.py:49
  705.6 90.7 %copy-start.3 = (bf16[3,2,3072]{2,1,0:T(2,128)(2,1)}, bf16[3,2,3072]{2,1,0:T(2,128)(2,1)S(1)}, u32[]{:S(2)}) copy-start(bf16[3,2,3072]{2,1,0:T(2,128)(2,1)S(1)} %fusion.87) | copy-start | bytes 110596
  705.6 5.3 collective-permute-start.2
  823.1 112.5 %all-to-all-start.3 = ((f32[3,64,2,3072]{3,2,0,1:T(2,128)}), f32[3,64,2,3072]{3,2,0,1:T(2,128)}, u32[]{:S(2)}, u32[]{:S(2)}) async-start(f32[3,64,2,3072]{3,2,0,1:T(2,128)} %copy.37), calls=%async_computation.3 | async-start | bytes 9437184 | tf_op jit(solution)/shard_map/all_to_all | solution.py:59
  828.5 110.8 %copy-start.4 = (bf16[3,2,3072]{2,1,0:T(2,128)(2,1)S(1)}, bf16[3,2,3072]{2,1,0:T(2,128)(2,1)}, u32[]{:S(2)}) copy-start(bf16[3,2,3072]{2,1,0:T(2,128)(2,1)} %copy-done.3) | copy-start | bytes 110596
Sparse Core Ops, SparseCore 0:
  10.1 82.5 all-gather.4
  249.4 76.9 all-gather.6
  480.5 77.3 all-gather.8
  712.0 77.3 all-gather.10
where the time goes:
time: 949 us; the launch traced here: 947 us
  waiting for transfers between devices  533 us (56%)
  blocking collectives  225 us (24%)
  local copies, waits for them, and re-layouts  76.8 us (8%)
  matrix products  56.6 us (6%)
  starting transfers between devices  23.8 us (3%)
  other arithmetic  18.2 us (2%)
  between operations  14 us (1%)
    all_gather x4, waiting for transfers between devices, shards(): gathered = lax.all_gather(normed, 'shard', axis=1, tiled=True)  315 us
    all_to_all x2, blocking collectives, shards(): lax.all_to_all(split_terms, 'shard', split_axis=1, concat_axis=1, tiled=T...  225 us
    all_to_all x2, waiting for transfers between devices, shards(): lax.all_to_all(split_terms, 'shard', split_axis=1, concat_axis=1, tiled=T...  214 us
    reshape x8, local copies, waits for them, and re-layouts, shards(): partial_sum.reshape(block_total, shard_count, local_rows, width)  46.4 us
    dot_general x8, matrix products, expert_rows(): return jnp.dot(hidden, down_part, preferred_element_type=jnp.float32)  42.9 us
  transfers between devices with their start and end apart: 9, of which 9 were waited for; matrix products, arithmetic and copies ran while one was open for 0% of the time, Pallas kernels for 0%

commit v1 on v0

v1 whole, which is shorter than its diff:
```python
import functools

import jax
import jax.numpy as jnp
from jax import lax
from jax.experimental import pallas as pl
from jax.experimental.pallas import tpu as pltpu
from jax.sharding import PartitionSpec as P

FF = 16384
LANES = 128


def shifted(value, axis, steps):
    count = lax.axis_size(axis)
    initial, last = (max(0, -steps), min(count, count - steps))
    return lax.ppermute(value, axis, [(source, source + steps) for source in range(initial, last)])


def normalize(rows, row_gain):
    values = rows.astype(jnp.float32)
    scale = lax.rsqrt(jnp.mean(values * values, axis=-1, keepdims=True) + 1e-05)
    return (values * scale * row_gain).astype(jnp.bfloat16)


def exchange_kernel(count, per_expert, x_ref, o_ref, send_sem, recv_sem):
    me = lax.axis_index("shard")
    segment = lax.axis_index("segment")

    def source(dest):
        return x_ref.at[dest // per_expert] if per_expert else x_ref.at[dest]

    def copy_to(dest):
        return pltpu.make_async_remote_copy(
            src_ref=source(dest),
            dst_ref=o_ref.at[me],
            send_sem=send_sem.at[dest],
            recv_sem=recv_sem.at[me],
            device_id=(segment, dest),
            device_id_type=pl.DeviceIdType.MESH,
        )

    def start(step, carry):
        copy_to(lax.rem(me + step, count)).start()
        return carry

    lax.fori_loop(1, count, start, 0)
    o_ref[me] = source(me)[...]

    def finish(step, carry):
        copy_to(lax.rem(me + step, count)).wait_send()
        origin = lax.rem(me + count - step, count)
        pltpu.make_async_remote_copy(
            src_ref=source(origin),
            dst_ref=o_ref.at[origin],
            send_sem=send_sem.at[origin],
            recv_sem=recv_sem.at[origin],
            device_id=(segment, origin),
            device_id_type=pl.DeviceIdType.MESH,
        ).wait_recv()
        return carry

    lax.fori_loop(1, count, finish, 0)


def exchange(pieces, count, per_expert):
    rows, lanes = pieces.shape[1], pieces.shape[2]
    return pl.pallas_call(
        functools.partial(exchange_kernel, count, per_expert),
        out_shape=jax.ShapeDtypeStruct((count, rows, lanes), pieces.dtype),
        in_specs=[pl.BlockSpec(memory_space=pltpu.VMEM)],
        out_specs=pl.BlockSpec(memory_space=pltpu.VMEM),
        scratch_shapes=[pltpu.SemaphoreType.DMA((count,)), pltpu.SemaphoreType.DMA((count,))],
        compiler_params=pltpu.CompilerParams(has_side_effects=True),
    )(pieces)


def shards(tokens, norm_gain, w_gate, w_up, w_down, block_counts, gate_prob):
    segment_index = lax.axis_index("segment")
    segment_count = lax.axis_size("segment")
    shard_count = lax.axis_size("shard")
    hidden_count = w_gate.shape[2]
    per_expert = FF // hidden_count
    zero_blocks = block_counts[0]
    row_gain = norm_gain[0]
    gate_part = w_gate[0]
    up_part = w_up[0]
    down_part = w_down[0]
    probs = gate_prob[0]
    local_rows = tokens.shape[1]
    width = tokens.shape[2]
    piece_rows = 2 * local_rows * width // LANES
    carried = tokens
    stored = jnp.zeros_like(tokens)
    for tick in range(segment_count):
        normed = normalize(carried, row_gain)
        pieces = jnp.stack([normed[0:2], normed[1:3]]).reshape(2, piece_rows, LANES)
        gathered = exchange(pieces, shard_count, per_expert)
        block_rows = gathered.reshape(shard_count * 2 * local_rows, width)
        gate_val = jnp.dot(block_rows, gate_part, preferred_element_type=jnp.float32)
        up_val = jnp.dot(block_rows, up_part, preferred_element_type=jnp.float32)
        hidden = (jax.nn.silu(gate_val) * up_val).astype(jnp.bfloat16)
        partial_sum = jnp.dot(hidden, down_part, preferred_element_type=jnp.float32)
        received = exchange(partial_sum.reshape(shard_count, piece_rows, LANES), shard_count, 0)
        received = received.reshape(2, shard_count // 2, 2, local_rows, width)
        first, second = jnp.sum(received[0], axis=0), jnp.sum(received[1], axis=0)
        middle = jnp.where(zero_blocks >= 2, first[1], second[0])
        mixed = jnp.stack([first[0], middle, second[1]])
        updated = (carried.astype(jnp.float32) + probs[:, :, None] * mixed).astype(jnp.bfloat16)
        stored = jnp.where(segment_index == tick, updated, stored)
        if tick + 1 < segment_count:
            carried = shifted(updated, "segment", 1)
    return stored[None]


def solution(mesh):
    placed = (
        P(None, "shard", None),
        P("segment", None),
        P("segment", None, "shard"),
        P("segment", None, "shard"),
        P("segment", "shard", None),
        P("segment"),
        P("segment", None, "shard"),
    )
    return jax.shard_map(
        shards,
        mesh=mesh,
        in_specs=placed,
        out_specs=P("segment", None, "shard", None),
        check_vma=False,
    )
```

time: 949 us -> 681 us (0.72)
  Pallas kernels: 0 us -> 569 us
  waiting for transfers between devices: 533 us -> 3.43 us
  blocking collectives: 225 us -> 0 us
  local copies, waits for them, and re-layouts: 76.8 us -> 39.4 us
  matrix products: 56.6 us -> 40.7 us
  starting transfers between devices: 23.8 us -> 9.34 us
  between operations: 14 us -> 0.97 us
    pallas_call x0 -> x8, Pallas kernels: none -> 569 us  [exchange(): pl.pallas_call(functools.partial(exchange_kernel, count, per_expert), out...]
    all_gather x4 -> x0, waiting for transfers between devices: 315 us -> none  [shards(): gathered = lax.all_gather(normed, 'shard', axis=1, tiled=True)]
    all_to_all x2 -> x0, blocking collectives: 225 us -> none  [shards(): lax.all_to_all(split_terms, 'shard', split_axis=1, concat_axis=1, tiled=T...]
    all_to_all x2 -> x0, waiting for transfers between devices: 214 us -> none  [shards(): lax.all_to_all(split_terms, 'shard', split_axis=1, concat_axis=1, tiled=T...]
    while x4 -> x0, local copies, waits for them, and re-layouts: 16.9 us -> none  [shards(): partial_sum = lax.fori_loop(first_block, last_block, add_block, partial_sum)]
    dot_general x16 -> x8, matrix products: 56.6 us -> 40.7 us  [the longest x4 24 us: shards(): partial_sum = jnp.dot(hidden, down_part, preferred_element_type=jnp.float32)]
    reshape x8, local copies, waits for them, and re-layouts: 46.4 us -> 33 us  [the longest x4 18.2 us: shards(): partial_sum.reshape(shard_count, piece_rows, LANES)]
    all_to_all x2 -> x0, starting transfers between devices: 10.9 us -> none  [shards(): lax.all_to_all(split_terms, 'shard', split_axis=1, concat_axis=1, tiled=T...]
  transfers between devices with their start and end apart: 9 -> 3, of which waited for: 9 -> 3; matrix products, arithmetic and copies ran while one was open for 0% -> 0% of each run, Pallas kernels for 0% -> 0%
where the time goes in v1:
time: 681 us; the launch traced here: 680 us
  Pallas kernels  569 us (84%)
  matrix products  40.7 us (6%)
  local copies, waits for them, and re-layouts  39.4 us (6%)
  other arithmetic  17.3 us (3%)
  starting transfers between devices  9.34 us (1%)
    pallas_call x8, Pallas kernels, exchange(): pl.pallas_call(functools.partial(exchange_kernel, count, per_expert), out...  569 us
    dot_general x4, matrix products, shards(): partial_sum = jnp.dot(hidden, down_part, preferred_element_type=jnp.float32)  24 us
    reshape x4, local copies, waits for them, and re-layouts, shards(): partial_sum.reshape(shard_count, piece_rows, LANES)  18.2 us
    dot_general x4, matrix products, shards(): jnp.dot(block_rows, gate_part, preferred_element_type=jnp.float32)  16.6 us
    reshape x4, local copies, waits for them, and re-layouts, shards(): block_rows = gathered.reshape(shard_count * 2 * local_rows, width)  14.8 us
  transfers between devices with their start and end apart: 3, of which 3 were waited for; matrix products, arithmetic and copies ran while one was open for 0% of the time, Pallas kernels for 0%

profile of v1, /device:TPU:1, one launch (start us, length us, event | category | flops | bytes accessed | tf_op | source)
XLA Modules:
  0.0 679.9 jit_solution(4701799792006144249)
XLA Ops:
  2.7 57.8 %shard_map.73 = bf16[64,96,128]{2,1,0:T(8,128)(2,1)} custom-call(bf16[2,96,128]{2,1,0:T(8,128)(2,1)} %pad_maximum_fusion.x_ref), custom_call_target="tpu_custom_call" | custom-call | tf_op jit(solution)/shard_map/pallas_call | solution.py:68
  60.5 3.7 reshape.192
  64.2 4.2 fusion.22
  68.4 6.0 fusion.6
  74.4 4.5 reshape.193.x_ref
  78.9 87.1 %shard_map.74 = f32[64,96,128]{2,1,0:T(8,128)} custom-call(f32[64,96,128]{2,1,0:T(8,128)} %reshape.193.x_ref), custom_call_target="tpu_custom_call" | custom-call | tf_op jit(solution)/shard_map/pallas_call | solution.py:68
  166.0 2.1 slice_reduce_fusion.7
  169.0 3.1 collective-permute-start
  174.2 54.2 %shard_map.75 = bf16[64,96,128]{2,1,0:T(8,128)(2,1)} custom-call(bf16[2,96,128]{2,1,0:T(8,128)(2,1)} %pad_maximum_fusion.1.x_ref), custom_call_target="tpu_custom_call" | custom-call | tf_op jit(solution)/shard_map/pallas_call | solution.py:68
  228.4 3.7 reshape.194
  232.1 4.2 fusion.20
  236.3 6.0 fusion.4
  242.3 4.5 reshape.195.x_ref
  246.8 87.1 %shard_map.76 = f32[64,96,128]{2,1,0:T(8,128)} custom-call(f32[64,96,128]{2,1,0:T(8,128)} %reshape.195.x_ref), custom_call_target="tpu_custom_call" | custom-call | tf_op jit(solution)/shard_map/pallas_call | solution.py:68
  333.9 2.0 slice_reduce_fusion.5
  336.2 3.1 collective-permute-start.1
  341.3 54.2 %shard_map.77 = bf16[64,96,128]{2,1,0:T(8,128)(2,1)} custom-call(bf16[2,96,128]{2,1,0:T(8,128)(2,1)} %pad_maximum_fusion.2.x_ref), custom_call_target="tpu_custom_call" | custom-call | tf_op jit(solution)/shard_map/pallas_call | solution.py:68
  395.6 3.7 reshape.196
  399.3 4.2 fusion.18
  403.4 6.0 fusion.2
  409.4 4.5 reshape.197.x_ref
  414.0 87.1 %shard_map.78 = f32[64,96,128]{2,1,0:T(8,128)} custom-call(f32[64,96,128]{2,1,0:T(8,128)} %reshape.197.x_ref), custom_call_target="tpu_custom_call" | custom-call | tf_op jit(solution)/shard_map/pallas_call | solution.py:68
  501.1 2.0 slice_reduce_fusion.3
  503.9 3.1 collective-permute-start.2
  512.6 54.1 %shard_map.79 = bf16[64,96,128]{2,1,0:T(8,128)(2,1)} custom-call(bf16[2,96,128]{2,1,0:T(8,128)(2,1)} %pad_maximum_fusion.3.x_ref), custom_call_target="tpu_custom_call" | custom-call | tf_op jit(solution)/shard_map/pallas_call | solution.py:68
  566.8 3.7 reshape.198
  570.5 4.2 fusion.16
  574.6 6.0 fusion
  580.6 4.5 reshape.199.x_ref
  585.2 87.1 %shard_map.80 = f32[64,96,128]{2,1,0:T(8,128)} custom-call(f32[64,96,128]{2,1,0:T(8,128)} %reshape.199.x_ref), custom_call_target="tpu_custom_call" | custom-call | tf_op jit(solution)/shard_map/pallas_call | solution.py:68
  672.3 2.0 slice_reduce_fusion.1
  678.3 1.7 fusion.96
  (59 shorter events, 17.4 us)
Async XLA Ops:
  0.0 68.3 %copy-start = (bf16[1,512,3072]{2,1,0:T(8,128)(2,1)S(1)}, bf16[1,512,3072]{2,1,0:T(8,128)(2,1)}, u32[]{:S(2)}) copy-start(bf16[1,512,3072]{2,1,0:T(8,128)(2,1)} %param.11) | copy-start | bytes 9437188
  166.0 2.8 copy-start.3
  166.0 2.9 copy-start.1
  166.0 7.3 %copy-start.2 = (f32[1,3072]{1,0:T(1,128)S(1)}, f32[1,3072]{1,0:T(1,128)}, u32[]{:S(2)}) copy-start(f32[1,3072]{1,0:T(1,128)} %param.8) | copy-start | bytes 36868
  169.0 4.2 collective-permute-start
  336.2 4.2 collective-permute-start.1
  503.9 4.5 collective-permute-start.2

commit v2 on v1

v2 whole, which is shorter than its diff:
```python
import functools

import jax
import jax.numpy as jnp
from jax import lax
from jax.experimental import pallas as pl
from jax.experimental.pallas import tpu as pltpu
from jax.sharding import PartitionSpec as P

FF = 16384
LANES = 128


def shifted(value, axis, steps):
    count = lax.axis_size(axis)
    initial, last = (max(0, -steps), min(count, count - steps))
    return lax.ppermute(value, axis, [(source, source + steps) for source in range(initial, last)])


def normalize(rows, row_gain):
    values = rows.astype(jnp.float32)
    scale = lax.rsqrt(jnp.mean(values * values, axis=-1, keepdims=True) + 1e-05)
    return (values * scale * row_gain).astype(jnp.bfloat16)


def chip_exchange_kernel(chips, per_expert, x_ref, o_ref, send_sem, recv_sem):
    me = lax.axis_index("shard")
    segment = lax.axis_index("segment")
    core = lax.rem(me, 2)
    chip = me // 2

    def source(dest_chip):
        return x_ref.at[dest_chip // per_expert] if per_expert else x_ref.at[dest_chip]

    def copy_of(dest_chip, slot):
        return pltpu.make_async_remote_copy(
            src_ref=source(dest_chip),
            dst_ref=o_ref.at[slot],
            send_sem=send_sem.at[dest_chip],
            recv_sem=recv_sem.at[slot],
            device_id=(segment, dest_chip * 2 + core),
            device_id_type=pl.DeviceIdType.MESH,
        )

    def start(step, carry):
        copy_of(lax.rem(chip + step, chips), chip).start()
        return carry

    lax.fori_loop(1, chips, start, 0)
    o_ref[chip] = source(chip)[...]

    def finish(step, carry):
        copy_of(lax.rem(chip + step, chips), chip).wait_send()
        copy_of(lax.rem(chip + chips - step, chips), lax.rem(chip + chips - step, chips)).wait_recv()
        return carry

    lax.fori_loop(1, chips, finish, 0)


def chip_exchange(pieces, chips, per_expert):
    rows, lanes = pieces.shape[1], pieces.shape[2]
    return pl.pallas_call(
        functools.partial(chip_exchange_kernel, chips, per_expert),
        out_shape=jax.ShapeDtypeStruct((chips, rows, lanes), pieces.dtype),
        in_specs=[pl.BlockSpec(memory_space=pltpu.VMEM)],
        out_specs=pl.BlockSpec(memory_space=pltpu.VMEM),
        scratch_shapes=[pltpu.SemaphoreType.DMA((chips,)), pltpu.SemaphoreType.DMA((chips,))],
        compiler_params=pltpu.CompilerParams(has_side_effects=True),
    )(pieces)


def pair_exchange_kernel(x_ref, o_ref, send_sem, recv_sem):
    me = lax.axis_index("shard")
    segment = lax.axis_index("segment")
    copy = pltpu.make_async_remote_copy(
        src_ref=x_ref,
        dst_ref=o_ref,
        send_sem=send_sem,
        recv_sem=recv_sem,
        device_id=(segment, me + 1 - 2 * lax.rem(me, 2)),
        device_id_type=pl.DeviceIdType.MESH,
    )
    copy.start()
    copy.wait()


def pair_exchange(value):
    return pl.pallas_call(
        pair_exchange_kernel,
        out_shape=jax.ShapeDtypeStruct(value.shape, value.dtype),
        in_specs=[pl.BlockSpec(memory_space=pltpu.VMEM)],
        out_specs=pl.BlockSpec(memory_space=pltpu.VMEM),
        scratch_shapes=[pltpu.SemaphoreType.DMA(()), pltpu.SemaphoreType.DMA(())],
        compiler_params=pltpu.CompilerParams(has_side_effects=True),
    )(value)


def shards(tokens, norm_gain, w_gate, w_up, w_down, block_counts, gate_prob):
    segment_index = lax.axis_index("segment")
    segment_count = lax.axis_size("segment")
    shard_count = lax.axis_size("shard")
    hidden_count = w_gate.shape[2]
    per_expert = FF // hidden_count
    zero_blocks = block_counts[0]
    row_gain = norm_gain[0]
    gate_part = w_gate[0]
    up_part = w_up[0]
    down_part = w_down[0]
    probs = gate_prob[0]
    local_rows = tokens.shape[1]
    width = tokens.shape[2]
    piece_rows = 2 * local_rows * width // LANES
    chips = shard_count // 2
    carried = tokens
    stored = jnp.zeros_like(tokens)
    for tick in range(segment_count):
        normed = normalize(carried, row_gain)
        pieces = jnp.stack([normed[0:2], normed[1:3]]).reshape(2, piece_rows, LANES)
        own_core = chip_exchange(pieces, chips, per_expert // 2)
        other_core = pair_exchange(own_core)
        block_rows = jnp.concatenate([own_core, other_core]).reshape(shard_count * 2 * local_rows, width)
        gate_val = jnp.dot(block_rows, gate_part, preferred_element_type=jnp.float32)
        up_val = jnp.dot(block_rows, up_part, preferred_element_type=jnp.float32)
        hidden = (jax.nn.silu(gate_val) * up_val).astype(jnp.bfloat16)
        partial_sum = jnp.dot(hidden, down_part, preferred_element_type=jnp.float32)
        partial_sum = partial_sum.reshape(2, chips, piece_rows, LANES)
        chip_sum = partial_sum[0] + pair_exchange(partial_sum[1])
        received = chip_exchange(chip_sum.astype(jnp.bfloat16), chips, 0).astype(jnp.float32)
        received = received.reshape(2, chips // 2, 2, local_rows, width)
        first, second = jnp.sum(received[0], axis=0), jnp.sum(received[1], axis=0)
        middle = jnp.where(zero_blocks >= 2, first[1], second[0])
        mixed = jnp.stack([first[0], middle, second[1]])
        updated = (carried.astype(jnp.float32) + probs[:, :, None] * mixed).astype(jnp.bfloat16)
        stored = jnp.where(segment_index == tick, updated, stored)
        if tick + 1 < segment_count:
            carried = shifted(updated, "segment", 1)
    return stored[None]


def solution(mesh):
    placed = (
        P(None, "shard", None),
        P("segment", None),
        P("segment", None, "shard"),
        P("segment", None, "shard"),
        P("segment", "shard", None),
        P("segment"),
        P("segment", None, "shard"),
    )
    return jax.shard_map(
        shards,
        mesh=mesh,
        in_specs=placed,
        out_specs=P("segment", None, "shard", None),
        check_vma=False,
    )
```

time: 681 us -> 561 us (0.82)
  Pallas kernels: 569 us -> 408 us
  other arithmetic: 17.3 us -> 37.3 us
  local copies, waits for them, and re-layouts: 39.4 us -> 57.4 us
    pallas_call x8 -> x16, Pallas kernels: 569 us -> 408 us  [the longest x8 281 us: chip_exchange(): pl.pallas_call(functools.partial(chip_exchange_kernel, chips, per_expert)...]
    squeeze x0 -> x8, local copies, waits for them, and re-layouts: none -> 20.5 us  [shards(): chip_sum = partial_sum[0] + pair_exchange(partial_sum[1])]
    reshape x8 -> x4, local copies, waits for them, and re-layouts: 33 us -> 14.8 us  [shards(): jnp.concatenate([own_core, other_core])]
    convert_element_type x0 -> x8, other arithmetic: none -> 17.2 us  [the longest x4 12 us: shards(): chip_sum.astype(jnp.bfloat16)]
    slice x0 -> x4, local copies, waits for them, and re-layouts: none -> 15.7 us  [shards(): chip_sum = partial_sum[0] + pair_exchange(partial_sum[1])]
    concatenate x0 -> x4, other arithmetic: none -> 10.6 us  [shards(): jnp.concatenate([own_core, other_core])]
    reduce_sum x4, other arithmetic: 8.19 us -> 0.31 us  [shards(): first, second = (jnp.sum(received[0], axis=0), jnp.sum(received[1], axis=0))]
where the time goes in v2:
time: 561 us; the launch traced here: 558 us
  Pallas kernels  408 us (73%)
  local copies, waits for them, and re-layouts  57.4 us (10%)
  matrix products  40.7 us (7%)
  other arithmetic  37.3 us (7%)
  starting transfers between devices  9.99 us (2%)
    pallas_call x8, Pallas kernels, chip_exchange(): pl.pallas_call(functools.partial(chip_exchange_kernel, chips, per_expert)...  281 us
    pallas_call x8, Pallas kernels, pair_exchange(): pl.pallas_call(pair_exchange_kernel, out_shape=jax.ShapeDtypeStruct(value...  127 us
    dot_general x4, matrix products, shards(): partial_sum = jnp.dot(hidden, down_part, preferred_element_type=jnp.float32)  24 us
    squeeze x8, local copies, waits for them, and re-layouts, shards(): chip_sum = partial_sum[0] + pair_exchange(partial_sum[1])  20.5 us
    dot_general x4, matrix products, shards(): jnp.dot(block_rows, gate_part, preferred_element_type=jnp.float32)  16.6 us
    slice x4, local copies, waits for them, and re-layouts, shards(): chip_sum = partial_sum[0] + pair_exchange(partial_sum[1])  15.7 us
    reshape x4, local copies, waits for them, and re-layouts, shards(): jnp.concatenate([own_core, other_core])  14.8 us
    convert_element_type x4, other arithmetic, shards(): chip_sum.astype(jnp.bfloat16)  12 us
  transfers between devices with their start and end apart: 3, of which 3 were waited for; matrix products, arithmetic and copies ran while one was open for 0% of the time, Pallas kernels for 0%

profile of v2, /device:TPU:1, one launch (start us, length us, event | category | flops | bytes accessed | tf_op | source)
XLA Modules:
  0.0 558.1 jit_solution(14594661184590156222)
XLA Ops:
  2.7 38.4 %shard_map.73.x_ref = bf16[32,96,128]{2,1,0:T(8,128)(2,1)} custom-call(bf16[2,96,128]{2,1,0:T(8,128)(2,1)} %pad_maximum_fusion.4.x_ref), custom_call_target="tpu_custom_call" | custom-call | tf_op jit(solution)/shard_map/pallas_call | solution.py:62
  41.0 14.3 %shard_map.74 = bf16[32,96,128]{2,1,0:T(8,128)(2,1)} custom-call(bf16[32,96,128]{2,1,0:T(8,128)(2,1)} %shard_map.73.x_ref), custom_call_target="tpu_custom_call" | custom-call | tf_op jit(solution)/shard_map/pallas_call | solution.py:88
  58.0 3.7 reshape.200
  61.7 4.2 fusion.22
  65.9 6.0 %fusion.6 = f32[256,3072]{1,0:T(8,128)} fusion(bf16[1,512,3072]{2,1,0:T(8,128)(2,1)S(1)} %copy-done, bf16[256,3072]{1,0:T(8,128)(2,1)} %reshape.200, bf16[1,3072,512]{2,1,0:T(8,128)(2,1)} %param.10, f32[256,512]{1,0:T(8,128)} %fusion.22), kind=kOutput, calls=%fused_computation.6 | convolution fusion | flops 1611399168 | bytes 11534336 | tf_op jit(solution)/shard_map/dot_general | solution.py:125
  71.9 3.9 fusion.104
  78.4 17.5 %shard_map.75 = f32[32,96,128]{2,1,0:T(8,128)} custom-call(f32[32,96,128]{2,1,0:T(8,128)} %squeeze.26.x_ref), custom_call_target="tpu_custom_call" | custom-call | tf_op jit(solution)/shard_map/pallas_call | solution.py:88
  101.4 34.9 %shard_map.76 = bf16[32,96,128]{2,1,0:T(8,128)(2,1)} custom-call(bf16[32,96,128]{2,1,0:T(8,128)(2,1)} %add_convert_fusion.3.x_ref), custom_call_target="tpu_custom_call" | custom-call | tf_op jit(solution)/shard_map/pallas_call | solution.py:62
  144.1 34.4 %shard_map.77.x_ref = bf16[32,96,128]{2,1,0:T(8,128)(2,1)} custom-call(bf16[2,96,128]{2,1,0:T(8,128)(2,1)} %pad_maximum_fusion.5.x_ref), custom_call_target="tpu_custom_call" | custom-call | tf_op jit(solution)/shard_map/pallas_call | solution.py:62
  178.5 14.3 %shard_map.78 = bf16[32,96,128]{2,1,0:T(8,128)(2,1)} custom-call(bf16[32,96,128]{2,1,0:T(8,128)(2,1)} %shard_map.77.x_ref), custom_call_target="tpu_custom_call" | custom-call | tf_op jit(solution)/shard_map/pallas_call | solution.py:88
  195.4 3.7 reshape.201
  199.1 4.2 fusion.20
  203.3 6.0 %fusion.4 = f32[256,3072]{1,0:T(8,128)} fusion(bf16[1,512,3072]{2,1,0:T(8,128)(2,1)S(1)} %copy-done, bf16[256,3072]{1,0:T(8,128)(2,1)} %reshape.201, bf16[1,3072,512]{2,1,0:T(8,128)(2,1)} %param.10, f32[256,512]{1,0:T(8,128)} %fusion.20), kind=kOutput, calls=%fused_computation.4 | convolution fusion | flops 1611399168 | bytes 11534336 | tf_op jit(solution)/shard_map/dot_general | solution.py:125
  209.3 3.9 fusion.103
  215.8 17.5 %shard_map.79 = f32[32,96,128]{2,1,0:T(8,128)} custom-call(f32[32,96,128]{2,1,0:T(8,128)} %squeeze.56.x_ref), custom_call_target="tpu_custom_call" | custom-call | tf_op jit(solution)/shard_map/pallas_call | solution.py:88
  238.8 34.9 %shard_map.80 = bf16[32,96,128]{2,1,0:T(8,128)(2,1)} custom-call(bf16[32,96,128]{2,1,0:T(8,128)(2,1)} %add_convert_fusion.2.x_ref), custom_call_target="tpu_custom_call" | custom-call | tf_op jit(solution)/shard_map/pallas_call | solution.py:62
  280.7 34.4 %shard_map.81.x_ref = bf16[32,96,128]{2,1,0:T(8,128)(2,1)} custom-call(bf16[2,96,128]{2,1,0:T(8,128)(2,1)} %pad_maximum_fusion.6.x_ref), custom_call_target="tpu_custom_call" | custom-call | tf_op jit(solution)/shard_map/pallas_call | solution.py:62
  315.1 14.5 %shard_map.82 = bf16[32,96,128]{2,1,0:T(8,128)(2,1)} custom-call(bf16[32,96,128]{2,1,0:T(8,128)(2,1)} %shard_map.81.x_ref), custom_call_target="tpu_custom_call" | custom-call | tf_op jit(solution)/shard_map/pallas_call | solution.py:88
  332.3 3.7 reshape.202
  336.0 4.2 fusion.18
  340.1 6.0 %fusion.2 = f32[256,3072]{1,0:T(8,128)} fusion(bf16[1,512,3072]{2,1,0:T(8,128)(2,1)S(1)} %copy-done, bf16[256,3072]{1,0:T(8,128)(2,1)} %reshape.202, bf16[1,3072,512]{2,1,0:T(8,128)(2,1)} %param.10, f32[256,512]{1,0:T(8,128)} %fusion.18), kind=kOutput, calls=%fused_computation.2 | convolution fusion | flops 1611399168 | bytes 11534336 | tf_op jit(solution)/shard_map/dot_general | solution.py:125
  346.1 3.9 fusion.102
  352.6 17.3 %shard_map.83 = f32[32,96,128]{2,1,0:T(8,128)} custom-call(f32[32,96,128]{2,1,0:T(8,128)} %squeeze.58.x_ref), custom_call_target="tpu_custom_call" | custom-call | tf_op jit(solution)/shard_map/pallas_call | solution.py:88
  375.5 34.9 %shard_map.84 = bf16[32,96,128]{2,1,0:T(8,128)(2,1)} custom-call(bf16[32,96,128]{2,1,0:T(8,128)(2,1)} %add_convert_fusion.1.x_ref), custom_call_target="tpu_custom_call" | custom-call | tf_op jit(solution)/shard_map/pallas_call | solution.py:62
  421.6 34.3 %shard_map.85.x_ref = bf16[32,96,128]{2,1,0:T(8,128)(2,1)} custom-call(bf16[2,96,128]{2,1,0:T(8,128)(2,1)} %pad_maximum_fusion.7.x_ref), custom_call_target="tpu_custom_call" | custom-call | tf_op jit(solution)/shard_map/pallas_call | solution.py:62
  455.9 14.3 %shard_map.86 = bf16[32,96,128]{2,1,0:T(8,128)(2,1)} custom-call(bf16[32,96,128]{2,1,0:T(8,128)(2,1)} %shard_map.85.x_ref), custom_call_target="tpu_custom_call" | custom-call | tf_op jit(solution)/shard_map/pallas_call | solution.py:88
  472.8 3.7 reshape.203
  476.5 4.2 fusion.16
  480.7 6.0 %fusion = f32[256,3072]{1,0:T(8,128)} fusion(bf16[1,512,3072]{2,1,0:T(8,128)(2,1)S(1)} %copy-done, bf16[256,3072]{1,0:T(8,128)(2,1)} %reshape.203, bf16[1,3072,512]{2,1,0:T(8,128)(2,1)} %param.10, f32[256,512]{1,0:T(8,128)} %fusion.16), kind=kOutput, calls=%fused_computation | convolution fusion | flops 1611399168 | bytes 11534336 | tf_op jit(solution)/shard_map/dot_general | solution.py:125
  486.7 3.9 fusion.101
  493.2 17.5 %shard_map.87 = f32[32,96,128]{2,1,0:T(8,128)} custom-call(f32[32,96,128]{2,1,0:T(8,128)} %squeeze.60.x_ref), custom_call_target="tpu_custom_call" | custom-call | tf_op jit(solution)/shard_map/pallas_call | solution.py:88
  516.2 34.9 %shard_map.88 = bf16[32,96,128]{2,1,0:T(8,128)(2,1)} custom-call(bf16[32,96,128]{2,1,0:T(8,128)(2,1)} %add_convert_fusion.x_ref), custom_call_target="tpu_custom_call" | custom-call | tf_op jit(solution)/shard_map/pallas_call | solution.py:62
  (87 shorter events, 77.7 us)
Async XLA Ops:
  0.0 65.9 %copy-start = (bf16[1,512,3072]{2,1,0:T(8,128)(2,1)S(1)}, bf16[1,512,3072]{2,1,0:T(8,128)(2,1)}, u32[]{:S(2)}) copy-start(bf16[1,512,3072]{2,1,0:T(8,128)(2,1)} %param.11) | copy-start | bytes 9437188
  137.6 0.9 copy-start.3
  137.6 0.9 copy-start.1
  137.6 5.6 copy-start.2
  138.7 4.4 collective-permute-start
  275.3 4.4 collective-permute-start.1
  412.6 4.7 collective-permute-start.2

commit v3 on v2

--- a/solution.py
+++ b/solution.py
@@ -28,6 +28,15 @@
     segment = lax.axis_index("segment")
     core = lax.rem(me, 2)
     chip = me // 2
+    barrier = pltpu.get_barrier_semaphore()
+
+    def greet(step, carry):
+        dest = lax.rem(chip + step, chips) * 2 + core
+        pl.semaphore_signal(barrier, 1, device_id=(segment, dest), device_id_type=pl.DeviceIdType.MESH)
+        return carry
+
+    lax.fori_loop(1, chips, greet, 0)
+    pl.semaphore_wait(barrier, chips - 1)
 
     def source(dest_chip):
         return x_ref.at[dest_chip // per_expert] if per_expert else x_ref.at[dest_chip]
@@ -57,7 +66,7 @@
     lax.fori_loop(1, chips, finish, 0)
 
 
-def chip_exchange(pieces, chips, per_expert):
+def chip_exchange(pieces, chips, per_expert, collective):
     rows, lanes = pieces.shape[1], pieces.shape[2]
     return pl.pallas_call(
         functools.partial(chip_exchange_kernel, chips, per_expert),
@@ -65,33 +74,37 @@
         in_specs=[pl.BlockSpec(memory_space=pltpu.VMEM)],
         out_specs=pl.BlockSpec(memory_space=pltpu.VMEM),
         scratch_shapes=[pltpu.SemaphoreType.DMA((chips,)), pltpu.SemaphoreType.DMA((chips,))],
-        compiler_params=pltpu.CompilerParams(has_side_effects=True),
+        compiler_params=pltpu.CompilerParams(collective_id=collective, has_side_effects=True),
     )(pieces)
 
 
 def pair_exchange_kernel(x_ref, o_ref, send_sem, recv_sem):
     me = lax.axis_index("shard")
     segment = lax.axis_index("segment")
+    partner = (segment, me + 1 - 2 * lax.rem(me, 2))
+    barrier = pltpu.get_barrier_semaphore()
+    pl.semaphore_signal(barrier, 1, device_id=partner, device_id_type=pl.DeviceIdType.MESH)
+    pl.semaphore_wait(barrier, 1)
     copy = pltpu.make_async_remote_copy(
         src_ref=x_ref,
         dst_ref=o_ref,
         send_sem=send_sem,
         recv_sem=recv_sem,
-        device_id=(segment, me + 1 - 2 * lax.rem(me, 2)),
+        device_id=partner,
         device_id_type=pl.DeviceIdType.MESH,
     )
     copy.start()
     copy.wait()
 
 
-def pair_exchange(value):
+def pair_exchange(value, collective):
     return pl.pallas_call(
         pair_exchange_kernel,
         out_shape=jax.ShapeDtypeStruct(value.shape, value.dtype),
         in_specs=[pl.BlockSpec(memory_space=pltpu.VMEM)],
         out_specs=pl.BlockSpec(memory_space=pltpu.VMEM),
         scratch_shapes=[pltpu.SemaphoreType.DMA(()), pltpu.SemaphoreType.DMA(())],
-        compiler_params=pltpu.CompilerParams(has_side_effects=True),
+        compiler_params=pltpu.CompilerParams(collective_id=collective, has_side_effects=True),
     )(value)
 
 
@@ -116,16 +129,16 @@
     for tick in range(segment_count):
         normed = normalize(carried, row_gain)
         pieces = jnp.stack([normed[0:2], normed[1:3]]).reshape(2, piece_rows, LANES)
-        own_core = chip_exchange(pieces, chips, per_expert // 2)
-        other_core = pair_exchange(own_core)
+        own_core = chip_exchange(pieces, chips, per_expert // 2, 0)
+        other_core = pair_exchange(own_core, 1)
         block_rows = jnp.concatenate([own_core, other_core]).reshape(shard_count * 2 * local_rows, width)
         gate_val = jnp.dot(block_rows, gate_part, preferred_element_type=jnp.float32)
         up_val = jnp.dot(block_rows, up_part, preferred_element_type=jnp.float32)
         hidden = (jax.nn.silu(gate_val) * up_val).astype(jnp.bfloat16)
         partial_sum = jnp.dot(hidden, down_part, preferred_element_type=jnp.float32)
         partial_sum = partial_sum.reshape(2, chips, piece_rows, LANES)
-        chip_sum = partial_sum[0] + pair_exchange(partial_sum[1])
-        received = chip_exchange(chip_sum.astype(jnp.bfloat16), chips, 0).astype(jnp.float32)
+        chip_sum = partial_sum[0] + pair_exchange(partial_sum[1], 2)
+        received = chip_exchange(chip_sum.astype(jnp.bfloat16), chips, 0, 3).astype(jnp.float32)
         received = received.reshape(2, chips // 2, 2, local_rows, width)
         first, second = jnp.sum(received[0], axis=0), jnp.sum(received[1], axis=0)
         middle = jnp.where(zero_blocks >= 2, first[1], second[0])

time: 561 us -> 417 us (0.74)
  Pallas kernels: 408 us -> 264 us
    pallas_call x8, Pallas kernels: 127 us -> 53.2 us  [pair_exchange(): pl.pallas_call(pair_exchange_kernel, out_shape=jax.ShapeDtypeStruct(value...]
    pallas_call x8, Pallas kernels: 281 us -> 211 us  [chip_exchange(): pl.pallas_call(functools.partial(chip_exchange_kernel, chips, per_expert)...]
where the time goes in v3:
time: 417 us; the launch traced here: 415 us
  Pallas kernels  264 us (63%)
  local copies, waits for them, and re-layouts  57.4 us (14%)
  matrix products  40.7 us (10%)
  other arithmetic  37.3 us (9%)
  starting transfers between devices  10.6 us (3%)
    pallas_call x8, Pallas kernels, chip_exchange(): pl.pallas_call(functools.partial(chip_exchange_kernel, chips, per_expert)...  211 us
    pallas_call x8, Pallas kernels, pair_exchange(): pl.pallas_call(pair_exchange_kernel, out_shape=jax.ShapeDtypeStruct(value...  53.2 us
    dot_general x4, matrix products, shards(): partial_sum = jnp.dot(hidden, down_part, preferred_element_type=jnp.float32)  24.1 us
    squeeze x8, local copies, waits for them, and re-layouts, shards(): chip_sum = partial_sum[0] + pair_exchange(partial_sum[1], 2)  20.5 us
    dot_general x4, matrix products, shards(): jnp.dot(block_rows, gate_part, preferred_element_type=jnp.float32)  16.6 us
    slice x4, local copies, waits for them, and re-layouts, shards(): chip_sum = partial_sum[0] + pair_exchange(partial_sum[1], 2)  15.7 us
    reshape x4, local copies, waits for them, and re-layouts, shards(): jnp.concatenate([own_core, other_core])  14.8 us
    convert_element_type x4, other arithmetic, shards(): chip_sum.astype(jnp.bfloat16)  12 us
  transfers between devices with their start and end apart: 3, of which 3 were waited for; matrix products, arithmetic and copies ran while one was open for 0% of the time, Pallas kernels for 0%

profile of v3, /device:TPU:1, one launch (start us, length us, event | category | flops | bytes accessed | tf_op | source)
XLA Modules:
  0.0 414.6 jit_solution(10450004366217499028)
XLA Ops:
  2.7 30.1 %shard_map.73.x_ref = bf16[32,96,128]{2,1,0:T(8,128)(2,1)} custom-call(bf16[2,96,128]{2,1,0:T(8,128)(2,1)} %pad_maximum_fusion.4.x_ref), custom_call_target="tpu_custom_call" | custom-call | tf_op jit(solution)/shard_map/pallas_call | solution.py:71
  32.8 5.8 %shard_map.74 = bf16[32,96,128]{2,1,0:T(8,128)(2,1)} custom-call(bf16[32,96,128]{2,1,0:T(8,128)(2,1)} %shard_map.73.x_ref), custom_call_target="tpu_custom_call" | custom-call | tf_op jit(solution)/shard_map/pallas_call | solution.py:101
  41.3 3.7 reshape.200
  45.0 4.2 %fusion.22 = f32[256,512]{1,0:T(8,128)} fusion(bf16[256,3072]{1,0:T(8,128)(2,1)} %reshape.200, bf16[1,3072,512]{2,1,0:T(8,128)(2,1)} %param.9), kind=kOutput, calls=%fused_computation.22 | convolution fusion | flops 805306368 | bytes 5242880 | tf_op jit(solution)/shard_map/dot_general | solution.py:135
  49.2 6.0 %fusion.6 = f32[256,3072]{1,0:T(8,128)} fusion(bf16[1,512,3072]{2,1,0:T(8,128)(2,1)S(1)} %copy-done, bf16[256,3072]{1,0:T(8,128)(2,1)} %reshape.200, bf16[1,3072,512]{2,1,0:T(8,128)(2,1)} %param.10, f32[256,512]{1,0:T(8,128)} %fusion.22), kind=kOutput, calls=%fused_computation.6 | convolution fusion | flops 1611399168 | bytes 11534336 | tf_op jit(solution)/shard_map/dot_general | solution.py:138
  55.2 3.9 fusion.104
  61.6 6.0 %shard_map.75 = f32[32,96,128]{2,1,0:T(8,128)} custom-call(f32[32,96,128]{2,1,0:T(8,128)} %squeeze.26.x_ref), custom_call_target="tpu_custom_call" | custom-call | tf_op jit(solution)/shard_map/pallas_call | solution.py:101
  73.2 26.7 %shard_map.76 = bf16[32,96,128]{2,1,0:T(8,128)(2,1)} custom-call(bf16[32,96,128]{2,1,0:T(8,128)(2,1)} %add_convert_fusion.3.x_ref), custom_call_target="tpu_custom_call" | custom-call | tf_op jit(solution)/shard_map/pallas_call | solution.py:71
  107.4 24.6 %shard_map.77.x_ref = bf16[32,96,128]{2,1,0:T(8,128)(2,1)} custom-call(bf16[2,96,128]{2,1,0:T(8,128)(2,1)} %pad_maximum_fusion.5.x_ref), custom_call_target="tpu_custom_call" | custom-call | tf_op jit(solution)/shard_map/pallas_call | solution.py:71
  132.0 7.4 %shard_map.78 = bf16[32,96,128]{2,1,0:T(8,128)(2,1)} custom-call(bf16[32,96,128]{2,1,0:T(8,128)(2,1)} %shard_map.77.x_ref), custom_call_target="tpu_custom_call" | custom-call | tf_op jit(solution)/shard_map/pallas_call | solution.py:101
  142.1 3.7 reshape.201
  145.8 4.2 %fusion.20 = f32[256,512]{1,0:T(8,128)} fusion(bf16[256,3072]{1,0:T(8,128)(2,1)} %reshape.201, bf16[1,3072,512]{2,1,0:T(8,128)(2,1)} %param.9), kind=kOutput, calls=%fused_computation.20 | convolution fusion | flops 805306368 | bytes 5242880 | tf_op jit(solution)/shard_map/dot_general | solution.py:135
  150.0 6.0 %fusion.4 = f32[256,3072]{1,0:T(8,128)} fusion(bf16[1,512,3072]{2,1,0:T(8,128)(2,1)S(1)} %copy-done, bf16[256,3072]{1,0:T(8,128)(2,1)} %reshape.201, bf16[1,3072,512]{2,1,0:T(8,128)(2,1)} %param.10, f32[256,512]{1,0:T(8,128)} %fusion.20), kind=kOutput, calls=%fused_computation.4 | convolution fusion | flops 1611399168 | bytes 11534336 | tf_op jit(solution)/shard_map/dot_general | solution.py:138
  156.0 3.9 fusion.103
  162.5 6.0 %shard_map.79 = f32[32,96,128]{2,1,0:T(8,128)} custom-call(f32[32,96,128]{2,1,0:T(8,128)} %squeeze.56.x_ref), custom_call_target="tpu_custom_call" | custom-call | tf_op jit(solution)/shard_map/pallas_call | solution.py:101
  174.0 27.8 %shard_map.80 = bf16[32,96,128]{2,1,0:T(8,128)(2,1)} custom-call(bf16[32,96,128]{2,1,0:T(8,128)(2,1)} %add_convert_fusion.2.x_ref), custom_call_target="tpu_custom_call" | custom-call | tf_op jit(solution)/shard_map/pallas_call | solution.py:71
  203.4 3.8 collective-permute-start.1
  209.1 23.3 %shard_map.81.x_ref = bf16[32,96,128]{2,1,0:T(8,128)(2,1)} custom-call(bf16[2,96,128]{2,1,0:T(8,128)(2,1)} %pad_maximum_fusion.6.x_ref), custom_call_target="tpu_custom_call" | custom-call | tf_op jit(solution)/shard_map/pallas_call | solution.py:71
  232.4 8.0 %shard_map.82 = bf16[32,96,128]{2,1,0:T(8,128)(2,1)} custom-call(bf16[32,96,128]{2,1,0:T(8,128)(2,1)} %shard_map.81.x_ref), custom_call_target="tpu_custom_call" | custom-call | tf_op jit(solution)/shard_map/pallas_call | solution.py:101
  243.1 3.7 reshape.202
  246.8 4.2 %fusion.18 = f32[256,512]{1,0:T(8,128)} fusion(bf16[256,3072]{1,0:T(8,128)(2,1)} %reshape.202, bf16[1,3072,512]{2,1,0:T(8,128)(2,1)} %param.9), kind=kOutput, calls=%fused_computation.18 | convolution fusion | flops 805306368 | bytes 5242880 | tf_op jit(solution)/shard_map/dot_general | solution.py:135
  251.0 6.0 %fusion.2 = f32[256,3072]{1,0:T(8,128)} fusion(bf16[1,512,3072]{2,1,0:T(8,128)(2,1)S(1)} %copy-done, bf16[256,3072]{1,0:T(8,128)(2,1)} %reshape.202, bf16[1,3072,512]{2,1,0:T(8,128)(2,1)} %param.10, f32[256,512]{1,0:T(8,128)} %fusion.18), kind=kOutput, calls=%fused_computation.2 | convolution fusion | flops 1611399168 | bytes 11534336 | tf_op jit(solution)/shard_map/dot_general | solution.py:138
  257.0 3.9 fusion.102
  263.4 6.0 %shard_map.83 = f32[32,96,128]{2,1,0:T(8,128)} custom-call(f32[32,96,128]{2,1,0:T(8,128)} %squeeze.58.x_ref), custom_call_target="tpu_custom_call" | custom-call | tf_op jit(solution)/shard_map/pallas_call | solution.py:101
  275.0 27.6 %shard_map.84 = bf16[32,96,128]{2,1,0:T(8,128)(2,1)} custom-call(bf16[32,96,128]{2,1,0:T(8,128)(2,1)} %add_convert_fusion.1.x_ref), custom_call_target="tpu_custom_call" | custom-call | tf_op jit(solution)/shard_map/pallas_call | solution.py:71
  314.1 23.3 %shard_map.85.x_ref = bf16[32,96,128]{2,1,0:T(8,128)(2,1)} custom-call(bf16[2,96,128]{2,1,0:T(8,128)(2,1)} %pad_maximum_fusion.7.x_ref), custom_call_target="tpu_custom_call" | custom-call | tf_op jit(solution)/shard_map/pallas_call | solution.py:71
  337.4 8.0 %shard_map.86 = bf16[32,96,128]{2,1,0:T(8,128)(2,1)} custom-call(bf16[32,96,128]{2,1,0:T(8,128)(2,1)} %shard_map.85.x_ref), custom_call_target="tpu_custom_call" | custom-call | tf_op jit(solution)/shard_map/pallas_call | solution.py:101
  351.8 4.2 %fusion.16 = f32[256,512]{1,0:T(8,128)} fusion(bf16[256,3072]{1,0:T(8,128)(2,1)} %reshape.203, bf16[1,3072,512]{2,1,0:T(8,128)(2,1)} %param.9), kind=kOutput, calls=%fused_computation.16 | convolution fusion | flops 805306368 | bytes 5242880 | tf_op jit(solution)/shard_map/dot_general | solution.py:135
  355.9 6.0 %fusion = f32[256,3072]{1,0:T(8,128)} fusion(bf16[1,512,3072]{2,1,0:T(8,128)(2,1)S(1)} %copy-done, bf16[256,3072]{1,0:T(8,128)(2,1)} %reshape.203, bf16[1,3072,512]{2,1,0:T(8,128)(2,1)} %param.10, f32[256,512]{1,0:T(8,128)} %fusion.16), kind=kOutput, calls=%fused_computation | convolution fusion | flops 1611399168 | bytes 11534336 | tf_op jit(solution)/shard_map/dot_general | solution.py:138
  361.9 3.9 fusion.101
  368.4 6.0 %shard_map.87 = f32[32,96,128]{2,1,0:T(8,128)} custom-call(f32[32,96,128]{2,1,0:T(8,128)} %squeeze.60.x_ref), custom_call_target="tpu_custom_call" | custom-call | tf_op jit(solution)/shard_map/pallas_call | solution.py:101
  380.0 27.6 %shard_map.88 = bf16[32,96,128]{2,1,0:T(8,128)(2,1)} custom-call(bf16[32,96,128]{2,1,0:T(8,128)(2,1)} %add_convert_fusion.x_ref), custom_call_target="tpu_custom_call" | custom-call | tf_op jit(solution)/shard_map/pallas_call | solution.py:71
  (87 shorter events, 78.0 us)
Async XLA Ops:
  0.0 49.2 %copy-start = (bf16[1,512,3072]{2,1,0:T(8,128)(2,1)S(1)}, bf16[1,512,3072]{2,1,0:T(8,128)(2,1)}, u32[]{:S(2)}) copy-start(bf16[1,512,3072]{2,1,0:T(8,128)(2,1)} %param.11) | copy-start | bytes 9437188
  101.2 0.9 copy-start.3
  101.2 0.9 copy-start.1
  101.2 5.4 %copy-start.2 = (f32[1,3072]{1,0:T(1,128)S(1)}, f32[1,3072]{1,0:T(1,128)}, u32[]{:S(2)}) copy-start(f32[1,3072]{1,0:T(1,128)} %param.8) | copy-start | bytes 36868
  102.2 4.2 %collective-permute-start = (bf16[3,2,3072]{2,1,0:T(2,128)(2,1)S(1)}, bf16[3,2,3072]{2,1,0:T(2,128)(2,1)S(1)}, u32[]{:S(2)}, u32[]{:S(2)}) collective-permute-start(bf16[3,2,3072]{2,1,0:T(2,128)(2,1)S(1)} %fusion.83), channel_id=1, source_target_pairs={{0,64},{64,128},{128,192},{1,65},{65,129},{129,193},{2,66},{66,130... | collective-permute-start | bytes 110600 | tf_op jit(solution)/shard_map/ppermute | solution.py:17
  203.4 4.7 %collective-permute-start.1 = (bf16[3,2,3072]{2,1,0:T(2,128)(2,1)S(1)}, bf16[3,2,3072]{2,1,0:T(2,128)(2,1)S(1)}, u32[]{:S(2)}, u32[]{:S(2)}) collective-permute-start(bf16[3,2,3072]{2,1,0:T(2,128)(2,1)S(1)} %fusion.87), channel_id=1, source_target_pairs={{0,64},{64,128},{128,192},{1,65},{65,129},{129,193},{2,66},{66,130... | collective-permute-start | bytes 110600 | tf_op jit(solution)/shard_map/ppermute | solution.py:17
  304.8 5.0 %collective-permute-start.2 = (bf16[3,2,3072]{2,1,0:T(2,128)(2,1)}, bf16[3,2,3072]{2,1,0:T(2,128)(2,1)S(1)}, u32[]{:S(2)}, u32[]{:S(2)}) collective-permute-start(bf16[3,2,3072]{2,1,0:T(2,128)(2,1)} %fusion.91), channel_id=1, source_target_pairs={{0,64},{64,128},{128,192},{1,65},{65,129},{129,193},{2,66},{66,130... | collective-permute-start | bytes 110600 | tf_op jit(solution)/shard_map/ppermute | solution.py:17

commit v4 on v3

--- a/solution.py
+++ b/solution.py
@@ -23,20 +23,24 @@
     return (values * scale * row_gain).astype(jnp.bfloat16)
 
 
-def chip_exchange_kernel(chips, per_expert, x_ref, o_ref, send_sem, recv_sem):
+def signed(index):
+    return (index + 1) // 2 * (2 * lax.rem(index, 2) - 1)
+
+
+def chip_exchange_kernel(ring_y, ring_z, per_expert, x_ref, o_ref, send_sem, recv_sem):
     me = lax.axis_index("shard")
     segment = lax.axis_index("segment")
     core = lax.rem(me, 2)
     chip = me // 2
-    barrier = pltpu.get_barrier_semaphore()
-
-    def greet(step, carry):
-        dest = lax.rem(chip + step, chips) * 2 + core
-        pl.semaphore_signal(barrier, 1, device_id=(segment, dest), device_id_type=pl.DeviceIdType.MESH)
-        return carry
-
-    lax.fori_loop(1, chips, greet, 0)
-    pl.semaphore_wait(barrier, chips - 1)
+    y, z = chip // ring_z, lax.rem(chip, ring_z)
+    chips = ring_y * ring_z
+
+    def peer(step, sign):
+        z_index = lax.rem(step, ring_z)
+        y_index = lax.rem(step // ring_z + z_index, ring_y)
+        peer_y = lax.rem(y + sign * signed(y_index) + ring_y, ring_y)
+        peer_z = lax.rem(z + sign * signed(z_index) + ring_z, ring_z)
+        return peer_y * ring_z + peer_z
 
     def source(dest_chip):
         return x_ref.at[dest_chip // per_expert] if per_expert else x_ref.at[dest_chip]
@@ -51,25 +55,37 @@
             device_id_type=pl.DeviceIdType.MESH,
         )
 
+    barrier = pltpu.get_barrier_semaphore()
+
+    def greet(step, carry):
+        dest = peer(step, 1) * 2 + core
+        pl.semaphore_signal(barrier, 1, device_id=(segment, dest), device_id_type=pl.DeviceIdType.MESH)
+        return carry
+
+    lax.fori_loop(1, chips, greet, 0)
+    pl.semaphore_wait(barrier, chips - 1)
+
     def start(step, carry):
-        copy_of(lax.rem(chip + step, chips), chip).start()
+        copy_of(peer(step, 1), chip).start()
         return carry
 
     lax.fori_loop(1, chips, start, 0)
     o_ref[chip] = source(chip)[...]
 
     def finish(step, carry):
-        copy_of(lax.rem(chip + step, chips), chip).wait_send()
-        copy_of(lax.rem(chip + chips - step, chips), lax.rem(chip + chips - step, chips)).wait_recv()
+        copy_of(peer(step, 1), chip).wait_send()
+        origin = peer(step, -1)
+        copy_of(origin, origin).wait_recv()
         return carry
 
     lax.fori_loop(1, chips, finish, 0)
 
 
-def chip_exchange(pieces, chips, per_expert, collective):
+def chip_exchange(pieces, ring_y, ring_z, per_expert, collective):
     rows, lanes = pieces.shape[1], pieces.shape[2]
+    chips = ring_y * ring_z
     return pl.pallas_call(
-        functools.partial(chip_exchange_kernel, chips, per_expert),
+        functools.partial(chip_exchange_kernel, ring_y, ring_z, per_expert),
         out_shape=jax.ShapeDtypeStruct((chips, rows, lanes), pieces.dtype),
         in_specs=[pl.BlockSpec(memory_space=pltpu.VMEM)],
         out_specs=pl.BlockSpec(memory_space=pltpu.VMEM),
@@ -78,15 +94,48 @@
     )(pieces)
 
 
-def pair_exchange_kernel(x_ref, o_ref, send_sem, recv_sem):
+def pair_barrier():
     me = lax.axis_index("shard")
-    segment = lax.axis_index("segment")
-    partner = (segment, me + 1 - 2 * lax.rem(me, 2))
+    partner = (lax.axis_index("segment"), me + 1 - 2 * lax.rem(me, 2))
     barrier = pltpu.get_barrier_semaphore()
     pl.semaphore_signal(barrier, 1, device_id=partner, device_id_type=pl.DeviceIdType.MESH)
     pl.semaphore_wait(barrier, 1)
+    return partner
+
+
+def pair_gather_kernel(x_ref, o_ref, send_sem, recv_sem, local_sem):
+    partner = pair_barrier()
     copy = pltpu.make_async_remote_copy(
         src_ref=x_ref,
+        dst_ref=o_ref.at[1],
+        send_sem=send_sem,
+        recv_sem=recv_sem,
+        device_id=partner,
+        device_id_type=pl.DeviceIdType.MESH,
+    )
+    copy.start()
+    local = pltpu.make_async_copy(x_ref, o_ref.at[0], local_sem)
+    local.start()
+    local.wait()
+    copy.wait()
+
+
+def pair_gather(value, collective):
+    return pl.pallas_call(
+        pair_gather_kernel,
+        out_shape=jax.ShapeDtypeStruct((2,) + value.shape, value.dtype),
+        in_specs=[pl.BlockSpec(memory_space=pltpu.VMEM)],
+        out_specs=pl.BlockSpec(memory_space=pltpu.VMEM),
+        scratch_shapes=[pltpu.SemaphoreType.DMA(()), pltpu.SemaphoreType.DMA(()), pltpu.SemaphoreType.DMA(())],
+        compiler_params=pltpu.CompilerParams(collective_id=collective, has_side_effects=True),
+    )(value)
+
+
+def pair_send_kernel(x_ref, o_ref, send_sem, recv_sem):
+    partner = pair_barrier()
+    rows = o_ref.shape[0]
+    copy = pltpu.make_async_remote_copy(
+        src_ref=x_ref.at[pl.ds(rows, rows)],
         dst_ref=o_ref,
         send_sem=send_sem,
         recv_sem=recv_sem,
@@ -97,10 +146,10 @@
     copy.wait()
 
 
-def pair_exchange(value, collective):
+def pair_send(value, collective):
     return pl.pallas_call(
-        pair_exchange_kernel,
-        out_shape=jax.ShapeDtypeStruct(value.shape, value.dtype),
+        pair_send_kernel,
+        out_shape=jax.ShapeDtypeStruct((value.shape[0] // 2, value.shape[1]), value.dtype),
         in_specs=[pl.BlockSpec(memory_space=pltpu.VMEM)],
         out_specs=pl.BlockSpec(memory_space=pltpu.VMEM),
         scratch_shapes=[pltpu.SemaphoreType.DMA(()), pltpu.SemaphoreType.DMA(())],
@@ -124,21 +173,23 @@
     width = tokens.shape[2]
     piece_rows = 2 * local_rows * width // LANES
     chips = shard_count // 2
+    ring_z = 8
+    ring_y = chips // ring_z
     carried = tokens
     stored = jnp.zeros_like(tokens)
     for tick in range(segment_count):
         normed = normalize(carried, row_gain)
         pieces = jnp.stack([normed[0:2], normed[1:3]]).reshape(2, piece_rows, LANES)
-        own_core = chip_exchange(pieces, chips, per_expert // 2, 0)
-        other_core = pair_exchange(own_core, 1)
-        block_rows = jnp.concatenate([own_core, other_core]).reshape(shard_count * 2 * local_rows, width)
+        own_core = chip_exchange(pieces, ring_y, ring_z, per_expert // 2, 0)
+        block_rows = pair_gather(own_core, 1).reshape(shard_count * 2 * local_rows, width)
         gate_val = jnp.dot(block_rows, gate_part, preferred_element_type=jnp.float32)
         up_val = jnp.dot(block_rows, up_part, preferred_element_type=jnp.float32)
         hidden = (jax.nn.silu(gate_val) * up_val).astype(jnp.bfloat16)
         partial_sum = jnp.dot(hidden, down_part, preferred_element_type=jnp.float32)
-        partial_sum = partial_sum.reshape(2, chips, piece_rows, LANES)
-        chip_sum = partial_sum[0] + pair_exchange(partial_sum[1], 2)
-        received = chip_exchange(chip_sum.astype(jnp.bfloat16), chips, 0, 3).astype(jnp.float32)
+        half = partial_sum.shape[0] // 2
+        chip_sum = (partial_sum[:half] + pair_send(partial_sum, 2)).astype(jnp.bfloat16)
+        received = chip_exchange(chip_sum.reshape(chips, piece_rows, LANES), ring_y, ring_z, 0, 3)
+        received = received.astype(jnp.float32)
         received = received.reshape(2, chips // 2, 2, local_rows, width)
         first, second = jnp.sum(received[0], axis=0), jnp.sum(received[1], axis=0)
         middle = jnp.where(zero_blocks >= 2, first[1], second[0])

time: 417 us -> 384 us (0.921)
  local copies, waits for them, and re-layouts: 57.4 us -> 30 us
  other arithmetic: 37.3 us -> 26.5 us
  Pallas kernels: 264 us -> 270 us
    squeeze x8 -> x0, local copies, waits for them, and re-layouts: 20.5 us -> none  [shards(): chip_sum = partial_sum[0] + pair_exchange(partial_sum[1], 2)]
    slice x4 -> x0, local copies, waits for them, and re-layouts: 15.7 us -> none  [shards(): chip_sum = partial_sum[0] + pair_exchange(partial_sum[1], 2)]
    concatenate x4 -> x0, other arithmetic: 10.6 us -> none  [shards(): jnp.concatenate([own_core, other_core])]
    reshape x4 -> x8, local copies, waits for them, and re-layouts: 14.8 us -> 23.5 us  [the longest x4 14.8 us: shards(): pair_gather(own_core, 1).reshape(shard_count * 2 * local_rows, width)]
    pallas_call x16, Pallas kernels: 264 us -> 270 us  [the longest x8 217 us: chip_exchange(): pl.pallas_call(functools.partial(chip_exchange_kernel, ring_y, ring_z, pe...]
where the time goes in v4:
time: 384 us; the launch traced here: 383 us
  Pallas kernels  270 us (70%)
  matrix products  40.7 us (11%)
  local copies, waits for them, and re-layouts  30 us (8%)
  other arithmetic  26.5 us (7%)
  starting transfers between devices  10.6 us (3%)
    pallas_call x8, Pallas kernels, chip_exchange(): pl.pallas_call(functools.partial(chip_exchange_kernel, ring_y, ring_z, pe...  217 us
    pallas_call x4, Pallas kernels, pair_gather(): pl.pallas_call(pair_gather_kernel, out_shape=jax.ShapeDtypeStruct((2,) +...  27.6 us
    pallas_call x4, Pallas kernels, pair_send(): pl.pallas_call(pair_send_kernel, out_shape=jax.ShapeDtypeStruct((value.sh...  25.8 us
    dot_general x4, matrix products, shards(): partial_sum = jnp.dot(hidden, down_part, preferred_element_type=jnp.float32)  24 us
    dot_general x4, matrix products, shards(): jnp.dot(block_rows, gate_part, preferred_element_type=jnp.float32)  16.6 us
    reshape x4, local copies, waits for them, and re-layouts, shards(): pair_gather(own_core, 1).reshape(shard_count * 2 * local_rows, width)  14.8 us
    convert_element_type x4, other arithmetic, shards(): (partial_sum[:half] + pair_send(partial_sum, 2)).astype(jnp.bfloat16)  11.8 us
    ppermute x3, starting transfers between devices, shifted(): lax.ppermute(value, axis, [(source, source + steps) for source in range(i...  10.6 us
  transfers between devices with their start and end apart: 3, of which 3 were waited for; matrix products, arithmetic and copies ran while one was open for 0% of the time, Pallas kernels for 0%

profile of v4, /device:TPU:1, one launch (start us, length us, event | category | flops | bytes accessed | tf_op | source)
XLA Modules:
  0.0 382.5 jit_solution(7850697597885322819)
XLA Ops:
  2.7 30.0 %shard_map.73.x_ref = bf16[32,96,128]{2,1,0:T(8,128)(2,1)} custom-call(bf16[2,96,128]{2,1,0:T(8,128)(2,1)} %pad_maximum_fusion.x_ref), custom_call_target="tpu_custom_call" | custom-call | tf_op jit(solution)/shard_map/pallas_call | solution.py:87
  32.7 6.5 %shard_map.74 = bf16[2,32,96,128]{3,2,1,0:T(8,128)(2,1)} custom-call(bf16[32,96,128]{2,1,0:T(8,128)(2,1)} %shard_map.73.x_ref), custom_call_target="tpu_custom_call" | custom-call | tf_op jit(solution)/shard_map/pallas_call | solution.py:124
  39.1 3.7 reshape.192
  42.9 4.2 %fusion.22 = f32[256,512]{1,0:T(8,128)} fusion(bf16[256,3072]{1,0:T(8,128)(2,1)} %reshape.192, bf16[1,3072,512]{2,1,0:T(8,128)(2,1)} %param.9), kind=kOutput, calls=%fused_computation.22 | convolution fusion | flops 805306368 | bytes 5242880 | tf_op jit(solution)/shard_map/dot_general | solution.py:185
  47.0 6.0 %fusion.6.x_ref = f32[256,3072]{1,0:T(8,128)} fusion(bf16[1,512,3072]{2,1,0:T(8,128)(2,1)S(1)} %copy-done, bf16[256,3072]{1,0:T(8,128)(2,1)} %reshape.192, bf16[1,3072,512]{2,1,0:T(8,128)(2,1)} %param.10, f32[256,512]{1,0:T(8,128)} %fusion.22), kind=kOutput, calls=%fused_computation.6 | convolution fusion | flops 1611399168 | bytes 11534336 | tf_op jit(solution)/shard_map/dot_general | solution.py:188
  53.0 6.5 %shard_map.75 = f32[128,3072]{1,0:T(8,128)} custom-call(f32[256,3072]{1,0:T(8,128)} %fusion.6.x_ref), custom_call_target="tpu_custom_call" | custom-call | tf_op jit(solution)/shard_map/pallas_call | solution.py:150
  64.6 27.4 %shard_map.76 = bf16[32,96,128]{2,1,0:T(8,128)(2,1)} custom-call(bf16[32,96,128]{2,1,0:T(8,128)(2,1)} %reshape.193.x_ref), custom_call_target="tpu_custom_call" | custom-call | tf_op jit(solution)/shard_map/pallas_call | solution.py:87
  94.4 3.1 collective-permute-start
  99.5 25.5 %shard_map.77.x_ref = bf16[32,96,128]{2,1,0:T(8,128)(2,1)} custom-call(bf16[2,96,128]{2,1,0:T(8,128)(2,1)} %pad_maximum_fusion.1.x_ref), custom_call_target="tpu_custom_call" | custom-call | tf_op jit(solution)/shard_map/pallas_call | solution.py:87
  125.1 7.2 %shard_map.78 = bf16[2,32,96,128]{3,2,1,0:T(8,128)(2,1)} custom-call(bf16[32,96,128]{2,1,0:T(8,128)(2,1)} %shard_map.77.x_ref), custom_call_target="tpu_custom_call" | custom-call | tf_op jit(solution)/shard_map/pallas_call | solution.py:124
  132.3 3.7 reshape.194
  136.0 4.2 %fusion.20 = f32[256,512]{1,0:T(8,128)} fusion(bf16[256,3072]{1,0:T(8,128)(2,1)} %reshape.194, bf16[1,3072,512]{2,1,0:T(8,128)(2,1)} %param.9), kind=kOutput, calls=%fused_computation.20 | convolution fusion | flops 805306368 | bytes 5242880 | tf_op jit(solution)/shard_map/dot_general | solution.py:185
  140.1 6.0 %fusion.4.x_ref = f32[256,3072]{1,0:T(8,128)} fusion(bf16[1,512,3072]{2,1,0:T(8,128)(2,1)S(1)} %copy-done, bf16[256,3072]{1,0:T(8,128)(2,1)} %reshape.194, bf16[1,3072,512]{2,1,0:T(8,128)(2,1)} %param.10, f32[256,512]{1,0:T(8,128)} %fusion.20), kind=kOutput, calls=%fused_computation.4 | convolution fusion | flops 1611399168 | bytes 11534336 | tf_op jit(solution)/shard_map/dot_general | solution.py:188
  146.1 6.5 %shard_map.79 = f32[128,3072]{1,0:T(8,128)} custom-call(f32[256,3072]{1,0:T(8,128)} %fusion.4.x_ref), custom_call_target="tpu_custom_call" | custom-call | tf_op jit(solution)/shard_map/pallas_call | solution.py:150
  152.6 2.9 fusion.26
  157.7 28.1 %shard_map.80 = bf16[32,96,128]{2,1,0:T(8,128)(2,1)} custom-call(bf16[32,96,128]{2,1,0:T(8,128)(2,1)} %reshape.195.x_ref), custom_call_target="tpu_custom_call" | custom-call | tf_op jit(solution)/shard_map/pallas_call | solution.py:87
  187.5 3.8 %collective-permute-start.1 = (bf16[3,2,3072]{2,1,0:T(2,128)(2,1)S(1)}, bf16[3,2,3072]{2,1,0:T(2,128)(2,1)S(1)}, u32[]{:S(2)}, u32[]{:S(2)}) collective-permute-start(bf16[3,2,3072]{2,1,0:T(2,128)(2,1)S(1)} %fusion.91), channel_id=1, source_target_pairs={{0,64},{64,128},{128,192},{1,65},{65,129},{129,193},{2,66},{66,130... | collective-permute-start | bytes 110600 | tf_op jit(solution)/shard_map/ppermute | solution.py:17
  193.1 24.3 %shard_map.81.x_ref = bf16[32,96,128]{2,1,0:T(8,128)(2,1)} custom-call(bf16[2,96,128]{2,1,0:T(8,128)(2,1)} %pad_maximum_fusion.2.x_ref), custom_call_target="tpu_custom_call" | custom-call | tf_op jit(solution)/shard_map/pallas_call | solution.py:87
  217.5 7.3 %shard_map.82 = bf16[2,32,96,128]{3,2,1,0:T(8,128)(2,1)} custom-call(bf16[32,96,128]{2,1,0:T(8,128)(2,1)} %shard_map.81.x_ref), custom_call_target="tpu_custom_call" | custom-call | tf_op jit(solution)/shard_map/pallas_call | solution.py:124
  224.8 3.7 reshape.196
  228.5 4.2 %fusion.18 = f32[256,512]{1,0:T(8,128)} fusion(bf16[256,3072]{1,0:T(8,128)(2,1)} %reshape.196, bf16[1,3072,512]{2,1,0:T(8,128)(2,1)} %param.9), kind=kOutput, calls=%fused_computation.18 | convolution fusion | flops 805306368 | bytes 5242880 | tf_op jit(solution)/shard_map/dot_general | solution.py:185
  232.6 6.0 %fusion.2.x_ref = f32[256,3072]{1,0:T(8,128)} fusion(bf16[1,512,3072]{2,1,0:T(8,128)(2,1)S(1)} %copy-done, bf16[256,3072]{1,0:T(8,128)(2,1)} %reshape.196, bf16[1,3072,512]{2,1,0:T(8,128)(2,1)} %param.10, f32[256,512]{1,0:T(8,128)} %fusion.18), kind=kOutput, calls=%fused_computation.2 | convolution fusion | flops 1611399168 | bytes 11534336 | tf_op jit(solution)/shard_map/dot_general | solution.py:188
  238.6 6.5 %shard_map.83 = f32[128,3072]{1,0:T(8,128)} custom-call(f32[256,3072]{1,0:T(8,128)} %fusion.2.x_ref), custom_call_target="tpu_custom_call" | custom-call | tf_op jit(solution)/shard_map/pallas_call | solution.py:150
  250.2 28.1 %shard_map.84 = bf16[32,96,128]{2,1,0:T(8,128)(2,1)} custom-call(bf16[32,96,128]{2,1,0:T(8,128)(2,1)} %reshape.197.x_ref), custom_call_target="tpu_custom_call" | custom-call | tf_op jit(solution)/shard_map/pallas_call | solution.py:87
  280.5 3.6 collective-permute-start.2
  289.8 25.8 %shard_map.85.x_ref = bf16[32,96,128]{2,1,0:T(8,128)(2,1)} custom-call(bf16[2,96,128]{2,1,0:T(8,128)(2,1)} %pad_maximum_fusion.3.x_ref), custom_call_target="tpu_custom_call" | custom-call | tf_op jit(solution)/shard_map/pallas_call | solution.py:87
  315.6 6.7 %shard_map.86 = bf16[2,32,96,128]{3,2,1,0:T(8,128)(2,1)} custom-call(bf16[32,96,128]{2,1,0:T(8,128)(2,1)} %shard_map.85.x_ref), custom_call_target="tpu_custom_call" | custom-call | tf_op jit(solution)/shard_map/pallas_call | solution.py:124
  322.2 3.7 reshape.198
  325.9 4.2 %fusion.16 = f32[256,512]{1,0:T(8,128)} fusion(bf16[256,3072]{1,0:T(8,128)(2,1)} %reshape.198, bf16[1,3072,512]{2,1,0:T(8,128)(2,1)} %param.9), kind=kOutput, calls=%fused_computation.16 | convolution fusion | flops 805306368 | bytes 5242880 | tf_op jit(solution)/shard_map/dot_general | solution.py:185
  330.1 6.0 %fusion.x_ref = f32[256,3072]{1,0:T(8,128)} fusion(bf16[1,512,3072]{2,1,0:T(8,128)(2,1)S(1)} %copy-done, bf16[256,3072]{1,0:T(8,128)(2,1)} %reshape.198, bf16[1,3072,512]{2,1,0:T(8,128)(2,1)} %param.10, f32[256,512]{1,0:T(8,128)} %fusion.16), kind=kOutput, calls=%fused_computation | convolution fusion | flops 1611399168 | bytes 11534336 | tf_op jit(solution)/shard_map/dot_general | solution.py:188
  336.1 6.5 %shard_map.87 = f32[128,3072]{1,0:T(8,128)} custom-call(f32[256,3072]{1,0:T(8,128)} %fusion.x_ref), custom_call_target="tpu_custom_call" | custom-call | tf_op jit(solution)/shard_map/pallas_call | solution.py:150
  347.7 27.9 %shard_map.88 = bf16[32,96,128]{2,1,0:T(8,128)(2,1)} custom-call(bf16[32,96,128]{2,1,0:T(8,128)(2,1)} %reshape.199.x_ref), custom_call_target="tpu_custom_call" | custom-call | tf_op jit(solution)/shard_map/pallas_call | solution.py:87
  (75 shorter events, 42.0 us)
Async XLA Ops:
  0.0 47.0 %copy-start = (bf16[1,512,3072]{2,1,0:T(8,128)(2,1)S(1)}, bf16[1,512,3072]{2,1,0:T(8,128)(2,1)}, u32[]{:S(2)}) copy-start(bf16[1,512,3072]{2,1,0:T(8,128)(2,1)} %param.11) | copy-start | bytes 9437188
  93.3 0.9 copy-start.3
  93.3 0.9 copy-start.1
  93.3 5.4 %copy-start.2 = (f32[1,3072]{1,0:T(1,128)S(1)}, f32[1,3072]{1,0:T(1,128)}, u32[]{:S(2)}) copy-start(f32[1,3072]{1,0:T(1,128)} %param.8) | copy-start | bytes 36868
  94.4 4.2 %collective-permute-start = (bf16[3,2,3072]{2,1,0:T(2,128)(2,1)S(1)}, bf16[3,2,3072]{2,1,0:T(2,128)(2,1)S(1)}, u32[]{:S(2)}, u32[]{:S(2)}) collective-permute-start(bf16[3,2,3072]{2,1,0:T(2,128)(2,1)S(1)} %fusion.87), channel_id=1, source_target_pairs={{0,64},{64,128},{128,192},{1,65},{65,129},{129,193},{2,66},{66,130... | collective-permute-start | bytes 110600 | tf_op jit(solution)/shard_map/ppermute | solution.py:17
  187.5 4.7 %collective-permute-start.1 = (bf16[3,2,3072]{2,1,0:T(2,128)(2,1)S(1)}, bf16[3,2,3072]{2,1,0:T(2,128)(2,1)S(1)}, u32[]{:S(2)}, u32[]{:S(2)}) collective-permute-start(bf16[3,2,3072]{2,1,0:T(2,128)(2,1)S(1)} %fusion.91), channel_id=1, source_target_pairs={{0,64},{64,128},{128,192},{1,65},{65,129},{129,193},{2,66},{66,130... | collective-permute-start | bytes 110600 | tf_op jit(solution)/shard_map/ppermute | solution.py:17
  280.5 5.0 %collective-permute-start.2 = (bf16[3,2,3072]{2,1,0:T(2,128)(2,1)}, bf16[3,2,3072]{2,1,0:T(2,128)(2,1)S(1)}, u32[]{:S(2)}, u32[]{:S(2)}) collective-permute-start(bf16[3,2,3072]{2,1,0:T(2,128)(2,1)} %fusion.95), channel_id=1, source_target_pairs={{0,64},{64,128},{128,192},{1,65},{65,129},{129,193},{2,66},{66,130... | collective-permute-start | bytes 110600 | tf_op jit(solution)/shard_map/ppermute | solution.py:17

commit v5 on v4

--- a/solution.py
+++ b/solution.py
@@ -43,7 +43,9 @@
         return peer_y * ring_z + peer_z
 
     def source(dest_chip):
-        return x_ref.at[dest_chip // per_expert] if per_expert else x_ref.at[dest_chip]
+        if per_expert:
+            return x_ref.at[dest_chip // per_expert]
+        return x_ref.at[lax.rem(dest_chip, ring_z) * ring_y + dest_chip // ring_z]
 
     def copy_of(dest_chip, slot):
         return pltpu.make_async_remote_copy(
@@ -90,6 +92,104 @@
         in_specs=[pl.BlockSpec(memory_space=pltpu.VMEM)],
         out_specs=pl.BlockSpec(memory_space=pltpu.VMEM),
         scratch_shapes=[pltpu.SemaphoreType.DMA((chips,)), pltpu.SemaphoreType.DMA((chips,))],
+        compiler_params=pltpu.CompilerParams(collective_id=collective, has_side_effects=True),
+    )(pieces)
+
+
+def ring_gather_kernel(ring_y, ring_z, x_ref, o_ref, send_y, recv_y, send_up, send_down, recv_z, send_c, recv_c):
+    me = lax.axis_index("shard")
+    segment = lax.axis_index("segment")
+    core = lax.rem(me, 2)
+    chip = me // 2
+    y, z = chip // ring_z, lax.rem(chip, ring_z)
+    half_z = ring_z // 2
+
+    def device(peer_y, peer_z):
+        return (segment, (peer_y * ring_z + peer_z) * 2 + core)
+
+    up_z, down_z = lax.rem(z + 1, ring_z), lax.rem(z + ring_z - 1, ring_z)
+    partner = (segment, me + 1 - 2 * core)
+    barrier = pltpu.get_barrier_semaphore()
+    for step in range(1, ring_y):
+        pl.semaphore_signal(barrier, 1, device_id=device(lax.rem(y + step, ring_y), z), device_id_type=pl.DeviceIdType.MESH)
+    pl.semaphore_signal(barrier, 1, device_id=device(y, up_z), device_id_type=pl.DeviceIdType.MESH)
+    pl.semaphore_signal(barrier, 1, device_id=device(y, down_z), device_id_type=pl.DeviceIdType.MESH)
+    pl.semaphore_signal(barrier, 1, device_id=partner, device_id_type=pl.DeviceIdType.MESH)
+    pl.semaphore_wait(barrier, ring_y + 2)
+
+    def y_copy(peer_y, slot):
+        return pltpu.make_async_remote_copy(
+            src_ref=x_ref.at[peer_y * 2 // ring_y],
+            dst_ref=o_ref.at[0, z, slot],
+            send_sem=send_y.at[peer_y],
+            recv_sem=recv_y.at[slot],
+            device_id=device(peer_y, z),
+            device_id_type=pl.DeviceIdType.MESH,
+        )
+
+    for step in range(1, ring_y):
+        y_copy(lax.rem(y + step, ring_y), y).start()
+    o_ref[0, z, y] = x_ref[y * 2 // ring_y]
+    for step in range(1, ring_y):
+        origin = lax.rem(y + ring_y - step, ring_y)
+        y_copy(origin, origin).wait_recv()
+        y_copy(lax.rem(y + step, ring_y), y).wait_send()
+
+    def z_copy(slot, peer_z, sems, index):
+        return pltpu.make_async_remote_copy(
+            src_ref=o_ref.at[0, slot],
+            dst_ref=o_ref.at[0, slot],
+            send_sem=sems.at[index],
+            recv_sem=recv_z.at[slot],
+            device_id=device(y, peer_z),
+            device_id_type=pl.DeviceIdType.MESH,
+        )
+
+    for step in range(half_z):
+        up_slot = lax.rem(z + ring_z - step, ring_z)
+        if step > 0:
+            z_copy(up_slot, down_z, send_up, step).wait_recv()
+        z_copy(up_slot, up_z, send_up, step).start()
+        if step < half_z - 1:
+            down_slot = lax.rem(z + step, ring_z)
+            if step > 0:
+                z_copy(down_slot, up_z, send_down, step).wait_recv()
+            z_copy(down_slot, down_z, send_down, step).start()
+    z_copy(lax.rem(z + ring_z - half_z, ring_z), down_z, send_up, 0).wait_recv()
+    z_copy(lax.rem(z + half_z - 1, ring_z), up_z, send_down, 0).wait_recv()
+    for step in range(half_z):
+        z_copy(lax.rem(z + ring_z - step, ring_z), up_z, send_up, step).wait_send()
+        if step < half_z - 1:
+            z_copy(lax.rem(z + step, ring_z), down_z, send_down, step).wait_send()
+
+    pair = pltpu.make_async_remote_copy(
+        src_ref=o_ref.at[0],
+        dst_ref=o_ref.at[1],
+        send_sem=send_c,
+        recv_sem=recv_c,
+        device_id=partner,
+        device_id_type=pl.DeviceIdType.MESH,
+    )
+    pair.start()
+    pair.wait()
+
+
+def ring_gather(pieces, ring_y, ring_z, collective):
+    rows, lanes = pieces.shape[1], pieces.shape[2]
+    return pl.pallas_call(
+        functools.partial(ring_gather_kernel, ring_y, ring_z),
+        out_shape=jax.ShapeDtypeStruct((2, ring_z, ring_y, rows, lanes), pieces.dtype),
+        in_specs=[pl.BlockSpec(memory_space=pltpu.VMEM)],
+        out_specs=pl.BlockSpec(memory_space=pltpu.VMEM),
+        scratch_shapes=[
+            pltpu.SemaphoreType.DMA((ring_y,)),
+            pltpu.SemaphoreType.DMA((ring_y,)),
+            pltpu.SemaphoreType.DMA((ring_z // 2,)),
+            pltpu.SemaphoreType.DMA((ring_z // 2,)),
+            pltpu.SemaphoreType.DMA((ring_z,)),
+            pltpu.SemaphoreType.DMA(()),
+            pltpu.SemaphoreType.DMA(()),
+        ],
         compiler_params=pltpu.CompilerParams(collective_id=collective, has_side_effects=True),
     )(pieces)
 
@@ -180,8 +280,7 @@
     for tick in range(segment_count):
         normed = normalize(carried, row_gain)
         pieces = jnp.stack([normed[0:2], normed[1:3]]).reshape(2, piece_rows, LANES)
-        own_core = chip_exchange(pieces, ring_y, ring_z, per_expert // 2, 0)
-        block_rows = pair_gather(own_core, 1).reshape(shard_count * 2 * local_rows, width)
+        block_rows = ring_gather(pieces, ring_y, ring_z, 0).reshape(shard_count * 2 * local_rows, width)
         gate_val = jnp.dot(block_rows, gate_part, preferred_element_type=jnp.float32)
         up_val = jnp.dot(block_rows, up_part, preferred_element_type=jnp.float32)
         hidden = (jax.nn.silu(gate_val) * up_val).astype(jnp.bfloat16)

time: 384 us -> 366 us (0.953)
  Pallas kernels: 270 us -> 249 us
    pallas_call x8 -> x4, Pallas kernels: 217 us -> 103 us  [chip_exchange(): pl.pallas_call(functools.partial(chip_exchange_kernel, ring_y, ring_z, pe...]
    pallas_call x4, Pallas kernels: 27.6 us -> 121 us  [ring_gather(): pl.pallas_call(functools.partial(ring_gather_kernel, ring_y, ring_z), out...]
where the time goes in v5:
time: 366 us; the launch traced here: 362 us
  Pallas kernels  249 us (68%)
  matrix products  40.7 us (11%)
  local copies, waits for them, and re-layouts  30 us (8%)
  other arithmetic  26.5 us (7%)
  starting transfers between devices  11.3 us (3%)
    pallas_call x4, Pallas kernels, ring_gather(): pl.pallas_call(functools.partial(ring_gather_kernel, ring_y, ring_z), out...  121 us
    pallas_call x4, Pallas kernels, chip_exchange(): pl.pallas_call(functools.partial(chip_exchange_kernel, ring_y, ring_z, pe...  103 us
    pallas_call x4, Pallas kernels, pair_send(): pl.pallas_call(pair_send_kernel, out_shape=jax.ShapeDtypeStruct((value.sh...  25.8 us
    dot_general x4, matrix products, shards(): partial_sum = jnp.dot(hidden, down_part, preferred_element_type=jnp.float32)  24.1 us
    dot_general x4, matrix products, shards(): jnp.dot(block_rows, gate_part, preferred_element_type=jnp.float32)  16.6 us
    reshape x4, local copies, waits for them, and re-layouts, shards(): ring_gather(pieces, ring_y, ring_z, 0)  14.8 us
    convert_element_type x4, other arithmetic, shards(): (partial_sum[:half] + pair_send(partial_sum, 2)).astype(jnp.bfloat16)  11.8 us
    ppermute x3, starting transfers between devices, shifted(): lax.ppermute(value, axis, [(source, source + steps) for source in range(i...  11.3 us
  transfers between devices with their start and end apart: 3, of which 3 were waited for; matrix products, arithmetic and copies ran while one was open for 0% of the time, Pallas kernels for 0%

profile of v5, /device:TPU:1, one launch (start us, length us, event | category | flops | bytes accessed | tf_op | source)
XLA Modules:
  0.0 362.1 jit_solution(7852492111480281372)
XLA Ops:
  2.7 32.4 %shard_map.73 = bf16[2,8,4,96,128]{4,3,2,1,0:T(8,128)(2,1)} custom-call(bf16[2,96,128]{2,1,0:T(8,128)(2,1)} %pad_maximum_fusion.x_ref), custom_call_target="tpu_custom_call" | custom-call | tf_op jit(solution)/shard_map/pallas_call | solution.py:179
  35.0 3.7 %reshape.192 = bf16[256,3072]{1,0:T(8,128)(2,1)} reshape(bf16[2,8,4,96,128]{4,3,2,1,0:T(8,128)(2,1)} %shard_map.73) | data formatting | bytes 3145728 | tf_op jit(solution)/shard_map/reshape | solution.py:283
  38.8 4.2 %fusion.22 = f32[256,512]{1,0:T(8,128)} fusion(bf16[256,3072]{1,0:T(8,128)(2,1)} %reshape.192, bf16[1,3072,512]{2,1,0:T(8,128)(2,1)} %param.9), kind=kOutput, calls=%fused_computation.22 | convolution fusion | flops 805306368 | bytes 5242880 | tf_op jit(solution)/shard_map/dot_general | solution.py:284
  42.9 6.0 %fusion.6.x_ref = f32[256,3072]{1,0:T(8,128)} fusion(bf16[1,512,3072]{2,1,0:T(8,128)(2,1)S(1)} %copy-done, bf16[256,3072]{1,0:T(8,128)(2,1)} %reshape.192, bf16[1,3072,512]{2,1,0:T(8,128)(2,1)} %param.10, f32[256,512]{1,0:T(8,128)} %fusion.22), kind=kOutput, calls=%fused_computation.6 | convolution fusion | flops 1611399168 | bytes 11534336 | tf_op jit(solution)/shard_map/dot_general | solution.py:287
  48.9 6.5 %shard_map.74 = f32[128,3072]{1,0:T(8,128)} custom-call(f32[256,3072]{1,0:T(8,128)} %fusion.6.x_ref), custom_call_target="tpu_custom_call" | custom-call | tf_op jit(solution)/shard_map/pallas_call | solution.py:250
  55.4 2.9 fusion.27
  58.3 2.2 reshape.193.x_ref
  60.5 26.9 %shard_map.75 = bf16[32,96,128]{2,1,0:T(8,128)(2,1)} custom-call(bf16[32,96,128]{2,1,0:T(8,128)(2,1)} %reshape.193.x_ref), custom_call_target="tpu_custom_call" | custom-call | tf_op jit(solution)/shard_map/pallas_call | solution.py:89
  89.8 3.1 collective-permute-start
  95.0 28.5 %shard_map.76 = bf16[2,8,4,96,128]{4,3,2,1,0:T(8,128)(2,1)} custom-call(bf16[2,96,128]{2,1,0:T(8,128)(2,1)} %pad_maximum_fusion.1.x_ref), custom_call_target="tpu_custom_call" | custom-call | tf_op jit(solution)/shard_map/pallas_call | solution.py:179
  123.5 3.7 %reshape.194 = bf16[256,3072]{1,0:T(8,128)(2,1)} reshape(bf16[2,8,4,96,128]{4,3,2,1,0:T(8,128)(2,1)} %shard_map.76) | data formatting | bytes 3145728 | tf_op jit(solution)/shard_map/reshape | solution.py:283
  127.2 4.2 %fusion.20 = f32[256,512]{1,0:T(8,128)} fusion(bf16[256,3072]{1,0:T(8,128)(2,1)} %reshape.194, bf16[1,3072,512]{2,1,0:T(8,128)(2,1)} %param.9), kind=kOutput, calls=%fused_computation.20 | convolution fusion | flops 805306368 | bytes 5242880 | tf_op jit(solution)/shard_map/dot_general | solution.py:284
  131.4 6.0 %fusion.4.x_ref = f32[256,3072]{1,0:T(8,128)} fusion(bf16[1,512,3072]{2,1,0:T(8,128)(2,1)S(1)} %copy-done, bf16[256,3072]{1,0:T(8,128)(2,1)} %reshape.194, bf16[1,3072,512]{2,1,0:T(8,128)(2,1)} %param.10, f32[256,512]{1,0:T(8,128)} %fusion.20), kind=kOutput, calls=%fused_computation.4 | convolution fusion | flops 1611399168 | bytes 11534336 | tf_op jit(solution)/shard_map/dot_general | solution.py:287
  137.4 6.5 %shard_map.77 = f32[128,3072]{1,0:T(8,128)} custom-call(f32[256,3072]{1,0:T(8,128)} %fusion.4.x_ref), custom_call_target="tpu_custom_call" | custom-call | tf_op jit(solution)/shard_map/pallas_call | solution.py:250
  143.9 2.9 fusion.26
  149.0 24.8 %shard_map.78 = bf16[32,96,128]{2,1,0:T(8,128)(2,1)} custom-call(bf16[32,96,128]{2,1,0:T(8,128)(2,1)} %reshape.195.x_ref), custom_call_target="tpu_custom_call" | custom-call | tf_op jit(solution)/shard_map/pallas_call | solution.py:89
  175.4 4.2 %collective-permute-start.1 = (bf16[3,2,3072]{2,1,0:T(2,128)(2,1)S(1)}, bf16[3,2,3072]{2,1,0:T(2,128)(2,1)S(1)}, u32[]{:S(2)}, u32[]{:S(2)}) collective-permute-start(bf16[3,2,3072]{2,1,0:T(2,128)(2,1)S(1)} %fusion.91), channel_id=1, source_target_pairs={{0,64},{64,128},{128,192},{1,65},{65,129},{129,193},{2,66},{66,130... | collective-permute-start | bytes 110600 | tf_op jit(solution)/shard_map/ppermute | solution.py:17
  181.5 29.9 %shard_map.79 = bf16[2,8,4,96,128]{4,3,2,1,0:T(8,128)(2,1)} custom-call(bf16[2,96,128]{2,1,0:T(8,128)(2,1)} %pad_maximum_fusion.2.x_ref), custom_call_target="tpu_custom_call" | custom-call | tf_op jit(solution)/shard_map/pallas_call | solution.py:179
  211.4 3.7 %reshape.196 = bf16[256,3072]{1,0:T(8,128)(2,1)} reshape(bf16[2,8,4,96,128]{4,3,2,1,0:T(8,128)(2,1)} %shard_map.79) | data formatting | bytes 3145728 | tf_op jit(solution)/shard_map/reshape | solution.py:283
  215.1 4.2 %fusion.18 = f32[256,512]{1,0:T(8,128)} fusion(bf16[256,3072]{1,0:T(8,128)(2,1)} %reshape.196, bf16[1,3072,512]{2,1,0:T(8,128)(2,1)} %param.9), kind=kOutput, calls=%fused_computation.18 | convolution fusion | flops 805306368 | bytes 5242880 | tf_op jit(solution)/shard_map/dot_general | solution.py:284
  219.3 6.0 %fusion.2.x_ref = f32[256,3072]{1,0:T(8,128)} fusion(bf16[1,512,3072]{2,1,0:T(8,128)(2,1)S(1)} %copy-done, bf16[256,3072]{1,0:T(8,128)(2,1)} %reshape.196, bf16[1,3072,512]{2,1,0:T(8,128)(2,1)} %param.10, f32[256,512]{1,0:T(8,128)} %fusion.18), kind=kOutput, calls=%fused_computation.2 | convolution fusion | flops 1611399168 | bytes 11534336 | tf_op jit(solution)/shard_map/dot_general | solution.py:287
  225.3 6.5 %shard_map.80 = f32[128,3072]{1,0:T(8,128)} custom-call(f32[256,3072]{1,0:T(8,128)} %fusion.2.x_ref), custom_call_target="tpu_custom_call" | custom-call | tf_op jit(solution)/shard_map/pallas_call | solution.py:250
  231.7 2.9 fusion.25
  236.8 25.4 %shard_map.81 = bf16[32,96,128]{2,1,0:T(8,128)(2,1)} custom-call(bf16[32,96,128]{2,1,0:T(8,128)(2,1)} %reshape.197.x_ref), custom_call_target="tpu_custom_call" | custom-call | tf_op jit(solution)/shard_map/pallas_call | solution.py:89
  264.5 4.0 %collective-permute-start.2 = (bf16[3,2,3072]{2,1,0:T(2,128)(2,1)}, bf16[3,2,3072]{2,1,0:T(2,128)(2,1)S(1)}, u32[]{:S(2)}, u32[]{:S(2)}) collective-permute-start(bf16[3,2,3072]{2,1,0:T(2,128)(2,1)} %fusion.95), channel_id=1, source_target_pairs={{0,64},{64,128},{128,192},{1,65},{65,129},{129,193},{2,66},{66,130... | collective-permute-start | bytes 110600 | tf_op jit(solution)/shard_map/ppermute | solution.py:17
  274.1 30.1 %shard_map.82 = bf16[2,8,4,96,128]{4,3,2,1,0:T(8,128)(2,1)} custom-call(bf16[2,96,128]{2,1,0:T(8,128)(2,1)} %pad_maximum_fusion.3.x_ref), custom_call_target="tpu_custom_call" | custom-call | tf_op jit(solution)/shard_map/pallas_call | solution.py:179
  304.2 3.7 %reshape.198 = bf16[256,3072]{1,0:T(8,128)(2,1)} reshape(bf16[2,8,4,96,128]{4,3,2,1,0:T(8,128)(2,1)} %shard_map.82) | data formatting | bytes 3145728 | tf_op jit(solution)/shard_map/reshape | solution.py:283
  308.0 4.2 %fusion.16 = f32[256,512]{1,0:T(8,128)} fusion(bf16[256,3072]{1,0:T(8,128)(2,1)} %reshape.198, bf16[1,3072,512]{2,1,0:T(8,128)(2,1)} %param.9), kind=kOutput, calls=%fused_computation.16 | convolution fusion | flops 805306368 | bytes 5242880 | tf_op jit(solution)/shard_map/dot_general | solution.py:284
  312.1 6.0 %fusion.x_ref = f32[256,3072]{1,0:T(8,128)} fusion(bf16[1,512,3072]{2,1,0:T(8,128)(2,1)S(1)} %copy-done, bf16[256,3072]{1,0:T(8,128)(2,1)} %reshape.198, bf16[1,3072,512]{2,1,0:T(8,128)(2,1)} %param.10, f32[256,512]{1,0:T(8,128)} %fusion.16), kind=kOutput, calls=%fused_computation | convolution fusion | flops 1611399168 | bytes 11534336 | tf_op jit(solution)/shard_map/dot_general | solution.py:287
  318.1 6.5 %shard_map.83 = f32[128,3072]{1,0:T(8,128)} custom-call(f32[256,3072]{1,0:T(8,128)} %fusion.x_ref), custom_call_target="tpu_custom_call" | custom-call | tf_op jit(solution)/shard_map/pallas_call | solution.py:250
  324.6 2.9 fusion.24
  329.7 25.4 %shard_map.84 = bf16[32,96,128]{2,1,0:T(8,128)(2,1)} custom-call(bf16[32,96,128]{2,1,0:T(8,128)(2,1)} %reshape.199.x_ref), custom_call_target="tpu_custom_call" | custom-call | tf_op jit(solution)/shard_map/pallas_call | solution.py:89
  (71 shorter events, 30.9 us)
Async XLA Ops:
  0.0 42.9 %copy-start = (bf16[1,512,3072]{2,1,0:T(8,128)(2,1)S(1)}, bf16[1,512,3072]{2,1,0:T(8,128)(2,1)}, u32[]{:S(2)}) copy-start(bf16[1,512,3072]{2,1,0:T(8,128)(2,1)} %param.11) | copy-start | bytes 9437188
  88.8 0.9 copy-start.3
  88.8 0.9 copy-start.1
  88.8 5.4 %copy-start.2 = (f32[1,3072]{1,0:T(1,128)S(1)}, f32[1,3072]{1,0:T(1,128)}, u32[]{:S(2)}) copy-start(f32[1,3072]{1,0:T(1,128)} %param.8) | copy-start | bytes 36868
  89.8 4.2 %collective-permute-start = (bf16[3,2,3072]{2,1,0:T(2,128)(2,1)S(1)}, bf16[3,2,3072]{2,1,0:T(2,128)(2,1)S(1)}, u32[]{:S(2)}, u32[]{:S(2)}) collective-permute-start(bf16[3,2,3072]{2,1,0:T(2,128)(2,1)S(1)} %fusion.87), channel_id=1, source_target_pairs={{0,64},{64,128},{128,192},{1,65},{65,129},{129,193},{2,66},{66,130... | collective-permute-start | bytes 110600 | tf_op jit(solution)/shard_map/ppermute | solution.py:17
  175.4 5.1 %collective-permute-start.1 = (bf16[3,2,3072]{2,1,0:T(2,128)(2,1)S(1)}, bf16[3,2,3072]{2,1,0:T(2,128)(2,1)S(1)}, u32[]{:S(2)}, u32[]{:S(2)}) collective-permute-start(bf16[3,2,3072]{2,1,0:T(2,128)(2,1)S(1)} %fusion.91), channel_id=1, source_target_pairs={{0,64},{64,128},{128,192},{1,65},{65,129},{129,193},{2,66},{66,130... | collective-permute-start | bytes 110600 | tf_op jit(solution)/shard_map/ppermute | solution.py:17
  264.5 5.4 %collective-permute-start.2 = (bf16[3,2,3072]{2,1,0:T(2,128)(2,1)}, bf16[3,2,3072]{2,1,0:T(2,128)(2,1)S(1)}, u32[]{:S(2)}, u32[]{:S(2)}) collective-permute-start(bf16[3,2,3072]{2,1,0:T(2,128)(2,1)} %fusion.95), channel_id=1, source_target_pairs={{0,64},{64,128},{128,192},{1,65},{65,129},{129,193},{2,66},{66,130... | collective-permute-start | bytes 110600 | tf_op jit(solution)/shard_map/ppermute | solution.py:17

commit v6 on v5

--- a/solution.py
+++ b/solution.py
@@ -192,6 +192,41 @@
         ],
         compiler_params=pltpu.CompilerParams(collective_id=collective, has_side_effects=True),
     )(pieces)
+
+
+def expert_kernel(x_ref, gate_ref, up_ref, down_ref, o_ref):
+    @pl.when(pl.program_id(0) == 0)
+    def _():
+        o_ref[...] = jnp.zeros_like(o_ref)
+
+    rows = x_ref[...]
+    gate_val = jnp.dot(rows, gate_ref[...], preferred_element_type=jnp.float32)
+    up_val = jnp.dot(rows, up_ref[...], preferred_element_type=jnp.float32)
+    hidden = (gate_val / (1.0 + jnp.exp(-gate_val)) * up_val).astype(jnp.bfloat16)
+    o_ref[...] += jnp.dot(hidden, down_ref[...], preferred_element_type=jnp.float32)
+
+
+def expert(rows, gate_part, up_part, down_part, chunk=128):
+    count, width = rows.shape
+    hidden = gate_part.shape[1]
+    return pl.pallas_call(
+        expert_kernel,
+        out_shape=jax.ShapeDtypeStruct((count, width), jnp.float32),
+        grid=(hidden // chunk,),
+        in_specs=[
+            pl.BlockSpec((count, width), lambda k: (0, 0)),
+            pl.BlockSpec((width, chunk), lambda k: (0, k)),
+            pl.BlockSpec((width, chunk), lambda k: (0, k)),
+            pl.BlockSpec((chunk, width), lambda k: (k, 0)),
+        ],
+        out_specs=pl.BlockSpec((count, width), lambda k: (0, 0)),
+        compiler_params=pltpu.CompilerParams(dimension_semantics=("arbitrary",)),
+        cost_estimate=pl.CostEstimate(
+            flops=6 * count * width * hidden,
+            transcendentals=count * hidden,
+            bytes_accessed=2 * (count * width + 3 * width * hidden) + 4 * count * width,
+        ),
+    )(rows, gate_part, up_part, down_part)
 
 
 def pair_barrier():
@@ -281,10 +316,7 @@
         normed = normalize(carried, row_gain)
         pieces = jnp.stack([normed[0:2], normed[1:3]]).reshape(2, piece_rows, LANES)
         block_rows = ring_gather(pieces, ring_y, ring_z, 0).reshape(shard_count * 2 * local_rows, width)
-        gate_val = jnp.dot(block_rows, gate_part, preferred_element_type=jnp.float32)
-        up_val = jnp.dot(block_rows, up_part, preferred_element_type=jnp.float32)
-        hidden = (jax.nn.silu(gate_val) * up_val).astype(jnp.bfloat16)
-        partial_sum = jnp.dot(hidden, down_part, preferred_element_type=jnp.float32)
+        partial_sum = expert(block_rows, gate_part, up_part, down_part)
         half = partial_sum.shape[0] // 2
         chip_sum = (partial_sum[:half] + pair_send(partial_sum, 2)).astype(jnp.bfloat16)
         received = chip_exchange(chip_sum.reshape(chips, piece_rows, LANES), ring_y, ring_z, 0, 3)

time: 366 us -> 356 us (0.973)
  Pallas kernels: 249 us -> 291 us
  matrix products: 40.7 us -> 0 us
  local copies, waits for them, and re-layouts: 30 us -> 24.3 us
  other arithmetic: 26.5 us -> 21.6 us
    pallas_call x0 -> x4, Pallas kernels: none -> 41.5 us  [expert(): pl.pallas_call(expert_kernel, out_shape=jax.ShapeDtypeStruct((count, widt...]
    dot_general x8 -> x0, matrix products: 40.7 us -> none  [the longest x4 24.1 us: shards(): partial_sum = jnp.dot(hidden, down_part, preferred_element_type=jnp.float32)]
where the time goes in v6:
time: 356 us; the launch traced here: 353 us
  Pallas kernels  291 us (82%)
  local copies, waits for them, and re-layouts  24.3 us (7%)
  other arithmetic  21.6 us (6%)
  starting transfers between devices  11.5 us (3%)
    pallas_call x4, Pallas kernels, ring_gather(): pl.pallas_call(functools.partial(ring_gather_kernel, ring_y, ring_z), out...  121 us
    pallas_call x4, Pallas kernels, chip_exchange(): pl.pallas_call(functools.partial(chip_exchange_kernel, ring_y, ring_z, pe...  103 us
    pallas_call x4, Pallas kernels, expert(): pl.pallas_call(expert_kernel, out_shape=jax.ShapeDtypeStruct((count, widt...  41.5 us
    pallas_call x4, Pallas kernels, pair_send(): pl.pallas_call(pair_send_kernel, out_shape=jax.ShapeDtypeStruct((value.sh...  26.4 us
    reshape x4, local copies, waits for them, and re-layouts, shards(): ring_gather(pieces, ring_y, ring_z, 0)  14.8 us
    ppermute x3, starting transfers between devices, shifted(): lax.ppermute(value, axis, [(source, source + steps) for source in range(i...  11.5 us
    convert_element_type x4, other arithmetic, shards(): (partial_sum[:half] + pair_send(partial_sum, 2)).astype(jnp.bfloat16)  9.75 us
    reshape x4, local copies, waits for them, and re-layouts, shards(): chip_sum.reshape(chips, piece_rows, LANES)  8.83 us
  transfers between devices with their start and end apart: 3, of which 3 were waited for; matrix products, arithmetic and copies ran while one was open for 0% of the time, Pallas kernels for 0%

profile of v6, /device:TPU:1, one launch (start us, length us, event | category | flops | bytes accessed | tf_op | source)
XLA Modules:
  0.0 352.8 jit_solution(6726922520255055204)
XLA Ops:
  2.5 32.4 %shard_map.73 = bf16[2,8,4,96,128]{4,3,2,1,0:T(8,128)(2,1)} custom-call(bf16[2,96,128]{2,1,0:T(8,128)(2,1)} %pad_maximum_fusion.x_ref), custom_call_target="tpu_custom_call" | custom-call | tf_op jit(solution)/shard_map/pallas_call | solution.py:179
  34.9 3.7 %reshape.192.x_ref = bf16[256,3072]{1,0:T(8,128)(2,1)} reshape(bf16[2,8,4,96,128]{4,3,2,1,0:T(8,128)(2,1)} %shard_map.73) | data formatting | bytes 3145728 | tf_op jit(solution)/shard_map/reshape | solution.py:318
  38.6 10.4 %shard_map.74.x_ref = f32[256,3072]{1,0:T(8,128)} custom-call(bf16[256,3072]{1,0:T(8,128)(2,1)} %reshape.192.x_ref, bf16[3072,512]{1,0:T(8,128)(2,1)} %bitcast.16, bf16[3072,512]{1,0:T(8,128)(2,1)} %bitcast.20, bf16[512,3072]{1,0:T(8,128)(2,1)} %bitcast.24), custom_call_target="tpu_custom_call" | custom-call | flops 2415919104 | bytes 14155776 | tf_op jit(solution)/shard_map/pallas_call | solution.py:212
  49.0 6.6 %shard_map.75 = f32[128,3072]{1,0:T(8,128)} custom-call(f32[256,3072]{1,0:T(8,128)} %shard_map.74.x_ref), custom_call_target="tpu_custom_call" | custom-call | tf_op jit(solution)/shard_map/pallas_call | solution.py:285
  55.6 2.4 fusion.3
  58.0 2.2 reshape.193.x_ref
  60.3 26.9 %shard_map.76 = bf16[32,96,128]{2,1,0:T(8,128)(2,1)} custom-call(bf16[32,96,128]{2,1,0:T(8,128)(2,1)} %reshape.193.x_ref), custom_call_target="tpu_custom_call" | custom-call | tf_op jit(solution)/shard_map/pallas_call | solution.py:89
  87.2 1.3 convert_element_type.67
  89.6 3.1 collective-permute-start
  94.7 28.6 %shard_map.77 = bf16[2,8,4,96,128]{4,3,2,1,0:T(8,128)(2,1)} custom-call(bf16[2,96,128]{2,1,0:T(8,128)(2,1)} %pad_maximum_fusion.1.x_ref), custom_call_target="tpu_custom_call" | custom-call | tf_op jit(solution)/shard_map/pallas_call | solution.py:179
  123.3 3.7 %reshape.194.x_ref = bf16[256,3072]{1,0:T(8,128)(2,1)} reshape(bf16[2,8,4,96,128]{4,3,2,1,0:T(8,128)(2,1)} %shard_map.77) | data formatting | bytes 3145728 | tf_op jit(solution)/shard_map/reshape | solution.py:318
  127.0 10.4 %shard_map.78.x_ref = f32[256,3072]{1,0:T(8,128)} custom-call(bf16[256,3072]{1,0:T(8,128)(2,1)} %reshape.194.x_ref, bf16[3072,512]{1,0:T(8,128)(2,1)} %bitcast.17, bf16[3072,512]{1,0:T(8,128)(2,1)} %bitcast.21, bf16[512,3072]{1,0:T(8,128)(2,1)} %bitcast.25), custom_call_target="tpu_custom_call" | custom-call | flops 2415919104 | bytes 14155776 | tf_op jit(solution)/shard_map/pallas_call | solution.py:212
  137.4 6.6 %shard_map.79 = f32[128,3072]{1,0:T(8,128)} custom-call(f32[256,3072]{1,0:T(8,128)} %shard_map.78.x_ref), custom_call_target="tpu_custom_call" | custom-call | tf_op jit(solution)/shard_map/pallas_call | solution.py:285
  144.0 2.4 fusion.2
  146.4 2.2 reshape.195.x_ref
  148.6 24.7 %shard_map.80 = bf16[32,96,128]{2,1,0:T(8,128)(2,1)} custom-call(bf16[32,96,128]{2,1,0:T(8,128)(2,1)} %reshape.195.x_ref), custom_call_target="tpu_custom_call" | custom-call | tf_op jit(solution)/shard_map/pallas_call | solution.py:89
  174.9 4.3 %collective-permute-start.1 = (bf16[3,2,3072]{2,1,0:T(2,128)(2,1)S(1)}, bf16[3,2,3072]{2,1,0:T(2,128)(2,1)S(1)}, u32[]{:S(2)}, u32[]{:S(2)}) collective-permute-start(bf16[3,2,3072]{2,1,0:T(2,128)(2,1)S(1)} %fusion.11), channel_id=1, source_target_pairs={{0,64},{64,128},{128,192},{1,65},{65,129},{129,193},{2,66},{66,130... | collective-permute-start | bytes 110600 | tf_op jit(solution)/shard_map/ppermute | solution.py:17
  181.1 29.9 %shard_map.81 = bf16[2,8,4,96,128]{4,3,2,1,0:T(8,128)(2,1)} custom-call(bf16[2,96,128]{2,1,0:T(8,128)(2,1)} %pad_maximum_fusion.2.x_ref), custom_call_target="tpu_custom_call" | custom-call | tf_op jit(solution)/shard_map/pallas_call | solution.py:179
  211.0 3.7 %reshape.196.x_ref = bf16[256,3072]{1,0:T(8,128)(2,1)} reshape(bf16[2,8,4,96,128]{4,3,2,1,0:T(8,128)(2,1)} %shard_map.81) | data formatting | bytes 3145728 | tf_op jit(solution)/shard_map/reshape | solution.py:318
  214.7 10.4 %shard_map.82.x_ref = f32[256,3072]{1,0:T(8,128)} custom-call(bf16[256,3072]{1,0:T(8,128)(2,1)} %reshape.196.x_ref, bf16[3072,512]{1,0:T(8,128)(2,1)} %bitcast.18, bf16[3072,512]{1,0:T(8,128)(2,1)} %bitcast.22, bf16[512,3072]{1,0:T(8,128)(2,1)} %bitcast.26), custom_call_target="tpu_custom_call" | custom-call | flops 2415919104 | bytes 14155776 | tf_op jit(solution)/shard_map/pallas_call | solution.py:212
  225.1 6.6 %shard_map.83 = f32[128,3072]{1,0:T(8,128)} custom-call(f32[256,3072]{1,0:T(8,128)} %shard_map.82.x_ref), custom_call_target="tpu_custom_call" | custom-call | tf_op jit(solution)/shard_map/pallas_call | solution.py:285
  231.7 2.4 fusion.1
  234.1 2.2 reshape.197.x_ref
  236.3 25.5 %shard_map.84 = bf16[32,96,128]{2,1,0:T(8,128)(2,1)} custom-call(bf16[32,96,128]{2,1,0:T(8,128)(2,1)} %reshape.197.x_ref), custom_call_target="tpu_custom_call" | custom-call | tf_op jit(solution)/shard_map/pallas_call | solution.py:89
  263.5 4.1 %collective-permute-start.2 = (bf16[3,2,3072]{2,1,0:T(2,128)(2,1)S(1)}, bf16[3,2,3072]{2,1,0:T(2,128)(2,1)S(1)}, u32[]{:S(2)}, u32[]{:S(2)}) collective-permute-start(bf16[3,2,3072]{2,1,0:T(2,128)(2,1)S(1)} %fusion.15), channel_id=1, source_target_pairs={{0,64},{64,128},{128,192},{1,65},{65,129},{129,193},{2,66},{66,130... | collective-permute-start | bytes 110600 | tf_op jit(solution)/shard_map/ppermute | solution.py:17
  269.6 29.9 %shard_map.85 = bf16[2,8,4,96,128]{4,3,2,1,0:T(8,128)(2,1)} custom-call(bf16[2,96,128]{2,1,0:T(8,128)(2,1)} %pad_maximum_fusion.3.x_ref), custom_call_target="tpu_custom_call" | custom-call | tf_op jit(solution)/shard_map/pallas_call | solution.py:179
  299.6 3.7 %reshape.198.x_ref = bf16[256,3072]{1,0:T(8,128)(2,1)} reshape(bf16[2,8,4,96,128]{4,3,2,1,0:T(8,128)(2,1)} %shard_map.85) | data formatting | bytes 3145728 | tf_op jit(solution)/shard_map/reshape | solution.py:318
  303.3 10.4 %shard_map.86.x_ref = f32[256,3072]{1,0:T(8,128)} custom-call(bf16[256,3072]{1,0:T(8,128)(2,1)} %reshape.198.x_ref, bf16[3072,512]{1,0:T(8,128)(2,1)} %bitcast.19, bf16[3072,512]{1,0:T(8,128)(2,1)} %bitcast.23, bf16[512,3072]{1,0:T(8,128)(2,1)} %bitcast.27), custom_call_target="tpu_custom_call" | custom-call | flops 2415919104 | bytes 14155776 | tf_op jit(solution)/shard_map/pallas_call | solution.py:212
  313.7 6.6 %shard_map.87 = f32[128,3072]{1,0:T(8,128)} custom-call(f32[256,3072]{1,0:T(8,128)} %shard_map.86.x_ref), custom_call_target="tpu_custom_call" | custom-call | tf_op jit(solution)/shard_map/pallas_call | solution.py:285
  320.3 2.4 fusion
  322.7 2.2 reshape.199.x_ref
  324.9 25.5 %shard_map.88 = bf16[32,96,128]{2,1,0:T(8,128)(2,1)} custom-call(bf16[32,96,128]{2,1,0:T(8,128)(2,1)} %reshape.199.x_ref), custom_call_target="tpu_custom_call" | custom-call | tf_op jit(solution)/shard_map/pallas_call | solution.py:89
  (73 shorter events, 14.1 us)
Async XLA Ops:
  49.0 6.6 %copy-start = (f32[256,3072]{1,0:T(8,128)S(1)}, f32[256,3072]{1,0:T(8,128)}, u32[]{:S(2)}) copy-start(f32[256,3072]{1,0:T(8,128)} %shard_map.74.x_ref) | copy-start | bytes 9437188
  88.5 0.9 copy-start.6
  88.5 0.9 copy-start.4
  88.5 5.4 %copy-start.5 = (f32[1,3072]{1,0:T(1,128)S(1)}, f32[1,3072]{1,0:T(1,128)}, u32[]{:S(2)}) copy-start(f32[1,3072]{1,0:T(1,128)} %param.8) | copy-start | bytes 36868
  89.6 4.2 %collective-permute-start = (bf16[3,2,3072]{2,1,0:T(2,128)(2,1)S(1)}, bf16[3,2,3072]{2,1,0:T(2,128)(2,1)S(1)}, u32[]{:S(2)}, u32[]{:S(2)}) collective-permute-start(bf16[3,2,3072]{2,1,0:T(2,128)(2,1)S(1)} %fusion.7), channel_id=1, source_target_pairs={{0,64},{64,128},{128,192},{1,65},{65,129},{129,193},{2,66},{66,130... | collective-permute-start | bytes 110600 | tf_op jit(solution)/shard_map/ppermute | solution.py:17
  137.3 6.6 %copy-start.1 = (f32[256,3072]{1,0:T(8,128)S(1)}, f32[256,3072]{1,0:T(8,128)}, u32[]{:S(2)}) copy-start(f32[256,3072]{1,0:T(8,128)} %shard_map.78.x_ref) | copy-start | bytes 9437188
  174.9 5.2 %collective-permute-start.1 = (bf16[3,2,3072]{2,1,0:T(2,128)(2,1)S(1)}, bf16[3,2,3072]{2,1,0:T(2,128)(2,1)S(1)}, u32[]{:S(2)}, u32[]{:S(2)}) collective-permute-start(bf16[3,2,3072]{2,1,0:T(2,128)(2,1)S(1)} %fusion.11), channel_id=1, source_target_pairs={{0,64},{64,128},{128,192},{1,65},{65,129},{129,193},{2,66},{66,130... | collective-permute-start | bytes 110600 | tf_op jit(solution)/shard_map/ppermute | solution.py:17
  225.1 6.6 %copy-start.2 = (f32[256,3072]{1,0:T(8,128)S(1)}, f32[256,3072]{1,0:T(8,128)}, u32[]{:S(2)}) copy-start(f32[256,3072]{1,0:T(8,128)} %shard_map.82.x_ref) | copy-start | bytes 9437188
  263.5 5.2 %collective-permute-start.2 = (bf16[3,2,3072]{2,1,0:T(2,128)(2,1)S(1)}, bf16[3,2,3072]{2,1,0:T(2,128)(2,1)S(1)}, u32[]{:S(2)}, u32[]{:S(2)}) collective-permute-start(bf16[3,2,3072]{2,1,0:T(2,128)(2,1)S(1)} %fusion.15), channel_id=1, source_target_pairs={{0,64},{64,128},{128,192},{1,65},{65,129},{129,193},{2,66},{66,130... | collective-permute-start | bytes 110600 | tf_op jit(solution)/shard_map/ppermute | solution.py:17
  313.7 6.6 %copy-start.3 = (f32[256,3072]{1,0:T(8,128)S(1)}, f32[256,3072]{1,0:T(8,128)}, u32[]{:S(2)}) copy-start(f32[256,3072]{1,0:T(8,128)} %shard_map.86.x_ref) | copy-start | bytes 9437188

commit v7 on v6

--- a/solution.py
+++ b/solution.py
@@ -195,18 +195,22 @@
 
 
 def expert_kernel(x_ref, gate_ref, up_ref, down_ref, o_ref):
-    @pl.when(pl.program_id(0) == 0)
-    def _():
-        o_ref[...] = jnp.zeros_like(o_ref)
-
     rows = x_ref[...]
     gate_val = jnp.dot(rows, gate_ref[...], preferred_element_type=jnp.float32)
     up_val = jnp.dot(rows, up_ref[...], preferred_element_type=jnp.float32)
     hidden = (gate_val / (1.0 + jnp.exp(-gate_val)) * up_val).astype(jnp.bfloat16)
-    o_ref[...] += jnp.dot(hidden, down_ref[...], preferred_element_type=jnp.float32)
-
-
-def expert(rows, gate_part, up_part, down_part, chunk=128):
+    term = jnp.dot(hidden, down_ref[...], preferred_element_type=jnp.float32)
+
+    @pl.when(pl.program_id(0) == 0)
+    def _():
+        o_ref[...] = term
+
+    @pl.when(pl.program_id(0) > 0)
+    def _():
+        o_ref[...] += term
+
+
+def expert(rows, gate_part, up_part, down_part, chunk=256):
     count, width = rows.shape
     hidden = gate_part.shape[1]
     return pl.pallas_call(

time: 356 us -> 348 us (0.978)
  Pallas kernels: 291 us -> 283 us
    pallas_call x4, Pallas kernels: 41.5 us -> 33.8 us  [expert(): pl.pallas_call(expert_kernel, out_shape=jax.ShapeDtypeStruct((count, widt...]
where the time goes in v7:
time: 348 us; the launch traced here: 345 us
  Pallas kernels  283 us (81%)
  local copies, waits for them, and re-layouts  24.3 us (7%)
  other arithmetic  21.6 us (6%)
  starting transfers between devices  11.5 us (3%)
    pallas_call x4, Pallas kernels, ring_gather(): pl.pallas_call(functools.partial(ring_gather_kernel, ring_y, ring_z), out...  120 us
    pallas_call x4, Pallas kernels, chip_exchange(): pl.pallas_call(functools.partial(chip_exchange_kernel, ring_y, ring_z, pe...  103 us
    pallas_call x4, Pallas kernels, expert(): pl.pallas_call(expert_kernel, out_shape=jax.ShapeDtypeStruct((count, widt...  33.8 us
    pallas_call x4, Pallas kernels, pair_send(): pl.pallas_call(pair_send_kernel, out_shape=jax.ShapeDtypeStruct((value.sh...  26.4 us
    reshape x4, local copies, waits for them, and re-layouts, shards(): ring_gather(pieces, ring_y, ring_z, 0)  14.8 us
    ppermute x3, starting transfers between devices, shifted(): lax.ppermute(value, axis, [(source, source + steps) for source in range(i...  11.5 us
    convert_element_type x4, other arithmetic, shards(): (partial_sum[:half] + pair_send(partial_sum, 2)).astype(jnp.bfloat16)  9.75 us
    reshape x4, local copies, waits for them, and re-layouts, shards(): chip_sum.reshape(chips, piece_rows, LANES)  8.83 us
  transfers between devices with their start and end apart: 3, of which 3 were waited for; matrix products, arithmetic and copies ran while one was open for 0% of the time, Pallas kernels for 0%

profile of v7, /device:TPU:1, one launch (start us, length us, event | category | flops | bytes accessed | tf_op | source)
XLA Modules:
  0.0 344.7 jit_solution(8965106450815353254)
XLA Ops:
  2.5 32.4 %shard_map.73 = bf16[2,8,4,96,128]{4,3,2,1,0:T(8,128)(2,1)} custom-call(bf16[2,96,128]{2,1,0:T(8,128)(2,1)} %pad_maximum_fusion.x_ref), custom_call_target="tpu_custom_call" | custom-call | tf_op jit(solution)/shard_map/pallas_call | solution.py:179
  34.9 3.7 %reshape.192.x_ref = bf16[256,3072]{1,0:T(8,128)(2,1)} reshape(bf16[2,8,4,96,128]{4,3,2,1,0:T(8,128)(2,1)} %shard_map.73) | data formatting | bytes 3145728 | tf_op jit(solution)/shard_map/reshape | solution.py:322
  38.6 8.4 %shard_map.74.x_ref = f32[256,3072]{1,0:T(8,128)} custom-call(bf16[256,3072]{1,0:T(8,128)(2,1)} %reshape.192.x_ref, bf16[3072,512]{1,0:T(8,128)(2,1)} %bitcast.16, bf16[3072,512]{1,0:T(8,128)(2,1)} %bitcast.20, bf16[512,3072]{1,0:T(8,128)(2,1)} %bitcast.24), custom_call_target="tpu_custom_call" | custom-call | flops 2415919104 | bytes 14155776 | tf_op jit(solution)/shard_map/pallas_call | solution.py:216
  47.1 6.6 %shard_map.75 = f32[128,3072]{1,0:T(8,128)} custom-call(f32[256,3072]{1,0:T(8,128)} %shard_map.74.x_ref), custom_call_target="tpu_custom_call" | custom-call | tf_op jit(solution)/shard_map/pallas_call | solution.py:289
  53.7 2.4 fusion.3
  56.1 2.2 reshape.193.x_ref
  58.3 26.9 %shard_map.76 = bf16[32,96,128]{2,1,0:T(8,128)(2,1)} custom-call(bf16[32,96,128]{2,1,0:T(8,128)(2,1)} %reshape.193.x_ref), custom_call_target="tpu_custom_call" | custom-call | tf_op jit(solution)/shard_map/pallas_call | solution.py:89
  85.3 1.3 convert_element_type.67
  87.6 3.1 collective-permute-start
  92.8 28.5 %shard_map.77 = bf16[2,8,4,96,128]{4,3,2,1,0:T(8,128)(2,1)} custom-call(bf16[2,96,128]{2,1,0:T(8,128)(2,1)} %pad_maximum_fusion.1.x_ref), custom_call_target="tpu_custom_call" | custom-call | tf_op jit(solution)/shard_map/pallas_call | solution.py:179
  121.3 3.7 %reshape.194.x_ref = bf16[256,3072]{1,0:T(8,128)(2,1)} reshape(bf16[2,8,4,96,128]{4,3,2,1,0:T(8,128)(2,1)} %shard_map.77) | data formatting | bytes 3145728 | tf_op jit(solution)/shard_map/reshape | solution.py:322
  125.0 8.5 %shard_map.78.x_ref = f32[256,3072]{1,0:T(8,128)} custom-call(bf16[256,3072]{1,0:T(8,128)(2,1)} %reshape.194.x_ref, bf16[3072,512]{1,0:T(8,128)(2,1)} %bitcast.17, bf16[3072,512]{1,0:T(8,128)(2,1)} %bitcast.21, bf16[512,3072]{1,0:T(8,128)(2,1)} %bitcast.25), custom_call_target="tpu_custom_call" | custom-call | flops 2415919104 | bytes 14155776 | tf_op jit(solution)/shard_map/pallas_call | solution.py:216
  133.5 6.6 %shard_map.79 = f32[128,3072]{1,0:T(8,128)} custom-call(f32[256,3072]{1,0:T(8,128)} %shard_map.78.x_ref), custom_call_target="tpu_custom_call" | custom-call | tf_op jit(solution)/shard_map/pallas_call | solution.py:289
  140.1 2.4 fusion.2
  142.5 2.2 reshape.195.x_ref
  144.7 24.8 %shard_map.80 = bf16[32,96,128]{2,1,0:T(8,128)(2,1)} custom-call(bf16[32,96,128]{2,1,0:T(8,128)(2,1)} %reshape.195.x_ref), custom_call_target="tpu_custom_call" | custom-call | tf_op jit(solution)/shard_map/pallas_call | solution.py:89
  171.2 4.2 %collective-permute-start.1 = (bf16[3,2,3072]{2,1,0:T(2,128)(2,1)S(1)}, bf16[3,2,3072]{2,1,0:T(2,128)(2,1)S(1)}, u32[]{:S(2)}, u32[]{:S(2)}) collective-permute-start(bf16[3,2,3072]{2,1,0:T(2,128)(2,1)S(1)} %fusion.11), channel_id=1, source_target_pairs={{0,64},{64,128},{128,192},{1,65},{65,129},{129,193},{2,66},{66,130... | collective-permute-start | bytes 110600 | tf_op jit(solution)/shard_map/ppermute | solution.py:17
  177.2 29.9 %shard_map.81 = bf16[2,8,4,96,128]{4,3,2,1,0:T(8,128)(2,1)} custom-call(bf16[2,96,128]{2,1,0:T(8,128)(2,1)} %pad_maximum_fusion.2.x_ref), custom_call_target="tpu_custom_call" | custom-call | tf_op jit(solution)/shard_map/pallas_call | solution.py:179
  207.1 3.7 %reshape.196.x_ref = bf16[256,3072]{1,0:T(8,128)(2,1)} reshape(bf16[2,8,4,96,128]{4,3,2,1,0:T(8,128)(2,1)} %shard_map.81) | data formatting | bytes 3145728 | tf_op jit(solution)/shard_map/reshape | solution.py:322
  210.8 8.5 %shard_map.82.x_ref = f32[256,3072]{1,0:T(8,128)} custom-call(bf16[256,3072]{1,0:T(8,128)(2,1)} %reshape.196.x_ref, bf16[3072,512]{1,0:T(8,128)(2,1)} %bitcast.18, bf16[3072,512]{1,0:T(8,128)(2,1)} %bitcast.22, bf16[512,3072]{1,0:T(8,128)(2,1)} %bitcast.26), custom_call_target="tpu_custom_call" | custom-call | flops 2415919104 | bytes 14155776 | tf_op jit(solution)/shard_map/pallas_call | solution.py:216
  219.3 6.6 %shard_map.83 = f32[128,3072]{1,0:T(8,128)} custom-call(f32[256,3072]{1,0:T(8,128)} %shard_map.82.x_ref), custom_call_target="tpu_custom_call" | custom-call | tf_op jit(solution)/shard_map/pallas_call | solution.py:289
  225.9 2.4 fusion.1
  228.3 2.2 reshape.197.x_ref
  230.6 25.9 %shard_map.84 = bf16[32,96,128]{2,1,0:T(8,128)(2,1)} custom-call(bf16[32,96,128]{2,1,0:T(8,128)(2,1)} %reshape.197.x_ref), custom_call_target="tpu_custom_call" | custom-call | tf_op jit(solution)/shard_map/pallas_call | solution.py:89
  258.1 4.1 %collective-permute-start.2 = (bf16[3,2,3072]{2,1,0:T(2,128)(2,1)S(1)}, bf16[3,2,3072]{2,1,0:T(2,128)(2,1)S(1)}, u32[]{:S(2)}, u32[]{:S(2)}) collective-permute-start(bf16[3,2,3072]{2,1,0:T(2,128)(2,1)S(1)} %fusion.15), channel_id=1, source_target_pairs={{0,64},{64,128},{128,192},{1,65},{65,129},{129,193},{2,66},{66,130... | collective-permute-start | bytes 110600 | tf_op jit(solution)/shard_map/ppermute | solution.py:17
  264.3 29.1 %shard_map.85 = bf16[2,8,4,96,128]{4,3,2,1,0:T(8,128)(2,1)} custom-call(bf16[2,96,128]{2,1,0:T(8,128)(2,1)} %pad_maximum_fusion.3.x_ref), custom_call_target="tpu_custom_call" | custom-call | tf_op jit(solution)/shard_map/pallas_call | solution.py:179
  293.4 3.7 %reshape.198.x_ref = bf16[256,3072]{1,0:T(8,128)(2,1)} reshape(bf16[2,8,4,96,128]{4,3,2,1,0:T(8,128)(2,1)} %shard_map.85) | data formatting | bytes 3145728 | tf_op jit(solution)/shard_map/reshape | solution.py:322
  297.1 8.4 %shard_map.86.x_ref = f32[256,3072]{1,0:T(8,128)} custom-call(bf16[256,3072]{1,0:T(8,128)(2,1)} %reshape.198.x_ref, bf16[3072,512]{1,0:T(8,128)(2,1)} %bitcast.19, bf16[3072,512]{1,0:T(8,128)(2,1)} %bitcast.23, bf16[512,3072]{1,0:T(8,128)(2,1)} %bitcast.27), custom_call_target="tpu_custom_call" | custom-call | flops 2415919104 | bytes 14155776 | tf_op jit(solution)/shard_map/pallas_call | solution.py:216
  305.6 6.6 %shard_map.87 = f32[128,3072]{1,0:T(8,128)} custom-call(f32[256,3072]{1,0:T(8,128)} %shard_map.86.x_ref), custom_call_target="tpu_custom_call" | custom-call | tf_op jit(solution)/shard_map/pallas_call | solution.py:289
  312.2 2.4 fusion
  314.6 2.2 reshape.199.x_ref
  316.8 25.5 %shard_map.88 = bf16[32,96,128]{2,1,0:T(8,128)(2,1)} custom-call(bf16[32,96,128]{2,1,0:T(8,128)(2,1)} %reshape.199.x_ref), custom_call_target="tpu_custom_call" | custom-call | tf_op jit(solution)/shard_map/pallas_call | solution.py:89
  (73 shorter events, 14.1 us)
Async XLA Ops:
  47.0 6.6 %copy-start = (f32[256,3072]{1,0:T(8,128)S(1)}, f32[256,3072]{1,0:T(8,128)}, u32[]{:S(2)}) copy-start(f32[256,3072]{1,0:T(8,128)} %shard_map.74.x_ref) | copy-start | bytes 9437188
  86.6 0.9 copy-start.6
  86.6 0.9 copy-start.4
  86.6 5.4 %copy-start.5 = (f32[1,3072]{1,0:T(1,128)S(1)}, f32[1,3072]{1,0:T(1,128)}, u32[]{:S(2)}) copy-start(f32[1,3072]{1,0:T(1,128)} %param.8) | copy-start | bytes 36868
  87.6 4.2 %collective-permute-start = (bf16[3,2,3072]{2,1,0:T(2,128)(2,1)S(1)}, bf16[3,2,3072]{2,1,0:T(2,128)(2,1)S(1)}, u32[]{:S(2)}, u32[]{:S(2)}) collective-permute-start(bf16[3,2,3072]{2,1,0:T(2,128)(2,1)S(1)} %fusion.7), channel_id=1, source_target_pairs={{0,64},{64,128},{128,192},{1,65},{65,129},{129,193},{2,66},{66,130... | collective-permute-start | bytes 110600 | tf_op jit(solution)/shard_map/ppermute | solution.py:17
  133.5 6.6 %copy-start.1 = (f32[256,3072]{1,0:T(8,128)S(1)}, f32[256,3072]{1,0:T(8,128)}, u32[]{:S(2)}) copy-start(f32[256,3072]{1,0:T(8,128)} %shard_map.78.x_ref) | copy-start | bytes 9437188
  171.2 5.1 %collective-permute-start.1 = (bf16[3,2,3072]{2,1,0:T(2,128)(2,1)S(1)}, bf16[3,2,3072]{2,1,0:T(2,128)(2,1)S(1)}, u32[]{:S(2)}, u32[]{:S(2)}) collective-permute-start(bf16[3,2,3072]{2,1,0:T(2,128)(2,1)S(1)} %fusion.11), channel_id=1, source_target_pairs={{0,64},{64,128},{128,192},{1,65},{65,129},{129,193},{2,66},{66,130... | collective-permute-start | bytes 110600 | tf_op jit(solution)/shard_map/ppermute | solution.py:17
  219.3 6.6 %copy-start.2 = (f32[256,3072]{1,0:T(8,128)S(1)}, f32[256,3072]{1,0:T(8,128)}, u32[]{:S(2)}) copy-start(f32[256,3072]{1,0:T(8,128)} %shard_map.82.x_ref) | copy-start | bytes 9437188
  258.1 5.2 %collective-permute-start.2 = (bf16[3,2,3072]{2,1,0:T(2,128)(2,1)S(1)}, bf16[3,2,3072]{2,1,0:T(2,128)(2,1)S(1)}, u32[]{:S(2)}, u32[]{:S(2)}) collective-permute-start(bf16[3,2,3072]{2,1,0:T(2,128)(2,1)S(1)} %fusion.15), channel_id=1, source_target_pairs={{0,64},{64,128},{128,192},{1,65},{65,129},{129,193},{2,66},{66,130... | collective-permute-start | bytes 110600 | tf_op jit(solution)/shard_map/ppermute | solution.py:17
  305.6 6.6 %copy-start.3 = (f32[256,3072]{1,0:T(8,128)S(1)}, f32[256,3072]{1,0:T(8,128)}, u32[]{:S(2)}) copy-start(f32[256,3072]{1,0:T(8,128)} %shard_map.86.x_ref) | copy-start | bytes 9437188

commit v8 on v7

--- a/solution.py
+++ b/solution.py
@@ -322,7 +322,8 @@
         block_rows = ring_gather(pieces, ring_y, ring_z, 0).reshape(shard_count * 2 * local_rows, width)
         partial_sum = expert(block_rows, gate_part, up_part, down_part)
         half = partial_sum.shape[0] // 2
-        chip_sum = (partial_sum[:half] + pair_send(partial_sum, 2)).astype(jnp.bfloat16)
+        partner_sum = pair_send(partial_sum.astype(jnp.bfloat16), 2).astype(jnp.float32)
+        chip_sum = (partial_sum[:half] + partner_sum).astype(jnp.bfloat16)
         received = chip_exchange(chip_sum.reshape(chips, piece_rows, LANES), ring_y, ring_z, 0, 3)
         received = received.astype(jnp.float32)
         received = received.reshape(2, chips // 2, 2, local_rows, width)

time: 348 us -> 353 us (1.014)
  other arithmetic: 21.6 us -> 34.1 us
  Pallas kernels: 283 us -> 276 us
    convert_element_type x4 -> x8, other arithmetic: 9.75 us -> 22.3 us  [the longest x4 13.6 us: shards(): partial_sum.astype(jnp.bfloat16)]
    pallas_call x4, Pallas kernels: 26.4 us -> 18.4 us  [pair_send(): pl.pallas_call(pair_send_kernel, out_shape=jax.ShapeDtypeStruct((value.sh...]
where the time goes in v8:
time: 353 us; the launch traced here: 350 us
  Pallas kernels  276 us (78%)
  other arithmetic  34.1 us (10%)
  local copies, waits for them, and re-layouts  24.2 us (7%)
  starting transfers between devices  11.6 us (3%)
    pallas_call x4, Pallas kernels, ring_gather(): pl.pallas_call(functools.partial(ring_gather_kernel, ring_y, ring_z), out...  119 us
    pallas_call x4, Pallas kernels, chip_exchange(): pl.pallas_call(functools.partial(chip_exchange_kernel, ring_y, ring_z, pe...  105 us
    pallas_call x4, Pallas kernels, expert(): pl.pallas_call(expert_kernel, out_shape=jax.ShapeDtypeStruct((count, widt...  33.8 us
    pallas_call x4, Pallas kernels, pair_send(): pl.pallas_call(pair_send_kernel, out_shape=jax.ShapeDtypeStruct((value.sh...  18.4 us
    reshape x4, local copies, waits for them, and re-layouts, shards(): ring_gather(pieces, ring_y, ring_z, 0)  14.8 us
    convert_element_type x4, other arithmetic, shards(): partial_sum.astype(jnp.bfloat16)  13.6 us
    ppermute x3, starting transfers between devices, shifted(): lax.ppermute(value, axis, [(source, source + steps) for source in range(i...  11.6 us
    convert_element_type x4, other arithmetic, shards(): chip_sum = (partial_sum[:half] + partner_sum).astype(jnp.bfloat16)  8.74 us
  transfers between devices with their start and end apart: 3, of which 3 were waited for; matrix products, arithmetic and copies ran while one was open for 0% of the time, Pallas kernels for 0%

profile of v8, /device:TPU:1, one launch (start us, length us, event | category | flops | bytes accessed | tf_op | source)
XLA Modules:
  0.0 350.3 jit_solution(14679754920595489742)
XLA Ops:
  2.5 32.4 %shard_map.73 = bf16[2,8,4,96,128]{4,3,2,1,0:T(8,128)(2,1)} custom-call(bf16[2,96,128]{2,1,0:T(8,128)(2,1)} %pad_maximum_fusion.x_ref), custom_call_target="tpu_custom_call" | custom-call | tf_op jit(solution)/shard_map/pallas_call | solution.py:179
  34.9 3.7 %reshape.192.x_ref = bf16[256,3072]{1,0:T(8,128)(2,1)} reshape(bf16[2,8,4,96,128]{4,3,2,1,0:T(8,128)(2,1)} %shard_map.73) | data formatting | bytes 3145728 | tf_op jit(solution)/shard_map/reshape | solution.py:322
  38.6 8.4 %shard_map.74 = f32[256,3072]{1,0:T(8,128)} custom-call(bf16[256,3072]{1,0:T(8,128)(2,1)} %reshape.192.x_ref, bf16[3072,512]{1,0:T(8,128)(2,1)} %bitcast.16, bf16[3072,512]{1,0:T(8,128)(2,1)} %bitcast.20, bf16[512,3072]{1,0:T(8,128)(2,1)} %bitcast.24), custom_call_target="tpu_custom_call" | custom-call | flops 2415919104 | bytes 14155776 | tf_op jit(solution)/shard_map/pallas_call | solution.py:216
  47.1 3.4 convert_element_type.90.x_ref
  50.4 4.6 %shard_map.75 = bf16[128,3072]{1,0:T(8,128)(2,1)} custom-call(bf16[256,3072]{1,0:T(8,128)(2,1)} %convert_element_type.90.x_ref), custom_call_target="tpu_custom_call" | custom-call | tf_op jit(solution)/shard_map/pallas_call | solution.py:289
  55.1 2.2 fusion.3
  57.2 2.2 reshape.193.x_ref
  59.4 27.0 %shard_map.76 = bf16[32,96,128]{2,1,0:T(8,128)(2,1)} custom-call(bf16[32,96,128]{2,1,0:T(8,128)(2,1)} %reshape.193.x_ref), custom_call_target="tpu_custom_call" | custom-call | tf_op jit(solution)/shard_map/pallas_call | solution.py:89
  88.8 3.1 collective-permute-start
  93.9 28.5 %shard_map.77 = bf16[2,8,4,96,128]{4,3,2,1,0:T(8,128)(2,1)} custom-call(bf16[2,96,128]{2,1,0:T(8,128)(2,1)} %pad_maximum_fusion.1.x_ref), custom_call_target="tpu_custom_call" | custom-call | tf_op jit(solution)/shard_map/pallas_call | solution.py:179
  122.4 3.7 %reshape.194.x_ref = bf16[256,3072]{1,0:T(8,128)(2,1)} reshape(bf16[2,8,4,96,128]{4,3,2,1,0:T(8,128)(2,1)} %shard_map.77) | data formatting | bytes 3145728 | tf_op jit(solution)/shard_map/reshape | solution.py:322
  126.2 8.5 %shard_map.78 = f32[256,3072]{1,0:T(8,128)} custom-call(bf16[256,3072]{1,0:T(8,128)(2,1)} %reshape.194.x_ref, bf16[3072,512]{1,0:T(8,128)(2,1)} %bitcast.17, bf16[3072,512]{1,0:T(8,128)(2,1)} %bitcast.21, bf16[512,3072]{1,0:T(8,128)(2,1)} %bitcast.25), custom_call_target="tpu_custom_call" | custom-call | flops 2415919104 | bytes 14155776 | tf_op jit(solution)/shard_map/pallas_call | solution.py:216
  134.6 3.4 convert_element_type.97.x_ref
  138.0 4.6 %shard_map.79 = bf16[128,3072]{1,0:T(8,128)(2,1)} custom-call(bf16[256,3072]{1,0:T(8,128)(2,1)} %convert_element_type.97.x_ref), custom_call_target="tpu_custom_call" | custom-call | tf_op jit(solution)/shard_map/pallas_call | solution.py:289
  142.6 2.2 fusion.2
  147.0 24.8 %shard_map.80 = bf16[32,96,128]{2,1,0:T(8,128)(2,1)} custom-call(bf16[32,96,128]{2,1,0:T(8,128)(2,1)} %reshape.195.x_ref), custom_call_target="tpu_custom_call" | custom-call | tf_op jit(solution)/shard_map/pallas_call | solution.py:89
  173.4 4.2 %collective-permute-start.1 = (bf16[3,2,3072]{2,1,0:T(2,128)(2,1)S(1)}, bf16[3,2,3072]{2,1,0:T(2,128)(2,1)S(1)}, u32[]{:S(2)}, u32[]{:S(2)}) collective-permute-start(bf16[3,2,3072]{2,1,0:T(2,128)(2,1)S(1)} %fusion.11), channel_id=1, source_target_pairs={{0,64},{64,128},{128,192},{1,65},{65,129},{129,193},{2,66},{66,130... | collective-permute-start | bytes 110600 | tf_op jit(solution)/shard_map/ppermute | solution.py:17
  179.4 30.0 %shard_map.81 = bf16[2,8,4,96,128]{4,3,2,1,0:T(8,128)(2,1)} custom-call(bf16[2,96,128]{2,1,0:T(8,128)(2,1)} %pad_maximum_fusion.2.x_ref), custom_call_target="tpu_custom_call" | custom-call | tf_op jit(solution)/shard_map/pallas_call | solution.py:179
  209.5 3.7 %reshape.196.x_ref = bf16[256,3072]{1,0:T(8,128)(2,1)} reshape(bf16[2,8,4,96,128]{4,3,2,1,0:T(8,128)(2,1)} %shard_map.81) | data formatting | bytes 3145728 | tf_op jit(solution)/shard_map/reshape | solution.py:322
  213.2 8.5 %shard_map.82 = f32[256,3072]{1,0:T(8,128)} custom-call(bf16[256,3072]{1,0:T(8,128)(2,1)} %reshape.196.x_ref, bf16[3072,512]{1,0:T(8,128)(2,1)} %bitcast.18, bf16[3072,512]{1,0:T(8,128)(2,1)} %bitcast.22, bf16[512,3072]{1,0:T(8,128)(2,1)} %bitcast.26), custom_call_target="tpu_custom_call" | custom-call | flops 2415919104 | bytes 14155776 | tf_op jit(solution)/shard_map/pallas_call | solution.py:216
  221.6 3.4 convert_element_type.104.x_ref
  225.0 4.6 %shard_map.83 = bf16[128,3072]{1,0:T(8,128)(2,1)} custom-call(bf16[256,3072]{1,0:T(8,128)(2,1)} %convert_element_type.104.x_ref), custom_call_target="tpu_custom_call" | custom-call | tf_op jit(solution)/shard_map/pallas_call | solution.py:289
  229.6 2.2 fusion.1
  234.0 25.8 %shard_map.84 = bf16[32,96,128]{2,1,0:T(8,128)(2,1)} custom-call(bf16[32,96,128]{2,1,0:T(8,128)(2,1)} %reshape.197.x_ref), custom_call_target="tpu_custom_call" | custom-call | tf_op jit(solution)/shard_map/pallas_call | solution.py:89
  261.4 4.3 %collective-permute-start.2 = (bf16[3,2,3072]{2,1,0:T(2,128)(2,1)S(1)}, bf16[3,2,3072]{2,1,0:T(2,128)(2,1)S(1)}, u32[]{:S(2)}, u32[]{:S(2)}) collective-permute-start(bf16[3,2,3072]{2,1,0:T(2,128)(2,1)S(1)} %fusion.15), channel_id=1, source_target_pairs={{0,64},{64,128},{128,192},{1,65},{65,129},{129,193},{2,66},{66,130... | collective-permute-start | bytes 110600 | tf_op jit(solution)/shard_map/ppermute | solution.py:17
  267.7 27.9 %shard_map.85 = bf16[2,8,4,96,128]{4,3,2,1,0:T(8,128)(2,1)} custom-call(bf16[2,96,128]{2,1,0:T(8,128)(2,1)} %pad_maximum_fusion.3.x_ref), custom_call_target="tpu_custom_call" | custom-call | tf_op jit(solution)/shard_map/pallas_call | solution.py:179
  295.7 3.7 %reshape.198.x_ref = bf16[256,3072]{1,0:T(8,128)(2,1)} reshape(bf16[2,8,4,96,128]{4,3,2,1,0:T(8,128)(2,1)} %shard_map.85) | data formatting | bytes 3145728 | tf_op jit(solution)/shard_map/reshape | solution.py:322
  299.4 8.5 %shard_map.86 = f32[256,3072]{1,0:T(8,128)} custom-call(bf16[256,3072]{1,0:T(8,128)(2,1)} %reshape.198.x_ref, bf16[3072,512]{1,0:T(8,128)(2,1)} %bitcast.19, bf16[3072,512]{1,0:T(8,128)(2,1)} %bitcast.23, bf16[512,3072]{1,0:T(8,128)(2,1)} %bitcast.27), custom_call_target="tpu_custom_call" | custom-call | flops 2415919104 | bytes 14155776 | tf_op jit(solution)/shard_map/pallas_call | solution.py:216
  307.8 3.4 convert_element_type.111.x_ref
  311.2 4.6 %shard_map.87 = bf16[128,3072]{1,0:T(8,128)(2,1)} custom-call(bf16[256,3072]{1,0:T(8,128)(2,1)} %convert_element_type.111.x_ref), custom_call_target="tpu_custom_call" | custom-call | tf_op jit(solution)/shard_map/pallas_call | solution.py:289
  315.9 2.2 fusion
  320.2 27.7 %shard_map.88 = bf16[32,96,128]{2,1,0:T(8,128)(2,1)} custom-call(bf16[32,96,128]{2,1,0:T(8,128)(2,1)} %reshape.199.x_ref), custom_call_target="tpu_custom_call" | custom-call | tf_op jit(solution)/shard_map/pallas_call | solution.py:89
  (77 shorter events, 21.9 us)
Async XLA Ops:
  47.0 8.0 %copy-start = (f32[256,3072]{1,0:T(8,128)S(1)}, f32[256,3072]{1,0:T(8,128)}, u32[]{:S(2)}) copy-start(f32[256,3072]{1,0:T(8,128)} %shard_map.74) | copy-start | bytes 9437188
  87.7 0.9 copy-start.6
  87.7 0.9 copy-start.4
  87.7 5.4 %copy-start.5 = (f32[1,3072]{1,0:T(1,128)S(1)}, f32[1,3072]{1,0:T(1,128)}, u32[]{:S(2)}) copy-start(f32[1,3072]{1,0:T(1,128)} %param.8) | copy-start | bytes 36868
  88.8 4.2 %collective-permute-start = (bf16[3,2,3072]{2,1,0:T(2,128)(2,1)S(1)}, bf16[3,2,3072]{2,1,0:T(2,128)(2,1)S(1)}, u32[]{:S(2)}, u32[]{:S(2)}) collective-permute-start(bf16[3,2,3072]{2,1,0:T(2,128)(2,1)S(1)} %fusion.7), channel_id=1, source_target_pairs={{0,64},{64,128},{128,192},{1,65},{65,129},{129,193},{2,66},{66,130... | collective-permute-start | bytes 110600 | tf_op jit(solution)/shard_map/ppermute | solution.py:17
  134.6 8.0 %copy-start.1 = (f32[256,3072]{1,0:T(8,128)S(1)}, f32[256,3072]{1,0:T(8,128)}, u32[]{:S(2)}) copy-start(f32[256,3072]{1,0:T(8,128)} %shard_map.78) | copy-start | bytes 9437188
  173.4 5.0 %collective-permute-start.1 = (bf16[3,2,3072]{2,1,0:T(2,128)(2,1)S(1)}, bf16[3,2,3072]{2,1,0:T(2,128)(2,1)S(1)}, u32[]{:S(2)}, u32[]{:S(2)}) collective-permute-start(bf16[3,2,3072]{2,1,0:T(2,128)(2,1)S(1)} %fusion.11), channel_id=1, source_target_pairs={{0,64},{64,128},{128,192},{1,65},{65,129},{129,193},{2,66},{66,130... | collective-permute-start | bytes 110600 | tf_op jit(solution)/shard_map/ppermute | solution.py:17
  221.6 8.0 %copy-start.2 = (f32[256,3072]{1,0:T(8,128)S(1)}, f32[256,3072]{1,0:T(8,128)}, u32[]{:S(2)}) copy-start(f32[256,3072]{1,0:T(8,128)} %shard_map.82) | copy-start | bytes 9437188
  261.4 5.4 %collective-permute-start.2 = (bf16[3,2,3072]{2,1,0:T(2,128)(2,1)S(1)}, bf16[3,2,3072]{2,1,0:T(2,128)(2,1)S(1)}, u32[]{:S(2)}, u32[]{:S(2)}) collective-permute-start(bf16[3,2,3072]{2,1,0:T(2,128)(2,1)S(1)} %fusion.15), channel_id=1, source_target_pairs={{0,64},{64,128},{128,192},{1,65},{65,129},{129,193},{2,66},{66,130... | collective-permute-start | bytes 110600 | tf_op jit(solution)/shard_map/ppermute | solution.py:17
  307.8 8.0 %copy-start.3 = (f32[256,3072]{1,0:T(8,128)S(1)}, f32[256,3072]{1,0:T(8,128)}, u32[]{:S(2)}) copy-start(f32[256,3072]{1,0:T(8,128)} %shard_map.86) | copy-start | bytes 9437188

commit v9 on v7

--- a/solution.py
+++ b/solution.py
@@ -231,6 +231,44 @@
             bytes_accessed=2 * (count * width + 3 * width * hidden) + 4 * count * width,
         ),
     )(rows, gate_part, up_part, down_part)
+
+
+def segment_shift_kernel(x_ref, o_ref, send_sem, recv_sem):
+    me = lax.axis_index("shard")
+    segment = lax.axis_index("segment")
+    count = lax.axis_size("segment")
+    after = (lax.rem(segment + 1, count), me)
+    before = (lax.rem(segment + count - 1, count), me)
+    barrier = pltpu.get_barrier_semaphore()
+    pl.semaphore_signal(barrier, 1, device_id=after, device_id_type=pl.DeviceIdType.MESH)
+    pl.semaphore_signal(barrier, 1, device_id=before, device_id_type=pl.DeviceIdType.MESH)
+    pl.semaphore_wait(barrier, 2)
+    copies = [
+        pltpu.make_async_remote_copy(
+            src_ref=x_ref,
+            dst_ref=o_ref.at[slot],
+            send_sem=send_sem.at[slot],
+            recv_sem=recv_sem.at[slot],
+            device_id=peer,
+            device_id_type=pl.DeviceIdType.MESH,
+        )
+        for slot, peer in ((0, after), (1, before))
+    ]
+    for copy in copies:
+        copy.start()
+    for copy in copies:
+        copy.wait()
+
+
+def segment_shift(value, collective):
+    return pl.pallas_call(
+        segment_shift_kernel,
+        out_shape=jax.ShapeDtypeStruct((2,) + value.shape, value.dtype),
+        in_specs=[pl.BlockSpec(memory_space=pltpu.VMEM)],
+        out_specs=pl.BlockSpec(memory_space=pltpu.VMEM),
+        scratch_shapes=[pltpu.SemaphoreType.DMA((2,)), pltpu.SemaphoreType.DMA((2,))],
+        compiler_params=pltpu.CompilerParams(collective_id=collective, has_side_effects=True),
+    )(value)[0]
 
 
 def pair_barrier():
@@ -332,7 +370,7 @@
         updated = (carried.astype(jnp.float32) + probs[:, :, None] * mixed).astype(jnp.bfloat16)
         stored = jnp.where(segment_index == tick, updated, stored)
         if tick + 1 < segment_count:
-            carried = shifted(updated, "segment", 1)
+            carried = segment_shift(updated, 4)
     return stored[None]
 
 

time: 348 us -> 360 us (1.034)
  Pallas kernels: 283 us -> 301 us
  starting transfers between devices: 11.5 us -> 0 us
  other arithmetic: 21.6 us -> 28 us
    pallas_call x0 -> x3, Pallas kernels: none -> 16.7 us  [segment_shift(): pl.pallas_call(segment_shift_kernel, out_shape=jax.ShapeDtypeStruct((2,)...]
    ppermute x3 -> x0, starting transfers between devices: 11.5 us -> none  [shifted(): lax.ppermute(value, axis, [(source, source + steps) for source in range(i...]
  transfers between devices with their start and end apart: 3 -> 0, of which waited for: 3 -> 0; matrix products, arithmetic and copies ran while one was open for 0% -> 0% of each run, Pallas kernels for 0% -> 0%
where the time goes in v9:
time: 360 us; the launch traced here: 357 us
  Pallas kernels  301 us (84%)
  other arithmetic  28 us (8%)
  local copies, waits for them, and re-layouts  26.4 us (7%)
    pallas_call x4, Pallas kernels, ring_gather(): pl.pallas_call(functools.partial(ring_gather_kernel, ring_y, ring_z), out...  122 us
    pallas_call x4, Pallas kernels, chip_exchange(): pl.pallas_call(functools.partial(chip_exchange_kernel, ring_y, ring_z, pe...  102 us
    pallas_call x4, Pallas kernels, expert(): pl.pallas_call(expert_kernel, out_shape=jax.ShapeDtypeStruct((count, widt...  33.8 us
    pallas_call x4, Pallas kernels, pair_send(): pl.pallas_call(pair_send_kernel, out_shape=jax.ShapeDtypeStruct((value.sh...  26.4 us
    pallas_call x3, Pallas kernels, segment_shift(): pl.pallas_call(segment_shift_kernel, out_shape=jax.ShapeDtypeStruct((2,)...  16.7 us
    reshape x4, local copies, waits for them, and re-layouts, shards(): ring_gather(pieces, ring_y, ring_z, 0)  14.8 us
    convert_element_type x4, other arithmetic, shards(): (partial_sum[:half] + pair_send(partial_sum, 2)).astype(jnp.bfloat16)  9.75 us
    reshape x4, local copies, waits for them, and re-layouts, shards(): chip_sum.reshape(chips, piece_rows, LANES)  8.83 us

profile of v9, /device:TPU:1, one launch (start us, length us, event | category | flops | bytes accessed | tf_op | source)
XLA Modules:
  0.0 356.8 jit_solution(2643140896927334224)
XLA Ops:
  2.5 32.4 %shard_map.73 = bf16[2,8,4,96,128]{4,3,2,1,0:T(8,128)(2,1)} custom-call(bf16[2,96,128]{2,1,0:T(8,128)(2,1)} %pad_maximum_fusion.x_ref), custom_call_target="tpu_custom_call" | custom-call | tf_op jit(solution)/shard_map/pallas_call | solution.py:179
  34.9 3.7 %reshape.198.x_ref = bf16[256,3072]{1,0:T(8,128)(2,1)} reshape(bf16[2,8,4,96,128]{4,3,2,1,0:T(8,128)(2,1)} %shard_map.73) | data formatting | bytes 3145728 | tf_op jit(solution)/shard_map/reshape | solution.py:360
  38.6 8.4 %shard_map.74.x_ref = f32[256,3072]{1,0:T(8,128)} custom-call(bf16[256,3072]{1,0:T(8,128)(2,1)} %reshape.198.x_ref, bf16[3072,512]{1,0:T(8,128)(2,1)} %bitcast.37, bf16[3072,512]{1,0:T(8,128)(2,1)} %bitcast.41, bf16[512,3072]{1,0:T(8,128)(2,1)} %bitcast.45), custom_call_target="tpu_custom_call" | custom-call | flops 2415919104 | bytes 14155776 | tf_op jit(solution)/shard_map/pallas_call | solution.py:216
  47.1 6.6 %shard_map.75 = f32[128,3072]{1,0:T(8,128)} custom-call(f32[256,3072]{1,0:T(8,128)} %shard_map.74.x_ref), custom_call_target="tpu_custom_call" | custom-call | tf_op jit(solution)/shard_map/pallas_call | solution.py:327
  53.7 2.4 fusion.3
  56.1 2.2 reshape.199.x_ref
  58.3 26.9 %shard_map.76 = bf16[32,96,128]{2,1,0:T(8,128)(2,1)} custom-call(bf16[32,96,128]{2,1,0:T(8,128)(2,1)} %reshape.199.x_ref), custom_call_target="tpu_custom_call" | custom-call | tf_op jit(solution)/shard_map/pallas_call | solution.py:89
  85.3 1.3 convert_element_type.76
  88.3 5.8 %shard_map.77 = bf16[2,3,2,3072]{3,2,1,0:T(2,128)(2,1)} custom-call(bf16[3,2,3072]{2,1,0:T(2,128)(2,1)} %fusion.7.x_ref), custom_call_target="tpu_custom_call" | custom-call | tf_op jit(solution)/shard_map/pallas_call | solution.py:264
  96.5 29.0 %shard_map.78 = bf16[2,8,4,96,128]{4,3,2,1,0:T(8,128)(2,1)} custom-call(bf16[2,96,128]{2,1,0:T(8,128)(2,1)} %pad_maximum_fusion.1.x_ref), custom_call_target="tpu_custom_call" | custom-call | tf_op jit(solution)/shard_map/pallas_call | solution.py:179
  125.5 3.7 %reshape.200.x_ref = bf16[256,3072]{1,0:T(8,128)(2,1)} reshape(bf16[2,8,4,96,128]{4,3,2,1,0:T(8,128)(2,1)} %shard_map.78) | data formatting | bytes 3145728 | tf_op jit(solution)/shard_map/reshape | solution.py:360
  129.2 8.5 %shard_map.79.x_ref = f32[256,3072]{1,0:T(8,128)} custom-call(bf16[256,3072]{1,0:T(8,128)(2,1)} %reshape.200.x_ref, bf16[3072,512]{1,0:T(8,128)(2,1)} %bitcast.38, bf16[3072,512]{1,0:T(8,128)(2,1)} %bitcast.42, bf16[512,3072]{1,0:T(8,128)(2,1)} %bitcast.46), custom_call_target="tpu_custom_call" | custom-call | flops 2415919104 | bytes 14155776 | tf_op jit(solution)/shard_map/pallas_call | solution.py:216
  137.7 6.6 %shard_map.80 = f32[128,3072]{1,0:T(8,128)} custom-call(f32[256,3072]{1,0:T(8,128)} %shard_map.79.x_ref), custom_call_target="tpu_custom_call" | custom-call | tf_op jit(solution)/shard_map/pallas_call | solution.py:327
  144.3 2.4 fusion.2
  146.7 2.2 reshape.201.x_ref
  148.9 24.8 %shard_map.81 = bf16[32,96,128]{2,1,0:T(8,128)(2,1)} custom-call(bf16[32,96,128]{2,1,0:T(8,128)(2,1)} %reshape.201.x_ref), custom_call_target="tpu_custom_call" | custom-call | tf_op jit(solution)/shard_map/pallas_call | solution.py:89
  176.6 5.5 %shard_map.82 = bf16[2,3,2,3072]{3,2,1,0:T(2,128)(2,1)} custom-call(bf16[3,2,3072]{2,1,0:T(2,128)(2,1)} %fusion.11.x_ref), custom_call_target="tpu_custom_call" | custom-call | tf_op jit(solution)/shard_map/pallas_call | solution.py:264
  184.6 29.9 %shard_map.83 = bf16[2,8,4,96,128]{4,3,2,1,0:T(8,128)(2,1)} custom-call(bf16[2,96,128]{2,1,0:T(8,128)(2,1)} %pad_maximum_fusion.2.x_ref), custom_call_target="tpu_custom_call" | custom-call | tf_op jit(solution)/shard_map/pallas_call | solution.py:179
  214.5 3.7 %reshape.202.x_ref = bf16[256,3072]{1,0:T(8,128)(2,1)} reshape(bf16[2,8,4,96,128]{4,3,2,1,0:T(8,128)(2,1)} %shard_map.83) | data formatting | bytes 3145728 | tf_op jit(solution)/shard_map/reshape | solution.py:360
  218.3 8.5 %shard_map.84.x_ref = f32[256,3072]{1,0:T(8,128)} custom-call(bf16[256,3072]{1,0:T(8,128)(2,1)} %reshape.202.x_ref, bf16[3072,512]{1,0:T(8,128)(2,1)} %bitcast.39, bf16[3072,512]{1,0:T(8,128)(2,1)} %bitcast.43, bf16[512,3072]{1,0:T(8,128)(2,1)} %bitcast.47), custom_call_target="tpu_custom_call" | custom-call | flops 2415919104 | bytes 14155776 | tf_op jit(solution)/shard_map/pallas_call | solution.py:216
  226.7 6.6 %shard_map.85 = f32[128,3072]{1,0:T(8,128)} custom-call(f32[256,3072]{1,0:T(8,128)} %shard_map.84.x_ref), custom_call_target="tpu_custom_call" | custom-call | tf_op jit(solution)/shard_map/pallas_call | solution.py:327
  233.3 2.4 fusion.1
  235.8 2.2 reshape.203.x_ref
  238.0 25.6 %shard_map.86 = bf16[32,96,128]{2,1,0:T(8,128)(2,1)} custom-call(bf16[32,96,128]{2,1,0:T(8,128)(2,1)} %reshape.203.x_ref), custom_call_target="tpu_custom_call" | custom-call | tf_op jit(solution)/shard_map/pallas_call | solution.py:89
  266.5 5.5 %shard_map.87 = bf16[2,3,2,3072]{3,2,1,0:T(2,128)(2,1)} custom-call(bf16[3,2,3072]{2,1,0:T(2,128)(2,1)} %fusion.15.x_ref), custom_call_target="tpu_custom_call" | custom-call | tf_op jit(solution)/shard_map/pallas_call | solution.py:264
  274.4 30.9 %shard_map.88 = bf16[2,8,4,96,128]{4,3,2,1,0:T(8,128)(2,1)} custom-call(bf16[2,96,128]{2,1,0:T(8,128)(2,1)} %pad_maximum_fusion.3.x_ref), custom_call_target="tpu_custom_call" | custom-call | tf_op jit(solution)/shard_map/pallas_call | solution.py:179
  305.3 3.7 %reshape.204.x_ref = bf16[256,3072]{1,0:T(8,128)(2,1)} reshape(bf16[2,8,4,96,128]{4,3,2,1,0:T(8,128)(2,1)} %shard_map.88) | data formatting | bytes 3145728 | tf_op jit(solution)/shard_map/reshape | solution.py:360
  309.0 8.4 %shard_map.89.x_ref = f32[256,3072]{1,0:T(8,128)} custom-call(bf16[256,3072]{1,0:T(8,128)(2,1)} %reshape.204.x_ref, bf16[3072,512]{1,0:T(8,128)(2,1)} %bitcast.40, bf16[3072,512]{1,0:T(8,128)(2,1)} %bitcast.44, bf16[512,3072]{1,0:T(8,128)(2,1)} %bitcast.48), custom_call_target="tpu_custom_call" | custom-call | flops 2415919104 | bytes 14155776 | tf_op jit(solution)/shard_map/pallas_call | solution.py:216
  317.5 6.6 %shard_map.90 = f32[128,3072]{1,0:T(8,128)} custom-call(f32[256,3072]{1,0:T(8,128)} %shard_map.89.x_ref), custom_call_target="tpu_custom_call" | custom-call | tf_op jit(solution)/shard_map/pallas_call | solution.py:327
  324.1 2.4 fusion
  326.5 2.2 reshape.205.x_ref
  328.7 25.0 %shard_map.91 = bf16[32,96,128]{2,1,0:T(8,128)(2,1)} custom-call(bf16[32,96,128]{2,1,0:T(8,128)(2,1)} %reshape.205.x_ref), custom_call_target="tpu_custom_call" | custom-call | tf_op jit(solution)/shard_map/pallas_call | solution.py:89
  (78 shorter events, 19.7 us)
Async XLA Ops:
  47.0 6.6 %copy-start = (f32[256,3072]{1,0:T(8,128)S(1)}, f32[256,3072]{1,0:T(8,128)}, u32[]{:S(2)}) copy-start(f32[256,3072]{1,0:T(8,128)} %shard_map.74.x_ref) | copy-start | bytes 9437188
  86.6 0.9 copy-start.10
  86.6 0.9 copy-start.6
  86.6 8.3 %copy-start.8 = (f32[1,3072]{1,0:T(1,128)S(1)}, f32[1,3072]{1,0:T(1,128)}, u32[]{:S(2)}) copy-start(f32[1,3072]{1,0:T(1,128)} %param.8) | copy-start | bytes 36868
  137.7 6.6 %copy-start.1 = (f32[256,3072]{1,0:T(8,128)S(1)}, f32[256,3072]{1,0:T(8,128)}, u32[]{:S(2)}) copy-start(f32[256,3072]{1,0:T(8,128)} %shard_map.79.x_ref) | copy-start | bytes 9437188
  175.0 0.9 copy-start.4
  226.7 6.6 %copy-start.2 = (f32[256,3072]{1,0:T(8,128)S(1)}, f32[256,3072]{1,0:T(8,128)}, u32[]{:S(2)}) copy-start(f32[256,3072]{1,0:T(8,128)} %shard_map.84.x_ref) | copy-start | bytes 9437188
  264.9 0.9 copy-start.5
  264.9 8.0 %copy-start.9 = (f32[1,3072]{1,0:T(1,128)S(1)}, f32[1,3072]{1,0:T(1,128)}, u32[]{:S(2)}) copy-start(f32[1,3072]{1,0:T(1,128)} %param.8) | copy-start | bytes 36868
  317.5 6.6 %copy-start.3 = (f32[256,3072]{1,0:T(8,128)S(1)}, f32[256,3072]{1,0:T(8,128)}, u32[]{:S(2)}) copy-start(f32[256,3072]{1,0:T(8,128)} %shard_map.89.x_ref) | copy-start | bytes 9437188
  355.0 0.9 copy-start.7

commit v10 on v7

--- a/solution.py
+++ b/solution.py
@@ -135,6 +135,18 @@
         y_copy(origin, origin).wait_recv()
         y_copy(lax.rem(y + step, ring_y), y).wait_send()
 
+    def pair_copy(slot):
+        return pltpu.make_async_remote_copy(
+            src_ref=o_ref.at[0, slot],
+            dst_ref=o_ref.at[1, slot],
+            send_sem=send_c.at[slot],
+            recv_sem=recv_c.at[slot],
+            device_id=partner,
+            device_id_type=pl.DeviceIdType.MESH,
+        )
+
+    pair_copy(z).start()
+
     def z_copy(slot, peer_z, sems, index):
         return pltpu.make_async_remote_copy(
             src_ref=o_ref.at[0, slot],
@@ -149,29 +161,28 @@
         up_slot = lax.rem(z + ring_z - step, ring_z)
         if step > 0:
             z_copy(up_slot, down_z, send_up, step).wait_recv()
+            pair_copy(up_slot).start()
         z_copy(up_slot, up_z, send_up, step).start()
         if step < half_z - 1:
             down_slot = lax.rem(z + step, ring_z)
             if step > 0:
                 z_copy(down_slot, up_z, send_down, step).wait_recv()
+                pair_copy(down_slot).start()
             z_copy(down_slot, down_z, send_down, step).start()
-    z_copy(lax.rem(z + ring_z - half_z, ring_z), down_z, send_up, 0).wait_recv()
-    z_copy(lax.rem(z + half_z - 1, ring_z), up_z, send_down, 0).wait_recv()
+    last_up = lax.rem(z + ring_z - half_z, ring_z)
+    z_copy(last_up, down_z, send_up, 0).wait_recv()
+    pair_copy(last_up).start()
+    last_down = lax.rem(z + half_z - 1, ring_z)
+    z_copy(last_down, up_z, send_down, 0).wait_recv()
+    pair_copy(last_down).start()
     for step in range(half_z):
         z_copy(lax.rem(z + ring_z - step, ring_z), up_z, send_up, step).wait_send()
         if step < half_z - 1:
             z_copy(lax.rem(z + step, ring_z), down_z, send_down, step).wait_send()
 
-    pair = pltpu.make_async_remote_copy(
-        src_ref=o_ref.at[0],
-        dst_ref=o_ref.at[1],
-        send_sem=send_c,
-        recv_sem=recv_c,
-        device_id=partner,
-        device_id_type=pl.DeviceIdType.MESH,
-    )
-    pair.start()
-    pair.wait()
+    for slot in range(ring_z):
+        pair_copy(slot).wait_send()
+        pair_copy(slot).wait_recv()
 
 
 def ring_gather(pieces, ring_y, ring_z, collective):
@@ -187,8 +198,8 @@
             pltpu.SemaphoreType.DMA((ring_z // 2,)),
             pltpu.SemaphoreType.DMA((ring_z // 2,)),
             pltpu.SemaphoreType.DMA((ring_z,)),
-            pltpu.SemaphoreType.DMA(()),
-            pltpu.SemaphoreType.DMA(()),
+            pltpu.SemaphoreType.DMA((ring_z,)),
+            pltpu.SemaphoreType.DMA((ring_z,)),
         ],
         compiler_params=pltpu.CompilerParams(collective_id=collective, has_side_effects=True),
     )(pieces)

time: 348 us -> 346 us (level)
  no operation moved by 1% of the time
where the time goes in v10:
time: 346 us; the launch traced here: 342 us
  Pallas kernels  281 us (81%)
  local copies, waits for them, and re-layouts  24.3 us (7%)
  other arithmetic  21.6 us (6%)
  starting transfers between devices  11.2 us (3%)
    pallas_call x4, Pallas kernels, ring_gather(): pl.pallas_call(functools.partial(ring_gather_kernel, ring_y, ring_z), out...  118 us
    pallas_call x4, Pallas kernels, chip_exchange(): pl.pallas_call(functools.partial(chip_exchange_kernel, ring_y, ring_z, pe...  102 us
    pallas_call x4, Pallas kernels, expert(): pl.pallas_call(expert_kernel, out_shape=jax.ShapeDtypeStruct((count, widt...  33.8 us
    pallas_call x4, Pallas kernels, pair_send(): pl.pallas_call(pair_send_kernel, out_shape=jax.ShapeDtypeStruct((value.sh...  26.4 us
    reshape x4, local copies, waits for them, and re-layouts, shards(): ring_gather(pieces, ring_y, ring_z, 0)  14.8 us
    ppermute x3, starting transfers between devices, shifted(): lax.ppermute(value, axis, [(source, source + steps) for source in range(i...  11.2 us
    convert_element_type x4, other arithmetic, shards(): (partial_sum[:half] + pair_send(partial_sum, 2)).astype(jnp.bfloat16)  9.75 us
    reshape x4, local copies, waits for them, and re-layouts, shards(): chip_sum.reshape(chips, piece_rows, LANES)  8.83 us
  transfers between devices with their start and end apart: 3, of which 3 were waited for; matrix products, arithmetic and copies ran while one was open for 0% of the time, Pallas kernels for 0%

profile of v10, /device:TPU:1, one launch (start us, length us, event | category | flops | bytes accessed | tf_op | source)
XLA Modules:
  0.0 342.0 jit_solution(17489930452390583522)
XLA Ops:
  2.5 31.7 %shard_map.73 = bf16[2,8,4,96,128]{4,3,2,1,0:T(8,128)(2,1)} custom-call(bf16[2,96,128]{2,1,0:T(8,128)(2,1)} %pad_maximum_fusion.x_ref), custom_call_target="tpu_custom_call" | custom-call | tf_op jit(solution)/shard_map/pallas_call | solution.py:190
  34.2 3.7 %reshape.192.x_ref = bf16[256,3072]{1,0:T(8,128)(2,1)} reshape(bf16[2,8,4,96,128]{4,3,2,1,0:T(8,128)(2,1)} %shard_map.73) | data formatting | bytes 3145728 | tf_op jit(solution)/shard_map/reshape | solution.py:333
  37.9 8.4 %shard_map.74.x_ref = f32[256,3072]{1,0:T(8,128)} custom-call(bf16[256,3072]{1,0:T(8,128)(2,1)} %reshape.192.x_ref, bf16[3072,512]{1,0:T(8,128)(2,1)} %bitcast.16, bf16[3072,512]{1,0:T(8,128)(2,1)} %bitcast.20, bf16[512,3072]{1,0:T(8,128)(2,1)} %bitcast.24), custom_call_target="tpu_custom_call" | custom-call | flops 2415919104 | bytes 14155776 | tf_op jit(solution)/shard_map/pallas_call | solution.py:227
  46.3 6.6 %shard_map.75 = f32[128,3072]{1,0:T(8,128)} custom-call(f32[256,3072]{1,0:T(8,128)} %shard_map.74.x_ref), custom_call_target="tpu_custom_call" | custom-call | tf_op jit(solution)/shard_map/pallas_call | solution.py:300
  53.0 2.4 fusion.3
  55.4 2.2 reshape.193.x_ref
  57.6 26.9 %shard_map.76 = bf16[32,96,128]{2,1,0:T(8,128)(2,1)} custom-call(bf16[32,96,128]{2,1,0:T(8,128)(2,1)} %reshape.193.x_ref), custom_call_target="tpu_custom_call" | custom-call | tf_op jit(solution)/shard_map/pallas_call | solution.py:89
  84.5 1.3 convert_element_type.67
  86.9 3.0 collective-permute-start
  91.9 28.0 %shard_map.77 = bf16[2,8,4,96,128]{4,3,2,1,0:T(8,128)(2,1)} custom-call(bf16[2,96,128]{2,1,0:T(8,128)(2,1)} %pad_maximum_fusion.1.x_ref), custom_call_target="tpu_custom_call" | custom-call | tf_op jit(solution)/shard_map/pallas_call | solution.py:190
  119.9 3.7 %reshape.194.x_ref = bf16[256,3072]{1,0:T(8,128)(2,1)} reshape(bf16[2,8,4,96,128]{4,3,2,1,0:T(8,128)(2,1)} %shard_map.77) | data formatting | bytes 3145728 | tf_op jit(solution)/shard_map/reshape | solution.py:333
  123.6 8.5 %shard_map.78.x_ref = f32[256,3072]{1,0:T(8,128)} custom-call(bf16[256,3072]{1,0:T(8,128)(2,1)} %reshape.194.x_ref, bf16[3072,512]{1,0:T(8,128)(2,1)} %bitcast.17, bf16[3072,512]{1,0:T(8,128)(2,1)} %bitcast.21, bf16[512,3072]{1,0:T(8,128)(2,1)} %bitcast.25), custom_call_target="tpu_custom_call" | custom-call | flops 2415919104 | bytes 14155776 | tf_op jit(solution)/shard_map/pallas_call | solution.py:227
  132.1 6.6 %shard_map.79 = f32[128,3072]{1,0:T(8,128)} custom-call(f32[256,3072]{1,0:T(8,128)} %shard_map.78.x_ref), custom_call_target="tpu_custom_call" | custom-call | tf_op jit(solution)/shard_map/pallas_call | solution.py:300
  138.7 2.4 fusion.2
  141.1 2.2 reshape.195.x_ref
  143.3 24.6 %shard_map.80 = bf16[32,96,128]{2,1,0:T(8,128)(2,1)} custom-call(bf16[32,96,128]{2,1,0:T(8,128)(2,1)} %reshape.195.x_ref), custom_call_target="tpu_custom_call" | custom-call | tf_op jit(solution)/shard_map/pallas_call | solution.py:89
  169.5 4.3 %collective-permute-start.1 = (bf16[3,2,3072]{2,1,0:T(2,128)(2,1)S(1)}, bf16[3,2,3072]{2,1,0:T(2,128)(2,1)S(1)}, u32[]{:S(2)}, u32[]{:S(2)}) collective-permute-start(bf16[3,2,3072]{2,1,0:T(2,128)(2,1)S(1)} %fusion.11), channel_id=1, source_target_pairs={{0,64},{64,128},{128,192},{1,65},{65,129},{129,193},{2,66},{66,130... | collective-permute-start | bytes 110600 | tf_op jit(solution)/shard_map/ppermute | solution.py:17
  175.7 29.3 %shard_map.81 = bf16[2,8,4,96,128]{4,3,2,1,0:T(8,128)(2,1)} custom-call(bf16[2,96,128]{2,1,0:T(8,128)(2,1)} %pad_maximum_fusion.2.x_ref), custom_call_target="tpu_custom_call" | custom-call | tf_op jit(solution)/shard_map/pallas_call | solution.py:190
  205.0 3.7 %reshape.196.x_ref = bf16[256,3072]{1,0:T(8,128)(2,1)} reshape(bf16[2,8,4,96,128]{4,3,2,1,0:T(8,128)(2,1)} %shard_map.81) | data formatting | bytes 3145728 | tf_op jit(solution)/shard_map/reshape | solution.py:333
  208.7 8.4 %shard_map.82.x_ref = f32[256,3072]{1,0:T(8,128)} custom-call(bf16[256,3072]{1,0:T(8,128)(2,1)} %reshape.196.x_ref, bf16[3072,512]{1,0:T(8,128)(2,1)} %bitcast.18, bf16[3072,512]{1,0:T(8,128)(2,1)} %bitcast.22, bf16[512,3072]{1,0:T(8,128)(2,1)} %bitcast.26), custom_call_target="tpu_custom_call" | custom-call | flops 2415919104 | bytes 14155776 | tf_op jit(solution)/shard_map/pallas_call | solution.py:227
  217.2 6.6 %shard_map.83 = f32[128,3072]{1,0:T(8,128)} custom-call(f32[256,3072]{1,0:T(8,128)} %shard_map.82.x_ref), custom_call_target="tpu_custom_call" | custom-call | tf_op jit(solution)/shard_map/pallas_call | solution.py:300
  223.8 2.4 fusion.1
  226.2 2.2 reshape.197.x_ref
  228.4 25.3 %shard_map.84 = bf16[32,96,128]{2,1,0:T(8,128)(2,1)} custom-call(bf16[32,96,128]{2,1,0:T(8,128)(2,1)} %reshape.197.x_ref), custom_call_target="tpu_custom_call" | custom-call | tf_op jit(solution)/shard_map/pallas_call | solution.py:89
  255.3 3.8 %collective-permute-start.2 = (bf16[3,2,3072]{2,1,0:T(2,128)(2,1)S(1)}, bf16[3,2,3072]{2,1,0:T(2,128)(2,1)S(1)}, u32[]{:S(2)}, u32[]{:S(2)}) collective-permute-start(bf16[3,2,3072]{2,1,0:T(2,128)(2,1)S(1)} %fusion.15), channel_id=1, source_target_pairs={{0,64},{64,128},{128,192},{1,65},{65,129},{129,193},{2,66},{66,130... | collective-permute-start | bytes 110600 | tf_op jit(solution)/shard_map/ppermute | solution.py:17
  261.2 29.6 %shard_map.85 = bf16[2,8,4,96,128]{4,3,2,1,0:T(8,128)(2,1)} custom-call(bf16[2,96,128]{2,1,0:T(8,128)(2,1)} %pad_maximum_fusion.3.x_ref), custom_call_target="tpu_custom_call" | custom-call | tf_op jit(solution)/shard_map/pallas_call | solution.py:190
  290.7 3.7 %reshape.198.x_ref = bf16[256,3072]{1,0:T(8,128)(2,1)} reshape(bf16[2,8,4,96,128]{4,3,2,1,0:T(8,128)(2,1)} %shard_map.85) | data formatting | bytes 3145728 | tf_op jit(solution)/shard_map/reshape | solution.py:333
  294.4 8.5 %shard_map.86.x_ref = f32[256,3072]{1,0:T(8,128)} custom-call(bf16[256,3072]{1,0:T(8,128)(2,1)} %reshape.198.x_ref, bf16[3072,512]{1,0:T(8,128)(2,1)} %bitcast.19, bf16[3072,512]{1,0:T(8,128)(2,1)} %bitcast.23, bf16[512,3072]{1,0:T(8,128)(2,1)} %bitcast.27), custom_call_target="tpu_custom_call" | custom-call | flops 2415919104 | bytes 14155776 | tf_op jit(solution)/shard_map/pallas_call | solution.py:227
  302.9 6.6 %shard_map.87 = f32[128,3072]{1,0:T(8,128)} custom-call(f32[256,3072]{1,0:T(8,128)} %shard_map.86.x_ref), custom_call_target="tpu_custom_call" | custom-call | tf_op jit(solution)/shard_map/pallas_call | solution.py:300
  309.5 2.4 fusion
  312.0 2.2 reshape.199.x_ref
  314.2 25.4 %shard_map.88 = bf16[32,96,128]{2,1,0:T(8,128)(2,1)} custom-call(bf16[32,96,128]{2,1,0:T(8,128)(2,1)} %reshape.199.x_ref), custom_call_target="tpu_custom_call" | custom-call | tf_op jit(solution)/shard_map/pallas_call | solution.py:89
  (73 shorter events, 14.1 us)
Async XLA Ops:
  46.3 6.6 %copy-start = (f32[256,3072]{1,0:T(8,128)S(1)}, f32[256,3072]{1,0:T(8,128)}, u32[]{:S(2)}) copy-start(f32[256,3072]{1,0:T(8,128)} %shard_map.74.x_ref) | copy-start | bytes 9437188
  85.8 0.9 copy-start.6
  85.8 0.9 copy-start.4
  85.8 5.3 %copy-start.5 = (f32[1,3072]{1,0:T(1,128)S(1)}, f32[1,3072]{1,0:T(1,128)}, u32[]{:S(2)}) copy-start(f32[1,3072]{1,0:T(1,128)} %param.8) | copy-start | bytes 36868
  86.9 4.1 %collective-permute-start = (bf16[3,2,3072]{2,1,0:T(2,128)(2,1)S(1)}, bf16[3,2,3072]{2,1,0:T(2,128)(2,1)S(1)}, u32[]{:S(2)}, u32[]{:S(2)}) collective-permute-start(bf16[3,2,3072]{2,1,0:T(2,128)(2,1)S(1)} %fusion.7), channel_id=1, source_target_pairs={{0,64},{64,128},{128,192},{1,65},{65,129},{129,193},{2,66},{66,130... | collective-permute-start | bytes 110600 | tf_op jit(solution)/shard_map/ppermute | solution.py:17
  132.1 6.6 %copy-start.1 = (f32[256,3072]{1,0:T(8,128)S(1)}, f32[256,3072]{1,0:T(8,128)}, u32[]{:S(2)}) copy-start(f32[256,3072]{1,0:T(8,128)} %shard_map.78.x_ref) | copy-start | bytes 9437188
  169.5 5.2 %collective-permute-start.1 = (bf16[3,2,3072]{2,1,0:T(2,128)(2,1)S(1)}, bf16[3,2,3072]{2,1,0:T(2,128)(2,1)S(1)}, u32[]{:S(2)}, u32[]{:S(2)}) collective-permute-start(bf16[3,2,3072]{2,1,0:T(2,128)(2,1)S(1)} %fusion.11), channel_id=1, source_target_pairs={{0,64},{64,128},{128,192},{1,65},{65,129},{129,193},{2,66},{66,130... | collective-permute-start | bytes 110600 | tf_op jit(solution)/shard_map/ppermute | solution.py:17
  217.2 6.6 %copy-start.2 = (f32[256,3072]{1,0:T(8,128)S(1)}, f32[256,3072]{1,0:T(8,128)}, u32[]{:S(2)}) copy-start(f32[256,3072]{1,0:T(8,128)} %shard_map.82.x_ref) | copy-start | bytes 9437188
  255.3 4.8 %collective-permute-start.2 = (bf16[3,2,3072]{2,1,0:T(2,128)(2,1)S(1)}, bf16[3,2,3072]{2,1,0:T(2,128)(2,1)S(1)}, u32[]{:S(2)}, u32[]{:S(2)}) collective-permute-start(bf16[3,2,3072]{2,1,0:T(2,128)(2,1)S(1)} %fusion.15), channel_id=1, source_target_pairs={{0,64},{64,128},{128,192},{1,65},{65,129},{129,193},{2,66},{66,130... | collective-permute-start | bytes 110600 | tf_op jit(solution)/shard_map/ppermute | solution.py:17
  302.9 6.6 %copy-start.3 = (f32[256,3072]{1,0:T(8,128)S(1)}, f32[256,3072]{1,0:T(8,128)}, u32[]{:S(2)}) copy-start(f32[256,3072]{1,0:T(8,128)} %shard_map.86.x_ref) | copy-start | bytes 9437188

commit v11 on v10

--- a/solution.py
+++ b/solution.py
@@ -205,28 +205,40 @@
     )(pieces)
 
 
-def expert_kernel(x_ref, gate_ref, up_ref, down_ref, o_ref):
+def expert_kernel(x_ref, gate_ref, up_ref, down_ref, own_ref, other_ref, acc_ref):
+    step, last = pl.program_id(0), pl.num_programs(0) - 1
     rows = x_ref[...]
     gate_val = jnp.dot(rows, gate_ref[...], preferred_element_type=jnp.float32)
     up_val = jnp.dot(rows, up_ref[...], preferred_element_type=jnp.float32)
     hidden = (gate_val / (1.0 + jnp.exp(-gate_val)) * up_val).astype(jnp.bfloat16)
     term = jnp.dot(hidden, down_ref[...], preferred_element_type=jnp.float32)
-
-    @pl.when(pl.program_id(0) == 0)
+    half = own_ref.shape[0]
+
+    @pl.when(step == 0)
     def _():
-        o_ref[...] = term
-
-    @pl.when(pl.program_id(0) > 0)
+        acc_ref[...] = term
+
+    @pl.when((step > 0) & (step < last))
     def _():
-        o_ref[...] += term
+        acc_ref[...] += term
+
+    @pl.when(step == last)
+    def _():
+        total = acc_ref[...] + term
+        own_ref[...] = total[:half]
+        other_ref[...] = total[half:].astype(other_ref.dtype)
 
 
 def expert(rows, gate_part, up_part, down_part, chunk=256):
     count, width = rows.shape
     hidden = gate_part.shape[1]
+    half = count // 2
     return pl.pallas_call(
         expert_kernel,
-        out_shape=jax.ShapeDtypeStruct((count, width), jnp.float32),
+        out_shape=(
+            jax.ShapeDtypeStruct((half, width), jnp.float32),
+            jax.ShapeDtypeStruct((half, width), jnp.bfloat16),
+        ),
         grid=(hidden // chunk,),
         in_specs=[
             pl.BlockSpec((count, width), lambda k: (0, 0)),
@@ -234,12 +246,16 @@
             pl.BlockSpec((width, chunk), lambda k: (0, k)),
             pl.BlockSpec((chunk, width), lambda k: (k, 0)),
         ],
-        out_specs=pl.BlockSpec((count, width), lambda k: (0, 0)),
+        out_specs=(
+            pl.BlockSpec((half, width), lambda k: (0, 0)),
+            pl.BlockSpec((half, width), lambda k: (0, 0)),
+        ),
+        scratch_shapes=[pltpu.VMEM((count, width), jnp.float32)],
         compiler_params=pltpu.CompilerParams(dimension_semantics=("arbitrary",)),
         cost_estimate=pl.CostEstimate(
             flops=6 * count * width * hidden,
             transcendentals=count * hidden,
-            bytes_accessed=2 * (count * width + 3 * width * hidden) + 4 * count * width,
+            bytes_accessed=2 * (count * width + 3 * width * hidden) + 3 * half * width * 2,
         ),
     )(rows, gate_part, up_part, down_part)
 
@@ -283,9 +299,8 @@
 
 def pair_send_kernel(x_ref, o_ref, send_sem, recv_sem):
     partner = pair_barrier()
-    rows = o_ref.shape[0]
     copy = pltpu.make_async_remote_copy(
-        src_ref=x_ref.at[pl.ds(rows, rows)],
+        src_ref=x_ref,
         dst_ref=o_ref,
         send_sem=send_sem,
         recv_sem=recv_sem,
@@ -299,7 +314,7 @@
 def pair_send(value, collective):
     return pl.pallas_call(
         pair_send_kernel,
-        out_shape=jax.ShapeDtypeStruct((value.shape[0] // 2, value.shape[1]), value.dtype),
+        out_shape=jax.ShapeDtypeStruct(value.shape, value.dtype),
         in_specs=[pl.BlockSpec(memory_space=pltpu.VMEM)],
         out_specs=pl.BlockSpec(memory_space=pltpu.VMEM),
         scratch_shapes=[pltpu.SemaphoreType.DMA(()), pltpu.SemaphoreType.DMA(())],
@@ -331,9 +346,8 @@
         normed = normalize(carried, row_gain)
         pieces = jnp.stack([normed[0:2], normed[1:3]]).reshape(2, piece_rows, LANES)
         block_rows = ring_gather(pieces, ring_y, ring_z, 0).reshape(shard_count * 2 * local_rows, width)
-        partial_sum = expert(block_rows, gate_part, up_part, down_part)
-        half = partial_sum.shape[0] // 2
-        chip_sum = (partial_sum[:half] + pair_send(partial_sum, 2)).astype(jnp.bfloat16)
+        own_rows, other_rows = expert(block_rows, gate_part, up_part, down_part)
+        chip_sum = (own_rows + pair_send(other_rows, 2).astype(jnp.float32)).astype(jnp.bfloat16)
         received = chip_exchange(chip_sum.reshape(chips, piece_rows, LANES), ring_y, ring_z, 0, 3)
         received = received.astype(jnp.float32)
         received = received.reshape(2, chips // 2, 2, local_rows, width)

time: 346 us -> 327 us (0.945)
  Pallas kernels: 281 us -> 273 us
  other arithmetic: 21.6 us -> 17 us
  local copies, waits for them, and re-layouts: 24.3 us -> 20.5 us
    pallas_call x8, Pallas kernels: 60.2 us -> 50.4 us  [the longest x4 32.7 us: expert(): pl.pallas_call(expert_kernel, out_shape=(jax.ShapeDtypeStruct((half, widt...]
    convert_element_type x4, other arithmetic: 9.75 us -> 5.14 us  [shards(): (own_rows + pair_send(other_rows, 2).astype(jnp.float32)).astype(jnp.bflo...]
    reshape x4, local copies, waits for them, and re-layouts: 8.83 us -> 4.94 us  [shards(): chip_sum.reshape(chips, piece_rows, LANES)]
where the time goes in v11:
time: 327 us; the launch traced here: 326 us
  Pallas kernels  273 us (83%)
  local copies, waits for them, and re-layouts  20.5 us (6%)
  other arithmetic  17 us (5%)
  starting transfers between devices  11.1 us (3%)
    pallas_call x4, Pallas kernels, ring_gather(): pl.pallas_call(functools.partial(ring_gather_kernel, ring_y, ring_z), out...  117 us
    pallas_call x4, Pallas kernels, chip_exchange(): pl.pallas_call(functools.partial(chip_exchange_kernel, ring_y, ring_z, pe...  106 us
    pallas_call x4, Pallas kernels, expert(): pl.pallas_call(expert_kernel, out_shape=(jax.ShapeDtypeStruct((half, widt...  32.7 us
    pallas_call x4, Pallas kernels, pair_send(): pl.pallas_call(pair_send_kernel, out_shape=jax.ShapeDtypeStruct(value.sha...  17.7 us
    reshape x4, local copies, waits for them, and re-layouts, shards(): ring_gather(pieces, ring_y, ring_z, 0)  14.9 us
    ppermute x3, starting transfers between devices, shifted(): lax.ppermute(value, axis, [(source, source + steps) for source in range(i...  11.1 us
  transfers between devices with their start and end apart: 3, of which 3 were waited for; matrix products, arithmetic and copies ran while one was open for 0% of the time, Pallas kernels for 0%

profile of v11, /device:TPU:1, one launch (start us, length us, event | category | flops | bytes accessed | tf_op | source)
XLA Modules:
  0.0 325.8 jit_solution(613714693539032326)
XLA Ops:
  2.5 31.7 %shard_map.73 = bf16[2,8,4,96,128]{4,3,2,1,0:T(8,128)(2,1)} custom-call(bf16[2,96,128]{2,1,0:T(8,128)(2,1)} %pad_maximum_fusion.x_ref), custom_call_target="tpu_custom_call" | custom-call | tf_op jit(solution)/shard_map/pallas_call | solution.py:190
  34.2 3.7 %reshape.192.x_ref = bf16[256,3072]{1,0:T(8,128)(2,1)} reshape(bf16[2,8,4,96,128]{4,3,2,1,0:T(8,128)(2,1)} %shard_map.73) | data formatting | bytes 3145728 | tf_op jit(solution)/shard_map/reshape | solution.py:348
  37.9 8.2 %shard_map.74 = (f32[128,3072]{1,0:T(8,128)}, bf16[128,3072]{1,0:T(8,128)(2,1)}) custom-call(bf16[256,3072]{1,0:T(8,128)(2,1)} %reshape.192.x_ref, bf16[3072,512]{1,0:T(8,128)(2,1)} %bitcast.16, bf16[3072,512]{1,0:T(8,128)(2,1)} %bitcast.20, bf16[512,3072]{1,0:T(8,128)(2,1)} %bitcast.24), custom_call_target="tpu_custom_call" | custom-call | flops 2415919104 | bytes 13369344 | tf_op jit(solution)/shard_map/pallas_call | solution.py:236
  46.1 4.4 %shard_map.75 = bf16[128,3072]{1,0:T(8,128)(2,1)} custom-call(bf16[128,3072]{1,0:T(8,128)(2,1)} %get-tuple-element.14.x_ref), custom_call_target="tpu_custom_call" | custom-call | tf_op jit(solution)/shard_map/pallas_call | solution.py:315
  50.5 1.3 add_convert_fusion.3
  51.8 1.2 reshape.193.x_ref
  53.1 26.8 %shard_map.76 = bf16[32,96,128]{2,1,0:T(8,128)(2,1)} custom-call(bf16[32,96,128]{2,1,0:T(8,128)(2,1)} %reshape.193.x_ref), custom_call_target="tpu_custom_call" | custom-call | tf_op jit(solution)/shard_map/pallas_call | solution.py:89
  79.9 1.3 convert_element_type.80
  82.3 3.2 collective-permute-start
  87.5 27.9 %shard_map.77 = bf16[2,8,4,96,128]{4,3,2,1,0:T(8,128)(2,1)} custom-call(bf16[2,96,128]{2,1,0:T(8,128)(2,1)} %pad_maximum_fusion.1.x_ref), custom_call_target="tpu_custom_call" | custom-call | tf_op jit(solution)/shard_map/pallas_call | solution.py:190
  115.4 3.7 %reshape.194.x_ref = bf16[256,3072]{1,0:T(8,128)(2,1)} reshape(bf16[2,8,4,96,128]{4,3,2,1,0:T(8,128)(2,1)} %shard_map.77) | data formatting | bytes 3145728 | tf_op jit(solution)/shard_map/reshape | solution.py:348
  119.2 8.2 %shard_map.78 = (f32[128,3072]{1,0:T(8,128)}, bf16[128,3072]{1,0:T(8,128)(2,1)}) custom-call(bf16[256,3072]{1,0:T(8,128)(2,1)} %reshape.194.x_ref, bf16[3072,512]{1,0:T(8,128)(2,1)} %bitcast.17, bf16[3072,512]{1,0:T(8,128)(2,1)} %bitcast.21, bf16[512,3072]{1,0:T(8,128)(2,1)} %bitcast.25), custom_call_target="tpu_custom_call" | custom-call | flops 2415919104 | bytes 13369344 | tf_op jit(solution)/shard_map/pallas_call | solution.py:236
  127.3 4.4 %shard_map.79 = bf16[128,3072]{1,0:T(8,128)(2,1)} custom-call(bf16[128,3072]{1,0:T(8,128)(2,1)} %get-tuple-element.16.x_ref), custom_call_target="tpu_custom_call" | custom-call | tf_op jit(solution)/shard_map/pallas_call | solution.py:315
  131.8 1.3 add_convert_fusion.2
  134.3 24.6 %shard_map.80 = bf16[32,96,128]{2,1,0:T(8,128)(2,1)} custom-call(bf16[32,96,128]{2,1,0:T(8,128)(2,1)} %reshape.195.x_ref), custom_call_target="tpu_custom_call" | custom-call | tf_op jit(solution)/shard_map/pallas_call | solution.py:89
  159.0 1.3 convert_element_type.86
  160.6 4.3 %collective-permute-start.1 = (bf16[3,2,3072]{2,1,0:T(2,128)(2,1)S(1)}, bf16[3,2,3072]{2,1,0:T(2,128)(2,1)S(1)}, u32[]{:S(2)}, u32[]{:S(2)}) collective-permute-start(bf16[3,2,3072]{2,1,0:T(2,128)(2,1)S(1)} %fusion.7), channel_id=1, source_target_pairs={{0,64},{64,128},{128,192},{1,65},{65,129},{129,193},{2,66},{66,130... | collective-permute-start | bytes 110600 | tf_op jit(solution)/shard_map/ppermute | solution.py:17
  166.7 29.2 %shard_map.81 = bf16[2,8,4,96,128]{4,3,2,1,0:T(8,128)(2,1)} custom-call(bf16[2,96,128]{2,1,0:T(8,128)(2,1)} %pad_maximum_fusion.2.x_ref), custom_call_target="tpu_custom_call" | custom-call | tf_op jit(solution)/shard_map/pallas_call | solution.py:190
  195.9 3.7 %reshape.196.x_ref = bf16[256,3072]{1,0:T(8,128)(2,1)} reshape(bf16[2,8,4,96,128]{4,3,2,1,0:T(8,128)(2,1)} %shard_map.81) | data formatting | bytes 3145728 | tf_op jit(solution)/shard_map/reshape | solution.py:348
  199.7 8.2 %shard_map.82 = (f32[128,3072]{1,0:T(8,128)}, bf16[128,3072]{1,0:T(8,128)(2,1)}) custom-call(bf16[256,3072]{1,0:T(8,128)(2,1)} %reshape.196.x_ref, bf16[3072,512]{1,0:T(8,128)(2,1)} %bitcast.18, bf16[3072,512]{1,0:T(8,128)(2,1)} %bitcast.22, bf16[512,3072]{1,0:T(8,128)(2,1)} %bitcast.26), custom_call_target="tpu_custom_call" | custom-call | flops 2415919104 | bytes 13369344 | tf_op jit(solution)/shard_map/pallas_call | solution.py:236
  207.8 4.4 %shard_map.83 = bf16[128,3072]{1,0:T(8,128)(2,1)} custom-call(bf16[128,3072]{1,0:T(8,128)(2,1)} %get-tuple-element.18.x_ref), custom_call_target="tpu_custom_call" | custom-call | tf_op jit(solution)/shard_map/pallas_call | solution.py:315
  212.3 1.3 add_convert_fusion.1
  214.8 25.6 %shard_map.84 = bf16[32,96,128]{2,1,0:T(8,128)(2,1)} custom-call(bf16[32,96,128]{2,1,0:T(8,128)(2,1)} %reshape.197.x_ref), custom_call_target="tpu_custom_call" | custom-call | tf_op jit(solution)/shard_map/pallas_call | solution.py:89
  240.4 1.3 convert_element_type.92
  242.0 3.6 %collective-permute-start.2 = (bf16[3,2,3072]{2,1,0:T(2,128)(2,1)S(1)}, bf16[3,2,3072]{2,1,0:T(2,128)(2,1)S(1)}, u32[]{:S(2)}, u32[]{:S(2)}) collective-permute-start(bf16[3,2,3072]{2,1,0:T(2,128)(2,1)S(1)} %fusion.11), channel_id=1, source_target_pairs={{0,64},{64,128},{128,192},{1,65},{65,129},{129,193},{2,66},{66,130... | collective-permute-start | bytes 110600 | tf_op jit(solution)/shard_map/ppermute | solution.py:17
  247.6 28.4 %shard_map.85 = bf16[2,8,4,96,128]{4,3,2,1,0:T(8,128)(2,1)} custom-call(bf16[2,96,128]{2,1,0:T(8,128)(2,1)} %pad_maximum_fusion.3.x_ref), custom_call_target="tpu_custom_call" | custom-call | tf_op jit(solution)/shard_map/pallas_call | solution.py:190
  276.0 3.7 %reshape.198.x_ref = bf16[256,3072]{1,0:T(8,128)(2,1)} reshape(bf16[2,8,4,96,128]{4,3,2,1,0:T(8,128)(2,1)} %shard_map.85) | data formatting | bytes 3145728 | tf_op jit(solution)/shard_map/reshape | solution.py:348
  279.8 8.2 %shard_map.86 = (f32[128,3072]{1,0:T(8,128)}, bf16[128,3072]{1,0:T(8,128)(2,1)}) custom-call(bf16[256,3072]{1,0:T(8,128)(2,1)} %reshape.198.x_ref, bf16[3072,512]{1,0:T(8,128)(2,1)} %bitcast.19, bf16[3072,512]{1,0:T(8,128)(2,1)} %bitcast.23, bf16[512,3072]{1,0:T(8,128)(2,1)} %bitcast.27), custom_call_target="tpu_custom_call" | custom-call | flops 2415919104 | bytes 13369344 | tf_op jit(solution)/shard_map/pallas_call | solution.py:236
  287.9 4.4 %shard_map.87 = bf16[128,3072]{1,0:T(8,128)(2,1)} custom-call(bf16[128,3072]{1,0:T(8,128)(2,1)} %get-tuple-element.20.x_ref), custom_call_target="tpu_custom_call" | custom-call | tf_op jit(solution)/shard_map/pallas_call | solution.py:315
  292.4 1.3 add_convert_fusion
  294.9 28.5 %shard_map.88 = bf16[32,96,128]{2,1,0:T(8,128)(2,1)} custom-call(bf16[32,96,128]{2,1,0:T(8,128)(2,1)} %reshape.199.x_ref), custom_call_target="tpu_custom_call" | custom-call | tf_op jit(solution)/shard_map/pallas_call | solution.py:89
  323.4 1.3 convert_element_type.98
  (73 shorter events, 13.9 us)
Async XLA Ops:
  46.1 4.4 %copy-start = (f32[128,3072]{1,0:T(8,128)S(1)}, f32[128,3072]{1,0:T(8,128)}, u32[]{:S(2)}) copy-start(f32[128,3072]{1,0:T(8,128)} %get-tuple-element.13) | copy-start | bytes 4718596
  81.2 0.9 copy-start.6
  81.2 0.9 copy-start.4
  81.2 5.4 %copy-start.5 = (f32[1,3072]{1,0:T(1,128)S(1)}, f32[1,3072]{1,0:T(1,128)}, u32[]{:S(2)}) copy-start(f32[1,3072]{1,0:T(1,128)} %param.8) | copy-start | bytes 36868
  82.3 4.2 %collective-permute-start = (bf16[3,2,3072]{2,1,0:T(2,128)(2,1)S(1)}, bf16[3,2,3072]{2,1,0:T(2,128)(2,1)S(1)}, u32[]{:S(2)}, u32[]{:S(2)}) collective-permute-start(bf16[3,2,3072]{2,1,0:T(2,128)(2,1)S(1)} %fusion.3), channel_id=1, source_target_pairs={{0,64},{64,128},{128,192},{1,65},{65,129},{129,193},{2,66},{66,130... | collective-permute-start | bytes 110600 | tf_op jit(solution)/shard_map/ppermute | solution.py:17
  127.3 4.4 %copy-start.1 = (f32[128,3072]{1,0:T(8,128)S(1)}, f32[128,3072]{1,0:T(8,128)}, u32[]{:S(2)}) copy-start(f32[128,3072]{1,0:T(8,128)} %get-tuple-element.15) | copy-start | bytes 4718596
  160.6 5.2 %collective-permute-start.1 = (bf16[3,2,3072]{2,1,0:T(2,128)(2,1)S(1)}, bf16[3,2,3072]{2,1,0:T(2,128)(2,1)S(1)}, u32[]{:S(2)}, u32[]{:S(2)}) collective-permute-start(bf16[3,2,3072]{2,1,0:T(2,128)(2,1)S(1)} %fusion.7), channel_id=1, source_target_pairs={{0,64},{64,128},{128,192},{1,65},{65,129},{129,193},{2,66},{66,130... | collective-permute-start | bytes 110600 | tf_op jit(solution)/shard_map/ppermute | solution.py:17
  207.8 4.4 %copy-start.2 = (f32[128,3072]{1,0:T(8,128)S(1)}, f32[128,3072]{1,0:T(8,128)}, u32[]{:S(2)}) copy-start(f32[128,3072]{1,0:T(8,128)} %get-tuple-element.17) | copy-start | bytes 4718596
  242.0 4.6 %collective-permute-start.2 = (bf16[3,2,3072]{2,1,0:T(2,128)(2,1)S(1)}, bf16[3,2,3072]{2,1,0:T(2,128)(2,1)S(1)}, u32[]{:S(2)}, u32[]{:S(2)}) collective-permute-start(bf16[3,2,3072]{2,1,0:T(2,128)(2,1)S(1)} %fusion.11), channel_id=1, source_target_pairs={{0,64},{64,128},{128,192},{1,65},{65,129},{129,193},{2,66},{66,130... | collective-permute-start | bytes 110600 | tf_op jit(solution)/shard_map/ppermute | solution.py:17
  287.9 4.4 %copy-start.3 = (f32[128,3072]{1,0:T(8,128)S(1)}, f32[128,3072]{1,0:T(8,128)}, u32[]{:S(2)}) copy-start(f32[128,3072]{1,0:T(8,128)} %get-tuple-element.19) | copy-start | bytes 4718596

commit v12 on v11

--- a/solution.py
+++ b/solution.py
@@ -68,7 +68,7 @@
     pl.semaphore_wait(barrier, chips - 1)
 
     def start(step, carry):
-        copy_of(peer(step, 1), chip).start()
+        copy_of(peer(chips - step, 1), chip).start()
         return carry
 
     lax.fori_loop(1, chips, start, 0)

time: 327 us -> 328 us (level)
  no operation moved by 1% of the time
where the time goes in v12:
time: 328 us; the launch traced here: 326 us
  Pallas kernels  273 us (83%)
  local copies, waits for them, and re-layouts  20.5 us (6%)
  other arithmetic  17 us (5%)
  starting transfers between devices  11.2 us (3%)
    pallas_call x4, Pallas kernels, ring_gather(): pl.pallas_call(functools.partial(ring_gather_kernel, ring_y, ring_z), out...  115 us
    pallas_call x4, Pallas kernels, chip_exchange(): pl.pallas_call(functools.partial(chip_exchange_kernel, ring_y, ring_z, pe...  108 us
    pallas_call x4, Pallas kernels, expert(): pl.pallas_call(expert_kernel, out_shape=(jax.ShapeDtypeStruct((half, widt...  32.7 us
    pallas_call x4, Pallas kernels, pair_send(): pl.pallas_call(pair_send_kernel, out_shape=jax.ShapeDtypeStruct(value.sha...  17.7 us
    reshape x4, local copies, waits for them, and re-layouts, shards(): ring_gather(pieces, ring_y, ring_z, 0)  14.9 us
    ppermute x3, starting transfers between devices, shifted(): lax.ppermute(value, axis, [(source, source + steps) for source in range(i...  11.2 us
  transfers between devices with their start and end apart: 3, of which 3 were waited for; matrix products, arithmetic and copies ran while one was open for 0% of the time, Pallas kernels for 0%

profile of v12, /device:TPU:1, one launch (start us, length us, event | category | flops | bytes accessed | tf_op | source)
XLA Modules:
  0.0 325.9 jit_solution(11107444459895706349)
XLA Ops:
  2.5 31.7 %shard_map.73 = bf16[2,8,4,96,128]{4,3,2,1,0:T(8,128)(2,1)} custom-call(bf16[2,96,128]{2,1,0:T(8,128)(2,1)} %pad_maximum_fusion.x_ref), custom_call_target="tpu_custom_call" | custom-call | tf_op jit(solution)/shard_map/pallas_call | solution.py:190
  34.2 3.7 %reshape.192.x_ref = bf16[256,3072]{1,0:T(8,128)(2,1)} reshape(bf16[2,8,4,96,128]{4,3,2,1,0:T(8,128)(2,1)} %shard_map.73) | data formatting | bytes 3145728 | tf_op jit(solution)/shard_map/reshape | solution.py:348
  37.9 8.2 %shard_map.74 = (f32[128,3072]{1,0:T(8,128)}, bf16[128,3072]{1,0:T(8,128)(2,1)}) custom-call(bf16[256,3072]{1,0:T(8,128)(2,1)} %reshape.192.x_ref, bf16[3072,512]{1,0:T(8,128)(2,1)} %bitcast.16, bf16[3072,512]{1,0:T(8,128)(2,1)} %bitcast.20, bf16[512,3072]{1,0:T(8,128)(2,1)} %bitcast.24), custom_call_target="tpu_custom_call" | custom-call | flops 2415919104 | bytes 13369344 | tf_op jit(solution)/shard_map/pallas_call | solution.py:236
  46.1 4.4 %shard_map.75 = bf16[128,3072]{1,0:T(8,128)(2,1)} custom-call(bf16[128,3072]{1,0:T(8,128)(2,1)} %get-tuple-element.14.x_ref), custom_call_target="tpu_custom_call" | custom-call | tf_op jit(solution)/shard_map/pallas_call | solution.py:315
  50.5 1.3 add_convert_fusion.3
  51.8 1.2 reshape.193.x_ref
  53.1 27.1 %shard_map.76 = bf16[32,96,128]{2,1,0:T(8,128)(2,1)} custom-call(bf16[32,96,128]{2,1,0:T(8,128)(2,1)} %reshape.193.x_ref), custom_call_target="tpu_custom_call" | custom-call | tf_op jit(solution)/shard_map/pallas_call | solution.py:89
  80.1 1.3 convert_element_type.80
  82.5 3.2 collective-permute-start
  87.7 27.8 %shard_map.77 = bf16[2,8,4,96,128]{4,3,2,1,0:T(8,128)(2,1)} custom-call(bf16[2,96,128]{2,1,0:T(8,128)(2,1)} %pad_maximum_fusion.1.x_ref), custom_call_target="tpu_custom_call" | custom-call | tf_op jit(solution)/shard_map/pallas_call | solution.py:190
  115.5 3.7 %reshape.194.x_ref = bf16[256,3072]{1,0:T(8,128)(2,1)} reshape(bf16[2,8,4,96,128]{4,3,2,1,0:T(8,128)(2,1)} %shard_map.77) | data formatting | bytes 3145728 | tf_op jit(solution)/shard_map/reshape | solution.py:348
  119.3 8.2 %shard_map.78 = (f32[128,3072]{1,0:T(8,128)}, bf16[128,3072]{1,0:T(8,128)(2,1)}) custom-call(bf16[256,3072]{1,0:T(8,128)(2,1)} %reshape.194.x_ref, bf16[3072,512]{1,0:T(8,128)(2,1)} %bitcast.17, bf16[3072,512]{1,0:T(8,128)(2,1)} %bitcast.21, bf16[512,3072]{1,0:T(8,128)(2,1)} %bitcast.25), custom_call_target="tpu_custom_call" | custom-call | flops 2415919104 | bytes 13369344 | tf_op jit(solution)/shard_map/pallas_call | solution.py:236
  127.4 4.4 %shard_map.79 = bf16[128,3072]{1,0:T(8,128)(2,1)} custom-call(bf16[128,3072]{1,0:T(8,128)(2,1)} %get-tuple-element.16.x_ref), custom_call_target="tpu_custom_call" | custom-call | tf_op jit(solution)/shard_map/pallas_call | solution.py:315
  131.9 1.3 add_convert_fusion.2
  134.4 26.4 %shard_map.80 = bf16[32,96,128]{2,1,0:T(8,128)(2,1)} custom-call(bf16[32,96,128]{2,1,0:T(8,128)(2,1)} %reshape.195.x_ref), custom_call_target="tpu_custom_call" | custom-call | tf_op jit(solution)/shard_map/pallas_call | solution.py:89
  160.8 1.3 convert_element_type.86
  162.4 4.2 %collective-permute-start.1 = (bf16[3,2,3072]{2,1,0:T(2,128)(2,1)S(1)}, bf16[3,2,3072]{2,1,0:T(2,128)(2,1)S(1)}, u32[]{:S(2)}, u32[]{:S(2)}) collective-permute-start(bf16[3,2,3072]{2,1,0:T(2,128)(2,1)S(1)} %fusion.7), channel_id=1, source_target_pairs={{0,64},{64,128},{128,192},{1,65},{65,129},{129,193},{2,66},{66,130... | collective-permute-start | bytes 110600 | tf_op jit(solution)/shard_map/ppermute | solution.py:17
  168.4 28.3 %shard_map.81 = bf16[2,8,4,96,128]{4,3,2,1,0:T(8,128)(2,1)} custom-call(bf16[2,96,128]{2,1,0:T(8,128)(2,1)} %pad_maximum_fusion.2.x_ref), custom_call_target="tpu_custom_call" | custom-call | tf_op jit(solution)/shard_map/pallas_call | solution.py:190
  196.7 3.7 %reshape.196.x_ref = bf16[256,3072]{1,0:T(8,128)(2,1)} reshape(bf16[2,8,4,96,128]{4,3,2,1,0:T(8,128)(2,1)} %shard_map.81) | data formatting | bytes 3145728 | tf_op jit(solution)/shard_map/reshape | solution.py:348
  200.5 8.2 %shard_map.82 = (f32[128,3072]{1,0:T(8,128)}, bf16[128,3072]{1,0:T(8,128)(2,1)}) custom-call(bf16[256,3072]{1,0:T(8,128)(2,1)} %reshape.196.x_ref, bf16[3072,512]{1,0:T(8,128)(2,1)} %bitcast.18, bf16[3072,512]{1,0:T(8,128)(2,1)} %bitcast.22, bf16[512,3072]{1,0:T(8,128)(2,1)} %bitcast.26), custom_call_target="tpu_custom_call" | custom-call | flops 2415919104 | bytes 13369344 | tf_op jit(solution)/shard_map/pallas_call | solution.py:236
  208.7 4.4 %shard_map.83 = bf16[128,3072]{1,0:T(8,128)(2,1)} custom-call(bf16[128,3072]{1,0:T(8,128)(2,1)} %get-tuple-element.18.x_ref), custom_call_target="tpu_custom_call" | custom-call | tf_op jit(solution)/shard_map/pallas_call | solution.py:315
  213.1 1.3 add_convert_fusion.1
  215.6 28.0 %shard_map.84 = bf16[32,96,128]{2,1,0:T(8,128)(2,1)} custom-call(bf16[32,96,128]{2,1,0:T(8,128)(2,1)} %reshape.197.x_ref), custom_call_target="tpu_custom_call" | custom-call | tf_op jit(solution)/shard_map/pallas_call | solution.py:89
  243.6 1.3 convert_element_type.92
  245.2 3.8 %collective-permute-start.2 = (bf16[3,2,3072]{2,1,0:T(2,128)(2,1)S(1)}, bf16[3,2,3072]{2,1,0:T(2,128)(2,1)S(1)}, u32[]{:S(2)}, u32[]{:S(2)}) collective-permute-start(bf16[3,2,3072]{2,1,0:T(2,128)(2,1)S(1)} %fusion.11), channel_id=1, source_target_pairs={{0,64},{64,128},{128,192},{1,65},{65,129},{129,193},{2,66},{66,130... | collective-permute-start | bytes 110600 | tf_op jit(solution)/shard_map/ppermute | solution.py:17
  251.1 27.1 %shard_map.85 = bf16[2,8,4,96,128]{4,3,2,1,0:T(8,128)(2,1)} custom-call(bf16[2,96,128]{2,1,0:T(8,128)(2,1)} %pad_maximum_fusion.3.x_ref), custom_call_target="tpu_custom_call" | custom-call | tf_op jit(solution)/shard_map/pallas_call | solution.py:190
  278.2 3.7 %reshape.198.x_ref = bf16[256,3072]{1,0:T(8,128)(2,1)} reshape(bf16[2,8,4,96,128]{4,3,2,1,0:T(8,128)(2,1)} %shard_map.85) | data formatting | bytes 3145728 | tf_op jit(solution)/shard_map/reshape | solution.py:348
  282.0 8.2 %shard_map.86 = (f32[128,3072]{1,0:T(8,128)}, bf16[128,3072]{1,0:T(8,128)(2,1)}) custom-call(bf16[256,3072]{1,0:T(8,128)(2,1)} %reshape.198.x_ref, bf16[3072,512]{1,0:T(8,128)(2,1)} %bitcast.19, bf16[3072,512]{1,0:T(8,128)(2,1)} %bitcast.23, bf16[512,3072]{1,0:T(8,128)(2,1)} %bitcast.27), custom_call_target="tpu_custom_call" | custom-call | flops 2415919104 | bytes 13369344 | tf_op jit(solution)/shard_map/pallas_call | solution.py:236
  290.2 4.4 %shard_map.87 = bf16[128,3072]{1,0:T(8,128)(2,1)} custom-call(bf16[128,3072]{1,0:T(8,128)(2,1)} %get-tuple-element.20.x_ref), custom_call_target="tpu_custom_call" | custom-call | tf_op jit(solution)/shard_map/pallas_call | solution.py:315
  294.6 1.3 add_convert_fusion
  297.1 26.3 %shard_map.88 = bf16[32,96,128]{2,1,0:T(8,128)(2,1)} custom-call(bf16[32,96,128]{2,1,0:T(8,128)(2,1)} %reshape.199.x_ref), custom_call_target="tpu_custom_call" | custom-call | tf_op jit(solution)/shard_map/pallas_call | solution.py:89
  323.5 1.3 convert_element_type.98
  (73 shorter events, 13.9 us)
Async XLA Ops:
  46.1 4.4 %copy-start = (f32[128,3072]{1,0:T(8,128)S(1)}, f32[128,3072]{1,0:T(8,128)}, u32[]{:S(2)}) copy-start(f32[128,3072]{1,0:T(8,128)} %get-tuple-element.13) | copy-start | bytes 4718596
  81.5 0.9 copy-start.6
  81.5 0.9 copy-start.4
  81.5 5.4 %copy-start.5 = (f32[1,3072]{1,0:T(1,128)S(1)}, f32[1,3072]{1,0:T(1,128)}, u32[]{:S(2)}) copy-start(f32[1,3072]{1,0:T(1,128)} %param.8) | copy-start | bytes 36868
  82.5 4.2 %collective-permute-start = (bf16[3,2,3072]{2,1,0:T(2,128)(2,1)S(1)}, bf16[3,2,3072]{2,1,0:T(2,128)(2,1)S(1)}, u32[]{:S(2)}, u32[]{:S(2)}) collective-permute-start(bf16[3,2,3072]{2,1,0:T(2,128)(2,1)S(1)} %fusion.3), channel_id=1, source_target_pairs={{0,64},{64,128},{128,192},{1,65},{65,129},{129,193},{2,66},{66,130... | collective-permute-start | bytes 110600 | tf_op jit(solution)/shard_map/ppermute | solution.py:17
  127.4 4.4 %copy-start.1 = (f32[128,3072]{1,0:T(8,128)S(1)}, f32[128,3072]{1,0:T(8,128)}, u32[]{:S(2)}) copy-start(f32[128,3072]{1,0:T(8,128)} %get-tuple-element.15) | copy-start | bytes 4718596
  162.4 5.1 %collective-permute-start.1 = (bf16[3,2,3072]{2,1,0:T(2,128)(2,1)S(1)}, bf16[3,2,3072]{2,1,0:T(2,128)(2,1)S(1)}, u32[]{:S(2)}, u32[]{:S(2)}) collective-permute-start(bf16[3,2,3072]{2,1,0:T(2,128)(2,1)S(1)} %fusion.7), channel_id=1, source_target_pairs={{0,64},{64,128},{128,192},{1,65},{65,129},{129,193},{2,66},{66,130... | collective-permute-start | bytes 110600 | tf_op jit(solution)/shard_map/ppermute | solution.py:17
  208.7 4.4 %copy-start.2 = (f32[128,3072]{1,0:T(8,128)S(1)}, f32[128,3072]{1,0:T(8,128)}, u32[]{:S(2)}) copy-start(f32[128,3072]{1,0:T(8,128)} %get-tuple-element.17) | copy-start | bytes 4718596
  245.2 4.9 %collective-permute-start.2 = (bf16[3,2,3072]{2,1,0:T(2,128)(2,1)S(1)}, bf16[3,2,3072]{2,1,0:T(2,128)(2,1)S(1)}, u32[]{:S(2)}, u32[]{:S(2)}) collective-permute-start(bf16[3,2,3072]{2,1,0:T(2,128)(2,1)S(1)} %fusion.11), channel_id=1, source_target_pairs={{0,64},{64,128},{128,192},{1,65},{65,129},{129,193},{2,66},{66,130... | collective-permute-start | bytes 110600 | tf_op jit(solution)/shard_map/ppermute | solution.py:17
  290.2 4.4 %copy-start.3 = (f32[128,3072]{1,0:T(8,128)S(1)}, f32[128,3072]{1,0:T(8,128)}, u32[]{:S(2)}) copy-start(f32[128,3072]{1,0:T(8,128)} %get-tuple-element.19) | copy-start | bytes 4718596

commit v13 on v11

--- a/solution.py
+++ b/solution.py
@@ -205,9 +205,14 @@
     )(pieces)
 
 
-def expert_kernel(x_ref, gate_ref, up_ref, down_ref, own_ref, other_ref, acc_ref):
+def expert_kernel(x_ref, gate_ref, up_ref, down_ref, own_ref, other_ref, acc_ref, rows_ref):
     step, last = pl.program_id(0), pl.num_programs(0) - 1
-    rows = x_ref[...]
+
+    @pl.when(step == 0)
+    def _():
+        rows_ref[...] = x_ref[...].reshape(rows_ref.shape)
+
+    rows = rows_ref[...]
     gate_val = jnp.dot(rows, gate_ref[...], preferred_element_type=jnp.float32)
     up_val = jnp.dot(rows, up_ref[...], preferred_element_type=jnp.float32)
     hidden = (gate_val / (1.0 + jnp.exp(-gate_val)) * up_val).astype(jnp.bfloat16)
@@ -230,7 +235,8 @@
 
 
 def expert(rows, gate_part, up_part, down_part, chunk=256):
-    count, width = rows.shape
+    width = gate_part.shape[0]
+    count = rows.size // width
     hidden = gate_part.shape[1]
     half = count // 2
     return pl.pallas_call(
@@ -241,7 +247,7 @@
         ),
         grid=(hidden // chunk,),
         in_specs=[
-            pl.BlockSpec((count, width), lambda k: (0, 0)),
+            pl.BlockSpec(rows.shape, lambda k: (0, 0, 0)),
             pl.BlockSpec((width, chunk), lambda k: (0, k)),
             pl.BlockSpec((width, chunk), lambda k: (0, k)),
             pl.BlockSpec((chunk, width), lambda k: (k, 0)),
@@ -250,7 +256,7 @@
             pl.BlockSpec((half, width), lambda k: (0, 0)),
             pl.BlockSpec((half, width), lambda k: (0, 0)),
         ),
-        scratch_shapes=[pltpu.VMEM((count, width), jnp.float32)],
+        scratch_shapes=[pltpu.VMEM((count, width), jnp.float32), pltpu.VMEM((count, width), rows.dtype)],
         compiler_params=pltpu.CompilerParams(dimension_semantics=("arbitrary",)),
         cost_estimate=pl.CostEstimate(
             flops=6 * count * width * hidden,
@@ -345,7 +351,7 @@
     for tick in range(segment_count):
         normed = normalize(carried, row_gain)
         pieces = jnp.stack([normed[0:2], normed[1:3]]).reshape(2, piece_rows, LANES)
-        block_rows = ring_gather(pieces, ring_y, ring_z, 0).reshape(shard_count * 2 * local_rows, width)
+        block_rows = ring_gather(pieces, ring_y, ring_z, 0).reshape(shard_count, piece_rows, LANES)
         own_rows, other_rows = expert(block_rows, gate_part, up_part, down_part)
         chip_sum = (own_rows + pair_send(other_rows, 2).astype(jnp.float32)).astype(jnp.bfloat16)
         received = chip_exchange(chip_sum.reshape(chips, piece_rows, LANES), ring_y, ring_z, 0, 3)

time: 327 us -> 320 us (0.979)
  local copies, waits for them, and re-layouts: 20.5 us -> 5.6 us
  Pallas kernels: 273 us -> 278 us
    reshape x4 -> x0, local copies, waits for them, and re-layouts: 14.9 us -> none  [shards(): ring_gather(pieces, ring_y, ring_z, 0)]
    pallas_call x4, Pallas kernels: 32.7 us -> 39.6 us  [expert(): pl.pallas_call(expert_kernel, out_shape=(jax.ShapeDtypeStruct((half, widt...]
where the time goes in v13:
time: 320 us; the launch traced here: 316 us
  Pallas kernels  278 us (87%)
  other arithmetic  16.9 us (5%)
  starting transfers between devices  11.4 us (4%)
  local copies, waits for them, and re-layouts  5.6 us (2%)
    pallas_call x4, Pallas kernels, ring_gather(): pl.pallas_call(functools.partial(ring_gather_kernel, ring_y, ring_z), out...  117 us
    pallas_call x4, Pallas kernels, chip_exchange(): pl.pallas_call(functools.partial(chip_exchange_kernel, ring_y, ring_z, pe...  104 us
    pallas_call x4, Pallas kernels, expert(): pl.pallas_call(expert_kernel, out_shape=(jax.ShapeDtypeStruct((half, widt...  39.6 us
    pallas_call x4, Pallas kernels, pair_send(): pl.pallas_call(pair_send_kernel, out_shape=jax.ShapeDtypeStruct(value.sha...  17.7 us
    ppermute x3, starting transfers between devices, shifted(): lax.ppermute(value, axis, [(source, source + steps) for source in range(i...  11.4 us
  transfers between devices with their start and end apart: 3, of which 3 were waited for; matrix products, arithmetic and copies ran while one was open for 0% of the time, Pallas kernels for 0%

profile of v13, /device:TPU:1, one launch (start us, length us, event | category | flops | bytes accessed | tf_op | source)
XLA Modules:
  0.0 315.8 jit_solution(5301863515521738274)
XLA Ops:
  2.5 31.7 %shard_map.73 = bf16[2,8,4,96,128]{4,3,2,1,0:T(8,128)(2,1)} custom-call(bf16[2,96,128]{2,1,0:T(8,128)(2,1)} %pad_maximum_fusion.x_ref), custom_call_target="tpu_custom_call" | custom-call | tf_op jit(solution)/shard_map/pallas_call | solution.py:190
  34.2 9.9 %shard_map.74 = (f32[128,3072]{1,0:T(8,128)}, bf16[128,3072]{1,0:T(8,128)(2,1)}) custom-call(bf16[64,96,128]{2,1,0:T(8,128)(2,1)} %bitcast.24, bf16[3072,512]{1,0:T(8,128)(2,1)} %bitcast.12, bf16[3072,512]{1,0:T(8,128)(2,1)} %bitcast.16, bf16[512,3072]{1,0:T(8,128)(2,1)} %bitcast.20), custom_call_target="tpu_custom_call" | custom-call | flops 2415919104 | bytes 13369344 | tf_op jit(solution)/shard_map/pallas_call | solution.py:242
  44.1 4.4 %shard_map.75 = bf16[128,3072]{1,0:T(8,128)(2,1)} custom-call(bf16[128,3072]{1,0:T(8,128)(2,1)} %get-tuple-element.14.x_ref), custom_call_target="tpu_custom_call" | custom-call | tf_op jit(solution)/shard_map/pallas_call | solution.py:321
  48.5 1.3 add_convert_fusion.3
  49.8 1.2 reshape.193.x_ref
  51.1 26.9 %shard_map.76 = bf16[32,96,128]{2,1,0:T(8,128)(2,1)} custom-call(bf16[32,96,128]{2,1,0:T(8,128)(2,1)} %reshape.193.x_ref), custom_call_target="tpu_custom_call" | custom-call | tf_op jit(solution)/shard_map/pallas_call | solution.py:89
  78.0 1.3 convert_element_type.80
  80.3 3.3 %collective-permute-start = (bf16[3,2,3072]{2,1,0:T(2,128)(2,1)S(1)}, bf16[3,2,3072]{2,1,0:T(2,128)(2,1)S(1)}, u32[]{:S(2)}, u32[]{:S(2)}) collective-permute-start(bf16[3,2,3072]{2,1,0:T(2,128)(2,1)S(1)} %fusion.3), channel_id=1, source_target_pairs={{0,64},{64,128},{128,192},{1,65},{65,129},{129,193},{2,66},{66,130... | collective-permute-start | bytes 110600 | tf_op jit(solution)/shard_map/ppermute | solution.py:17
  85.5 28.0 %shard_map.77 = bf16[2,8,4,96,128]{4,3,2,1,0:T(8,128)(2,1)} custom-call(bf16[2,96,128]{2,1,0:T(8,128)(2,1)} %pad_maximum_fusion.1.x_ref), custom_call_target="tpu_custom_call" | custom-call | tf_op jit(solution)/shard_map/pallas_call | solution.py:190
  113.4 9.9 %shard_map.78 = (f32[128,3072]{1,0:T(8,128)}, bf16[128,3072]{1,0:T(8,128)(2,1)}) custom-call(bf16[64,96,128]{2,1,0:T(8,128)(2,1)} %bitcast.25, bf16[3072,512]{1,0:T(8,128)(2,1)} %bitcast.13, bf16[3072,512]{1,0:T(8,128)(2,1)} %bitcast.17, bf16[512,3072]{1,0:T(8,128)(2,1)} %bitcast.21), custom_call_target="tpu_custom_call" | custom-call | flops 2415919104 | bytes 13369344 | tf_op jit(solution)/shard_map/pallas_call | solution.py:242
  123.3 4.4 %shard_map.79 = bf16[128,3072]{1,0:T(8,128)(2,1)} custom-call(bf16[128,3072]{1,0:T(8,128)(2,1)} %get-tuple-element.16.x_ref), custom_call_target="tpu_custom_call" | custom-call | tf_op jit(solution)/shard_map/pallas_call | solution.py:321
  127.8 1.3 add_convert_fusion.2
  129.1 1.2 reshape.195.x_ref
  130.3 24.6 %shard_map.80 = bf16[32,96,128]{2,1,0:T(8,128)(2,1)} custom-call(bf16[32,96,128]{2,1,0:T(8,128)(2,1)} %reshape.195.x_ref), custom_call_target="tpu_custom_call" | custom-call | tf_op jit(solution)/shard_map/pallas_call | solution.py:89
  154.9 1.3 convert_element_type.86
  156.5 4.1 %collective-permute-start.1 = (bf16[3,2,3072]{2,1,0:T(2,128)(2,1)S(1)}, bf16[3,2,3072]{2,1,0:T(2,128)(2,1)S(1)}, u32[]{:S(2)}, u32[]{:S(2)}) collective-permute-start(bf16[3,2,3072]{2,1,0:T(2,128)(2,1)S(1)} %fusion.7), channel_id=1, source_target_pairs={{0,64},{64,128},{128,192},{1,65},{65,129},{129,193},{2,66},{66,130... | collective-permute-start | bytes 110600 | tf_op jit(solution)/shard_map/ppermute | solution.py:17
  160.7 1.0 collective-permute-done.1
  162.7 29.3 %shard_map.81 = bf16[2,8,4,96,128]{4,3,2,1,0:T(8,128)(2,1)} custom-call(bf16[2,96,128]{2,1,0:T(8,128)(2,1)} %pad_maximum_fusion.2.x_ref), custom_call_target="tpu_custom_call" | custom-call | tf_op jit(solution)/shard_map/pallas_call | solution.py:190
  191.9 9.9 %shard_map.82 = (f32[128,3072]{1,0:T(8,128)}, bf16[128,3072]{1,0:T(8,128)(2,1)}) custom-call(bf16[64,96,128]{2,1,0:T(8,128)(2,1)} %bitcast.26, bf16[3072,512]{1,0:T(8,128)(2,1)} %bitcast.14, bf16[3072,512]{1,0:T(8,128)(2,1)} %bitcast.18, bf16[512,3072]{1,0:T(8,128)(2,1)} %bitcast.22), custom_call_target="tpu_custom_call" | custom-call | flops 2415919104 | bytes 13369344 | tf_op jit(solution)/shard_map/pallas_call | solution.py:242
  201.8 4.4 %shard_map.83 = bf16[128,3072]{1,0:T(8,128)(2,1)} custom-call(bf16[128,3072]{1,0:T(8,128)(2,1)} %get-tuple-element.18.x_ref), custom_call_target="tpu_custom_call" | custom-call | tf_op jit(solution)/shard_map/pallas_call | solution.py:321
  206.3 1.3 add_convert_fusion.1
  207.6 1.2 reshape.197.x_ref
  208.8 25.4 %shard_map.84 = bf16[32,96,128]{2,1,0:T(8,128)(2,1)} custom-call(bf16[32,96,128]{2,1,0:T(8,128)(2,1)} %reshape.197.x_ref), custom_call_target="tpu_custom_call" | custom-call | tf_op jit(solution)/shard_map/pallas_call | solution.py:89
  234.2 1.3 convert_element_type.92
  235.8 4.0 %collective-permute-start.2 = (bf16[3,2,3072]{2,1,0:T(2,128)(2,1)S(1)}, bf16[3,2,3072]{2,1,0:T(2,128)(2,1)S(1)}, u32[]{:S(2)}, u32[]{:S(2)}) collective-permute-start(bf16[3,2,3072]{2,1,0:T(2,128)(2,1)S(1)} %fusion.11), channel_id=1, source_target_pairs={{0,64},{64,128},{128,192},{1,65},{65,129},{129,193},{2,66},{66,130... | collective-permute-start | bytes 110600 | tf_op jit(solution)/shard_map/ppermute | solution.py:17
  241.6 28.2 %shard_map.85 = bf16[2,8,4,96,128]{4,3,2,1,0:T(8,128)(2,1)} custom-call(bf16[2,96,128]{2,1,0:T(8,128)(2,1)} %pad_maximum_fusion.3.x_ref), custom_call_target="tpu_custom_call" | custom-call | tf_op jit(solution)/shard_map/pallas_call | solution.py:190
  269.8 9.9 %shard_map.86 = (f32[128,3072]{1,0:T(8,128)}, bf16[128,3072]{1,0:T(8,128)(2,1)}) custom-call(bf16[64,96,128]{2,1,0:T(8,128)(2,1)} %bitcast.27, bf16[3072,512]{1,0:T(8,128)(2,1)} %bitcast.15, bf16[3072,512]{1,0:T(8,128)(2,1)} %bitcast.19, bf16[512,3072]{1,0:T(8,128)(2,1)} %bitcast.23), custom_call_target="tpu_custom_call" | custom-call | flops 2415919104 | bytes 13369344 | tf_op jit(solution)/shard_map/pallas_call | solution.py:242
  279.7 4.4 %shard_map.87 = bf16[128,3072]{1,0:T(8,128)(2,1)} custom-call(bf16[128,3072]{1,0:T(8,128)(2,1)} %get-tuple-element.20.x_ref), custom_call_target="tpu_custom_call" | custom-call | tf_op jit(solution)/shard_map/pallas_call | solution.py:321
  284.1 1.3 add_convert_fusion
  285.4 1.2 reshape.199.x_ref
  286.6 26.8 %shard_map.88 = bf16[32,96,128]{2,1,0:T(8,128)(2,1)} custom-call(bf16[32,96,128]{2,1,0:T(8,128)(2,1)} %reshape.199.x_ref), custom_call_target="tpu_custom_call" | custom-call | tf_op jit(solution)/shard_map/pallas_call | solution.py:89
  313.5 1.3 convert_element_type.98
  (69 shorter events, 8.9 us)
Async XLA Ops:
  44.1 4.4 %copy-start = (f32[128,3072]{1,0:T(8,128)S(1)}, f32[128,3072]{1,0:T(8,128)}, u32[]{:S(2)}) copy-start(f32[128,3072]{1,0:T(8,128)} %get-tuple-element.13) | copy-start | bytes 4718596
  79.3 0.9 copy-start.6
  79.3 0.9 copy-start.4
  79.3 5.3 %copy-start.5 = (f32[1,3072]{1,0:T(1,128)S(1)}, f32[1,3072]{1,0:T(1,128)}, u32[]{:S(2)}) copy-start(f32[1,3072]{1,0:T(1,128)} %param.8) | copy-start | bytes 36868
  80.3 4.1 %collective-permute-start = (bf16[3,2,3072]{2,1,0:T(2,128)(2,1)S(1)}, bf16[3,2,3072]{2,1,0:T(2,128)(2,1)S(1)}, u32[]{:S(2)}, u32[]{:S(2)}) collective-permute-start(bf16[3,2,3072]{2,1,0:T(2,128)(2,1)S(1)} %fusion.3), channel_id=1, source_target_pairs={{0,64},{64,128},{128,192},{1,65},{65,129},{129,193},{2,66},{66,130... | collective-permute-start | bytes 110600 | tf_op jit(solution)/shard_map/ppermute | solution.py:17
  123.3 4.4 %copy-start.1 = (f32[128,3072]{1,0:T(8,128)S(1)}, f32[128,3072]{1,0:T(8,128)}, u32[]{:S(2)}) copy-start(f32[128,3072]{1,0:T(8,128)} %get-tuple-element.15) | copy-start | bytes 4718596
  156.5 5.2 %collective-permute-start.1 = (bf16[3,2,3072]{2,1,0:T(2,128)(2,1)S(1)}, bf16[3,2,3072]{2,1,0:T(2,128)(2,1)S(1)}, u32[]{:S(2)}, u32[]{:S(2)}) collective-permute-start(bf16[3,2,3072]{2,1,0:T(2,128)(2,1)S(1)} %fusion.7), channel_id=1, source_target_pairs={{0,64},{64,128},{128,192},{1,65},{65,129},{129,193},{2,66},{66,130... | collective-permute-start | bytes 110600 | tf_op jit(solution)/shard_map/ppermute | solution.py:17
  201.8 4.4 %copy-start.2 = (f32[128,3072]{1,0:T(8,128)S(1)}, f32[128,3072]{1,0:T(8,128)}, u32[]{:S(2)}) copy-start(f32[128,3072]{1,0:T(8,128)} %get-tuple-element.17) | copy-start | bytes 4718596
  235.8 4.8 %collective-permute-start.2 = (bf16[3,2,3072]{2,1,0:T(2,128)(2,1)S(1)}, bf16[3,2,3072]{2,1,0:T(2,128)(2,1)S(1)}, u32[]{:S(2)}, u32[]{:S(2)}) collective-permute-start(bf16[3,2,3072]{2,1,0:T(2,128)(2,1)S(1)} %fusion.11), channel_id=1, source_target_pairs={{0,64},{64,128},{128,192},{1,65},{65,129},{129,193},{2,66},{66,130... | collective-permute-start | bytes 110600 | tf_op jit(solution)/shard_map/ppermute | solution.py:17
  279.7 4.4 %copy-start.3 = (f32[128,3072]{1,0:T(8,128)S(1)}, f32[128,3072]{1,0:T(8,128)}, u32[]{:S(2)}) copy-start(f32[128,3072]{1,0:T(8,128)} %get-tuple-element.19) | copy-start | bytes 4718596

commit v14 on v13

--- a/solution.py
+++ b/solution.py
@@ -205,7 +205,8 @@
     )(pieces)
 
 
-def expert_kernel(x_ref, gate_ref, up_ref, down_ref, own_ref, other_ref, acc_ref, rows_ref):
+def expert_kernel(single, x_ref, gate_ref, up_ref, down_ref, own_ref, other_ref, *scratch):
+    acc_ref, rows_ref = (None,) + scratch if single else scratch
     step, last = pl.program_id(0), pl.num_programs(0) - 1
 
     @pl.when(step == 0)
@@ -218,6 +219,10 @@
     hidden = (gate_val / (1.0 + jnp.exp(-gate_val)) * up_val).astype(jnp.bfloat16)
     term = jnp.dot(hidden, down_ref[...], preferred_element_type=jnp.float32)
     half = own_ref.shape[0]
+    if acc_ref is None:
+        own_ref[...] = term[:half]
+        other_ref[...] = term[half:].astype(other_ref.dtype)
+        return
 
     @pl.when(step == 0)
     def _():
@@ -234,13 +239,15 @@
         other_ref[...] = total[half:].astype(other_ref.dtype)
 
 
-def expert(rows, gate_part, up_part, down_part, chunk=256):
+def expert(rows, gate_part, up_part, down_part, chunk=512):
     width = gate_part.shape[0]
     count = rows.size // width
     hidden = gate_part.shape[1]
     half = count // 2
-    return pl.pallas_call(
-        expert_kernel,
+    single = hidden == chunk
+    accumulator = [] if single else [pltpu.VMEM((count, width), jnp.float32)]
+    return pl.pallas_call(
+        functools.partial(expert_kernel, single),
         out_shape=(
             jax.ShapeDtypeStruct((half, width), jnp.float32),
             jax.ShapeDtypeStruct((half, width), jnp.bfloat16),
@@ -256,7 +263,7 @@
             pl.BlockSpec((half, width), lambda k: (0, 0)),
             pl.BlockSpec((half, width), lambda k: (0, 0)),
         ),
-        scratch_shapes=[pltpu.VMEM((count, width), jnp.float32), pltpu.VMEM((count, width), rows.dtype)],
+        scratch_shapes=accumulator + [pltpu.VMEM((count, width), rows.dtype)],
         compiler_params=pltpu.CompilerParams(dimension_semantics=("arbitrary",)),
         cost_estimate=pl.CostEstimate(
             flops=6 * count * width * hidden,

time: 320 us -> 317 us (level)
  no operation moved by 1% of the time
where the time goes in v14:
time: 317 us; the launch traced here: 314 us
  Pallas kernels  276 us (87%)
  other arithmetic  16.9 us (5%)
  starting transfers between devices  11.3 us (4%)
  local copies, waits for them, and re-layouts  5.6 us (2%)
    pallas_call x4, Pallas kernels, ring_gather(): pl.pallas_call(functools.partial(ring_gather_kernel, ring_y, ring_z), out...  117 us
    pallas_call x4, Pallas kernels, chip_exchange(): pl.pallas_call(functools.partial(chip_exchange_kernel, ring_y, ring_z, pe...  104 us
    pallas_call x4, Pallas kernels, expert(): pl.pallas_call(functools.partial(expert_kernel, single), out_shape=(jax.S...  37.5 us
    pallas_call x4, Pallas kernels, pair_send(): pl.pallas_call(pair_send_kernel, out_shape=jax.ShapeDtypeStruct(value.sha...  17.7 us
    ppermute x3, starting transfers between devices, shifted(): lax.ppermute(value, axis, [(source, source + steps) for source in range(i...  11.3 us
  transfers between devices with their start and end apart: 3, of which 3 were waited for; matrix products, arithmetic and copies ran while one was open for 0% of the time, Pallas kernels for 0%

profile of v14, /device:TPU:1, one launch (start us, length us, event | category | flops | bytes accessed | tf_op | source)
XLA Modules:
  0.0 314.3 jit_solution(1350174183174817372)
XLA Ops:
  2.5 31.7 %shard_map.73 = bf16[2,8,4,96,128]{4,3,2,1,0:T(8,128)(2,1)} custom-call(bf16[2,96,128]{2,1,0:T(8,128)(2,1)} %pad_maximum_fusion.x_ref), custom_call_target="tpu_custom_call" | custom-call | tf_op jit(solution)/shard_map/pallas_call | solution.py:190
  34.2 9.4 %shard_map.74 = (f32[128,3072]{1,0:T(8,128)}, bf16[128,3072]{1,0:T(8,128)(2,1)}) custom-call(bf16[64,96,128]{2,1,0:T(8,128)(2,1)} %bitcast.24, bf16[3072,512]{1,0:T(8,128)(2,1)} %bitcast.12, bf16[3072,512]{1,0:T(8,128)(2,1)} %bitcast.16, bf16[512,3072]{1,0:T(8,128)(2,1)} %bitcast.20), custom_call_target="tpu_custom_call" | custom-call | flops 2415919104 | bytes 13369344 | tf_op jit(solution)/shard_map/pallas_call | solution.py:249
  43.6 4.4 %shard_map.75 = bf16[128,3072]{1,0:T(8,128)(2,1)} custom-call(bf16[128,3072]{1,0:T(8,128)(2,1)} %get-tuple-element.14.x_ref), custom_call_target="tpu_custom_call" | custom-call | tf_op jit(solution)/shard_map/pallas_call | solution.py:328
  48.0 1.3 add_convert_fusion.3
  49.3 1.2 reshape.193.x_ref
  50.5 26.9 %shard_map.76 = bf16[32,96,128]{2,1,0:T(8,128)(2,1)} custom-call(bf16[32,96,128]{2,1,0:T(8,128)(2,1)} %reshape.193.x_ref), custom_call_target="tpu_custom_call" | custom-call | tf_op jit(solution)/shard_map/pallas_call | solution.py:89
  77.4 1.3 convert_element_type.80
  79.8 3.1 collective-permute-start
  82.9 1.0 collective-permute-done
  84.9 27.9 %shard_map.77 = bf16[2,8,4,96,128]{4,3,2,1,0:T(8,128)(2,1)} custom-call(bf16[2,96,128]{2,1,0:T(8,128)(2,1)} %pad_maximum_fusion.1.x_ref), custom_call_target="tpu_custom_call" | custom-call | tf_op jit(solution)/shard_map/pallas_call | solution.py:190
  112.9 9.4 %shard_map.78 = (f32[128,3072]{1,0:T(8,128)}, bf16[128,3072]{1,0:T(8,128)(2,1)}) custom-call(bf16[64,96,128]{2,1,0:T(8,128)(2,1)} %bitcast.25, bf16[3072,512]{1,0:T(8,128)(2,1)} %bitcast.13, bf16[3072,512]{1,0:T(8,128)(2,1)} %bitcast.17, bf16[512,3072]{1,0:T(8,128)(2,1)} %bitcast.21), custom_call_target="tpu_custom_call" | custom-call | flops 2415919104 | bytes 13369344 | tf_op jit(solution)/shard_map/pallas_call | solution.py:249
  122.3 4.4 %shard_map.79 = bf16[128,3072]{1,0:T(8,128)(2,1)} custom-call(bf16[128,3072]{1,0:T(8,128)(2,1)} %get-tuple-element.16.x_ref), custom_call_target="tpu_custom_call" | custom-call | tf_op jit(solution)/shard_map/pallas_call | solution.py:328
  126.7 1.3 add_convert_fusion.2
  128.0 1.2 reshape.195.x_ref
  129.2 24.6 %shard_map.80 = bf16[32,96,128]{2,1,0:T(8,128)(2,1)} custom-call(bf16[32,96,128]{2,1,0:T(8,128)(2,1)} %reshape.195.x_ref), custom_call_target="tpu_custom_call" | custom-call | tf_op jit(solution)/shard_map/pallas_call | solution.py:89
  153.9 1.3 convert_element_type.86
  155.5 4.2 %collective-permute-start.1 = (bf16[3,2,3072]{2,1,0:T(2,128)(2,1)S(1)}, bf16[3,2,3072]{2,1,0:T(2,128)(2,1)S(1)}, u32[]{:S(2)}, u32[]{:S(2)}) collective-permute-start(bf16[3,2,3072]{2,1,0:T(2,128)(2,1)S(1)} %fusion.7), channel_id=1, source_target_pairs={{0,64},{64,128},{128,192},{1,65},{65,129},{129,193},{2,66},{66,130... | collective-permute-start | bytes 110600 | tf_op jit(solution)/shard_map/ppermute | solution.py:17
  161.6 29.5 %shard_map.81 = bf16[2,8,4,96,128]{4,3,2,1,0:T(8,128)(2,1)} custom-call(bf16[2,96,128]{2,1,0:T(8,128)(2,1)} %pad_maximum_fusion.2.x_ref), custom_call_target="tpu_custom_call" | custom-call | tf_op jit(solution)/shard_map/pallas_call | solution.py:190
  191.1 9.4 %shard_map.82 = (f32[128,3072]{1,0:T(8,128)}, bf16[128,3072]{1,0:T(8,128)(2,1)}) custom-call(bf16[64,96,128]{2,1,0:T(8,128)(2,1)} %bitcast.26, bf16[3072,512]{1,0:T(8,128)(2,1)} %bitcast.14, bf16[3072,512]{1,0:T(8,128)(2,1)} %bitcast.18, bf16[512,3072]{1,0:T(8,128)(2,1)} %bitcast.22), custom_call_target="tpu_custom_call" | custom-call | flops 2415919104 | bytes 13369344 | tf_op jit(solution)/shard_map/pallas_call | solution.py:249
  200.5 4.4 %shard_map.83 = bf16[128,3072]{1,0:T(8,128)(2,1)} custom-call(bf16[128,3072]{1,0:T(8,128)(2,1)} %get-tuple-element.18.x_ref), custom_call_target="tpu_custom_call" | custom-call | tf_op jit(solution)/shard_map/pallas_call | solution.py:328
  204.9 1.3 add_convert_fusion.1
  206.2 1.2 reshape.197.x_ref
  207.4 25.1 %shard_map.84 = bf16[32,96,128]{2,1,0:T(8,128)(2,1)} custom-call(bf16[32,96,128]{2,1,0:T(8,128)(2,1)} %reshape.197.x_ref), custom_call_target="tpu_custom_call" | custom-call | tf_op jit(solution)/shard_map/pallas_call | solution.py:89
  232.5 1.3 convert_element_type.92
  234.1 4.0 %collective-permute-start.2 = (bf16[3,2,3072]{2,1,0:T(2,128)(2,1)S(1)}, bf16[3,2,3072]{2,1,0:T(2,128)(2,1)S(1)}, u32[]{:S(2)}, u32[]{:S(2)}) collective-permute-start(bf16[3,2,3072]{2,1,0:T(2,128)(2,1)S(1)} %fusion.11), channel_id=1, source_target_pairs={{0,64},{64,128},{128,192},{1,65},{65,129},{129,193},{2,66},{66,130... | collective-permute-start | bytes 110600 | tf_op jit(solution)/shard_map/ppermute | solution.py:17
  240.1 28.2 %shard_map.85 = bf16[2,8,4,96,128]{4,3,2,1,0:T(8,128)(2,1)} custom-call(bf16[2,96,128]{2,1,0:T(8,128)(2,1)} %pad_maximum_fusion.3.x_ref), custom_call_target="tpu_custom_call" | custom-call | tf_op jit(solution)/shard_map/pallas_call | solution.py:190
  268.3 9.4 %shard_map.86 = (f32[128,3072]{1,0:T(8,128)}, bf16[128,3072]{1,0:T(8,128)(2,1)}) custom-call(bf16[64,96,128]{2,1,0:T(8,128)(2,1)} %bitcast.27, bf16[3072,512]{1,0:T(8,128)(2,1)} %bitcast.15, bf16[3072,512]{1,0:T(8,128)(2,1)} %bitcast.19, bf16[512,3072]{1,0:T(8,128)(2,1)} %bitcast.23), custom_call_target="tpu_custom_call" | custom-call | flops 2415919104 | bytes 13369344 | tf_op jit(solution)/shard_map/pallas_call | solution.py:249
  277.7 4.4 %shard_map.87 = bf16[128,3072]{1,0:T(8,128)(2,1)} custom-call(bf16[128,3072]{1,0:T(8,128)(2,1)} %get-tuple-element.20.x_ref), custom_call_target="tpu_custom_call" | custom-call | tf_op jit(solution)/shard_map/pallas_call | solution.py:328
  282.1 1.3 add_convert_fusion
  283.4 1.2 reshape.199.x_ref
  284.6 27.2 %shard_map.88 = bf16[32,96,128]{2,1,0:T(8,128)(2,1)} custom-call(bf16[32,96,128]{2,1,0:T(8,128)(2,1)} %reshape.199.x_ref), custom_call_target="tpu_custom_call" | custom-call | tf_op jit(solution)/shard_map/pallas_call | solution.py:89
  311.9 1.3 convert_element_type.98
  (69 shorter events, 9.1 us)
Async XLA Ops:
  43.6 4.4 %copy-start = (f32[128,3072]{1,0:T(8,128)S(1)}, f32[128,3072]{1,0:T(8,128)}, u32[]{:S(2)}) copy-start(f32[128,3072]{1,0:T(8,128)} %get-tuple-element.13) | copy-start | bytes 4718596
  78.7 0.9 copy-start.6
  78.7 0.9 copy-start.4
  78.8 5.3 %copy-start.5 = (f32[1,3072]{1,0:T(1,128)S(1)}, f32[1,3072]{1,0:T(1,128)}, u32[]{:S(2)}) copy-start(f32[1,3072]{1,0:T(1,128)} %param.8) | copy-start | bytes 36868
  79.8 4.2 %collective-permute-start = (bf16[3,2,3072]{2,1,0:T(2,128)(2,1)S(1)}, bf16[3,2,3072]{2,1,0:T(2,128)(2,1)S(1)}, u32[]{:S(2)}, u32[]{:S(2)}) collective-permute-start(bf16[3,2,3072]{2,1,0:T(2,128)(2,1)S(1)} %fusion.3), channel_id=1, source_target_pairs={{0,64},{64,128},{128,192},{1,65},{65,129},{129,193},{2,66},{66,130... | collective-permute-start | bytes 110600 | tf_op jit(solution)/shard_map/ppermute | solution.py:17
  122.3 4.4 %copy-start.1 = (f32[128,3072]{1,0:T(8,128)S(1)}, f32[128,3072]{1,0:T(8,128)}, u32[]{:S(2)}) copy-start(f32[128,3072]{1,0:T(8,128)} %get-tuple-element.15) | copy-start | bytes 4718596
  155.5 5.1 %collective-permute-start.1 = (bf16[3,2,3072]{2,1,0:T(2,128)(2,1)S(1)}, bf16[3,2,3072]{2,1,0:T(2,128)(2,1)S(1)}, u32[]{:S(2)}, u32[]{:S(2)}) collective-permute-start(bf16[3,2,3072]{2,1,0:T(2,128)(2,1)S(1)} %fusion.7), channel_id=1, source_target_pairs={{0,64},{64,128},{128,192},{1,65},{65,129},{129,193},{2,66},{66,130... | collective-permute-start | bytes 110600 | tf_op jit(solution)/shard_map/ppermute | solution.py:17
  200.5 4.4 %copy-start.2 = (f32[128,3072]{1,0:T(8,128)S(1)}, f32[128,3072]{1,0:T(8,128)}, u32[]{:S(2)}) copy-start(f32[128,3072]{1,0:T(8,128)} %get-tuple-element.17) | copy-start | bytes 4718596
  234.1 5.0 %collective-permute-start.2 = (bf16[3,2,3072]{2,1,0:T(2,128)(2,1)S(1)}, bf16[3,2,3072]{2,1,0:T(2,128)(2,1)S(1)}, u32[]{:S(2)}, u32[]{:S(2)}) collective-permute-start(bf16[3,2,3072]{2,1,0:T(2,128)(2,1)S(1)} %fusion.11), channel_id=1, source_target_pairs={{0,64},{64,128},{128,192},{1,65},{65,129},{129,193},{2,66},{66,130... | collective-permute-start | bytes 110600 | tf_op jit(solution)/shard_map/ppermute | solution.py:17
  277.6 4.4 %copy-start.3 = (f32[128,3072]{1,0:T(8,128)S(1)}, f32[128,3072]{1,0:T(8,128)}, u32[]{:S(2)}) copy-start(f32[128,3072]{1,0:T(8,128)} %get-tuple-element.19) | copy-start | bytes 4718596

commit v15 on v14

--- a/solution.py
+++ b/solution.py
@@ -362,9 +362,9 @@
         own_rows, other_rows = expert(block_rows, gate_part, up_part, down_part)
         chip_sum = (own_rows + pair_send(other_rows, 2).astype(jnp.float32)).astype(jnp.bfloat16)
         received = chip_exchange(chip_sum.reshape(chips, piece_rows, LANES), ring_y, ring_z, 0, 3)
-        received = received.astype(jnp.float32)
         received = received.reshape(2, chips // 2, 2, local_rows, width)
-        first, second = jnp.sum(received[0], axis=0), jnp.sum(received[1], axis=0)
+        first = jnp.sum(received[0], axis=0, dtype=jnp.float32)
+        second = jnp.sum(received[1], axis=0, dtype=jnp.float32)
         middle = jnp.where(zero_blocks >= 2, first[1], second[0])
         mixed = jnp.stack([first[0], middle, second[1]])
         updated = (carried.astype(jnp.float32) + probs[:, :, None] * mixed).astype(jnp.bfloat16)

time: 317 us -> 316 us (level)
    convert_element_type x4 -> x0, other arithmetic: 5.23 us -> none  [shards(): received = received.astype(jnp.float32)]
    reduce_sum x4, other arithmetic: 0.31 us -> 4.92 us  [shards(): first = jnp.sum(received[0], axis=0, dtype=jnp.float32)]
where the time goes in v15:
time: 316 us; the launch traced here: 314 us
  Pallas kernels  276 us (87%)
  other arithmetic  16.3 us (5%)
  starting transfers between devices  11.3 us (4%)
  local copies, waits for them, and re-layouts  5.6 us (2%)
    pallas_call x4, Pallas kernels, ring_gather(): pl.pallas_call(functools.partial(ring_gather_kernel, ring_y, ring_z), out...  117 us
    pallas_call x4, Pallas kernels, chip_exchange(): pl.pallas_call(functools.partial(chip_exchange_kernel, ring_y, ring_z, pe...  104 us
    pallas_call x4, Pallas kernels, expert(): pl.pallas_call(functools.partial(expert_kernel, single), out_shape=(jax.S...  37.5 us
    pallas_call x4, Pallas kernels, pair_send(): pl.pallas_call(pair_send_kernel, out_shape=jax.ShapeDtypeStruct(value.sha...  17.7 us
    ppermute x3, starting transfers between devices, shifted(): lax.ppermute(value, axis, [(source, source + steps) for source in range(i...  11.3 us
  transfers between devices with their start and end apart: 3, of which 3 were waited for; matrix products, arithmetic and copies ran while one was open for 0% of the time, Pallas kernels for 0%

profile of v15, /device:TPU:1, one launch (start us, length us, event | category | flops | bytes accessed | tf_op | source)
XLA Modules:
  0.0 313.8 jit_solution(10797015442740026526)
XLA Ops:
  2.5 31.7 %shard_map.73 = bf16[2,8,4,96,128]{4,3,2,1,0:T(8,128)(2,1)} custom-call(bf16[2,96,128]{2,1,0:T(8,128)(2,1)} %pad_maximum_fusion.x_ref), custom_call_target="tpu_custom_call" | custom-call | tf_op jit(solution)/shard_map/pallas_call | solution.py:190
  34.2 9.4 %shard_map.74 = (f32[128,3072]{1,0:T(8,128)}, bf16[128,3072]{1,0:T(8,128)(2,1)}) custom-call(bf16[64,96,128]{2,1,0:T(8,128)(2,1)} %bitcast.24, bf16[3072,512]{1,0:T(8,128)(2,1)} %bitcast.12, bf16[3072,512]{1,0:T(8,128)(2,1)} %bitcast.16, bf16[512,3072]{1,0:T(8,128)(2,1)} %bitcast.20), custom_call_target="tpu_custom_call" | custom-call | flops 2415919104 | bytes 13369344 | tf_op jit(solution)/shard_map/pallas_call | solution.py:249
  43.6 4.4 %shard_map.75 = bf16[128,3072]{1,0:T(8,128)(2,1)} custom-call(bf16[128,3072]{1,0:T(8,128)(2,1)} %get-tuple-element.14.x_ref), custom_call_target="tpu_custom_call" | custom-call | tf_op jit(solution)/shard_map/pallas_call | solution.py:328
  48.0 1.3 add_convert_fusion.3
  49.3 1.2 reshape.193.x_ref
  50.5 26.9 %shard_map.76 = bf16[32,96,128]{2,1,0:T(8,128)(2,1)} custom-call(bf16[32,96,128]{2,1,0:T(8,128)(2,1)} %reshape.193.x_ref), custom_call_target="tpu_custom_call" | custom-call | tf_op jit(solution)/shard_map/pallas_call | solution.py:89
  77.4 1.2 convert_reduce_fusion.7
  79.6 3.1 collective-permute-start
  82.7 1.0 collective-permute-done
  84.8 27.9 %shard_map.77 = bf16[2,8,4,96,128]{4,3,2,1,0:T(8,128)(2,1)} custom-call(bf16[2,96,128]{2,1,0:T(8,128)(2,1)} %pad_maximum_fusion.1.x_ref), custom_call_target="tpu_custom_call" | custom-call | tf_op jit(solution)/shard_map/pallas_call | solution.py:190
  112.7 9.4 %shard_map.78 = (f32[128,3072]{1,0:T(8,128)}, bf16[128,3072]{1,0:T(8,128)(2,1)}) custom-call(bf16[64,96,128]{2,1,0:T(8,128)(2,1)} %bitcast.25, bf16[3072,512]{1,0:T(8,128)(2,1)} %bitcast.13, bf16[3072,512]{1,0:T(8,128)(2,1)} %bitcast.17, bf16[512,3072]{1,0:T(8,128)(2,1)} %bitcast.21), custom_call_target="tpu_custom_call" | custom-call | flops 2415919104 | bytes 13369344 | tf_op jit(solution)/shard_map/pallas_call | solution.py:249
  122.1 4.4 %shard_map.79 = bf16[128,3072]{1,0:T(8,128)(2,1)} custom-call(bf16[128,3072]{1,0:T(8,128)(2,1)} %get-tuple-element.16.x_ref), custom_call_target="tpu_custom_call" | custom-call | tf_op jit(solution)/shard_map/pallas_call | solution.py:328
  126.5 1.3 add_convert_fusion.2
  127.8 1.2 reshape.195.x_ref
  129.1 24.6 %shard_map.80 = bf16[32,96,128]{2,1,0:T(8,128)(2,1)} custom-call(bf16[32,96,128]{2,1,0:T(8,128)(2,1)} %reshape.195.x_ref), custom_call_target="tpu_custom_call" | custom-call | tf_op jit(solution)/shard_map/pallas_call | solution.py:89
  153.7 1.2 convert_reduce_fusion.5
  155.1 4.2 %collective-permute-start.1 = (bf16[3,2,3072]{2,1,0:T(2,128)(2,1)S(1)}, bf16[3,2,3072]{2,1,0:T(2,128)(2,1)S(1)}, u32[]{:S(2)}, u32[]{:S(2)}) collective-permute-start(bf16[3,2,3072]{2,1,0:T(2,128)(2,1)S(1)} %fusion.7), channel_id=1, source_target_pairs={{0,64},{64,128},{128,192},{1,65},{65,129},{129,193},{2,66},{66,130... | collective-permute-start | bytes 110600 | tf_op jit(solution)/shard_map/ppermute | solution.py:17
  161.2 29.5 %shard_map.81 = bf16[2,8,4,96,128]{4,3,2,1,0:T(8,128)(2,1)} custom-call(bf16[2,96,128]{2,1,0:T(8,128)(2,1)} %pad_maximum_fusion.2.x_ref), custom_call_target="tpu_custom_call" | custom-call | tf_op jit(solution)/shard_map/pallas_call | solution.py:190
  190.7 9.4 %shard_map.82 = (f32[128,3072]{1,0:T(8,128)}, bf16[128,3072]{1,0:T(8,128)(2,1)}) custom-call(bf16[64,96,128]{2,1,0:T(8,128)(2,1)} %bitcast.26, bf16[3072,512]{1,0:T(8,128)(2,1)} %bitcast.14, bf16[3072,512]{1,0:T(8,128)(2,1)} %bitcast.18, bf16[512,3072]{1,0:T(8,128)(2,1)} %bitcast.22), custom_call_target="tpu_custom_call" | custom-call | flops 2415919104 | bytes 13369344 | tf_op jit(solution)/shard_map/pallas_call | solution.py:249
  200.1 4.4 %shard_map.83 = bf16[128,3072]{1,0:T(8,128)(2,1)} custom-call(bf16[128,3072]{1,0:T(8,128)(2,1)} %get-tuple-element.18.x_ref), custom_call_target="tpu_custom_call" | custom-call | tf_op jit(solution)/shard_map/pallas_call | solution.py:328
  204.6 1.3 add_convert_fusion.1
  205.8 1.2 reshape.197.x_ref
  207.1 25.1 %shard_map.84 = bf16[32,96,128]{2,1,0:T(8,128)(2,1)} custom-call(bf16[32,96,128]{2,1,0:T(8,128)(2,1)} %reshape.197.x_ref), custom_call_target="tpu_custom_call" | custom-call | tf_op jit(solution)/shard_map/pallas_call | solution.py:89
  232.2 1.2 convert_reduce_fusion.3
  233.6 4.0 %collective-permute-start.2 = (bf16[3,2,3072]{2,1,0:T(2,128)(2,1)S(1)}, bf16[3,2,3072]{2,1,0:T(2,128)(2,1)S(1)}, u32[]{:S(2)}, u32[]{:S(2)}) collective-permute-start(bf16[3,2,3072]{2,1,0:T(2,128)(2,1)S(1)} %fusion.11), channel_id=1, source_target_pairs={{0,64},{64,128},{128,192},{1,65},{65,129},{129,193},{2,66},{66,130... | collective-permute-start | bytes 110600 | tf_op jit(solution)/shard_map/ppermute | solution.py:17
  239.6 28.2 %shard_map.85 = bf16[2,8,4,96,128]{4,3,2,1,0:T(8,128)(2,1)} custom-call(bf16[2,96,128]{2,1,0:T(8,128)(2,1)} %pad_maximum_fusion.3.x_ref), custom_call_target="tpu_custom_call" | custom-call | tf_op jit(solution)/shard_map/pallas_call | solution.py:190
  267.8 9.4 %shard_map.86 = (f32[128,3072]{1,0:T(8,128)}, bf16[128,3072]{1,0:T(8,128)(2,1)}) custom-call(bf16[64,96,128]{2,1,0:T(8,128)(2,1)} %bitcast.27, bf16[3072,512]{1,0:T(8,128)(2,1)} %bitcast.15, bf16[3072,512]{1,0:T(8,128)(2,1)} %bitcast.19, bf16[512,3072]{1,0:T(8,128)(2,1)} %bitcast.23), custom_call_target="tpu_custom_call" | custom-call | flops 2415919104 | bytes 13369344 | tf_op jit(solution)/shard_map/pallas_call | solution.py:249
  277.2 4.4 %shard_map.87 = bf16[128,3072]{1,0:T(8,128)(2,1)} custom-call(bf16[128,3072]{1,0:T(8,128)(2,1)} %get-tuple-element.20.x_ref), custom_call_target="tpu_custom_call" | custom-call | tf_op jit(solution)/shard_map/pallas_call | solution.py:328
  281.7 1.3 add_convert_fusion
  282.9 1.2 reshape.199.x_ref
  284.2 27.4 %shard_map.88 = bf16[32,96,128]{2,1,0:T(8,128)(2,1)} custom-call(bf16[32,96,128]{2,1,0:T(8,128)(2,1)} %reshape.199.x_ref), custom_call_target="tpu_custom_call" | custom-call | tf_op jit(solution)/shard_map/pallas_call | solution.py:89
  311.5 1.2 convert_reduce_fusion.1
  (65 shorter events, 8.8 us)
Async XLA Ops:
  43.6 4.4 %copy-start = (f32[128,3072]{1,0:T(8,128)S(1)}, f32[128,3072]{1,0:T(8,128)}, u32[]{:S(2)}) copy-start(f32[128,3072]{1,0:T(8,128)} %get-tuple-element.13) | copy-start | bytes 4718596
  50.5 28.9 %copy-start.6 = (f32[1,3,2]{1,2,0:T(2,128)S(1)}, f32[1,3,2]{1,2,0:T(2,128)}, u32[]{:S(2)}) copy-start(f32[1,3,2]{1,2,0:T(2,128)} %param.13) | copy-start | bytes 76
  50.5 29.0 %copy-start.4 = (bf16[3,2,3072]{2,1,0:T(2,128)(2,1)S(1)}, bf16[3,2,3072]{2,1,0:T(2,128)(2,1)}, u32[]{:S(2)}) copy-start(bf16[3,2,3072]{2,1,0:T(2,128)(2,1)} %param.7) | copy-start | bytes 110596
  50.5 33.4 %copy-start.5 = (f32[1,3072]{1,0:T(1,128)S(1)}, f32[1,3072]{1,0:T(1,128)}, u32[]{:S(2)}) copy-start(f32[1,3072]{1,0:T(1,128)} %param.8) | copy-start | bytes 36868
  79.6 4.2 %collective-permute-start = (bf16[3,2,3072]{2,1,0:T(2,128)(2,1)S(1)}, bf16[3,2,3072]{2,1,0:T(2,128)(2,1)S(1)}, u32[]{:S(2)}, u32[]{:S(2)}) collective-permute-start(bf16[3,2,3072]{2,1,0:T(2,128)(2,1)S(1)} %fusion.3), channel_id=1, source_target_pairs={{0,64},{64,128},{128,192},{1,65},{65,129},{129,193},{2,66},{66,130... | collective-permute-start | bytes 110600 | tf_op jit(solution)/shard_map/ppermute | solution.py:17
  122.1 4.4 %copy-start.1 = (f32[128,3072]{1,0:T(8,128)S(1)}, f32[128,3072]{1,0:T(8,128)}, u32[]{:S(2)}) copy-start(f32[128,3072]{1,0:T(8,128)} %get-tuple-element.15) | copy-start | bytes 4718596
  155.1 5.1 %collective-permute-start.1 = (bf16[3,2,3072]{2,1,0:T(2,128)(2,1)S(1)}, bf16[3,2,3072]{2,1,0:T(2,128)(2,1)S(1)}, u32[]{:S(2)}, u32[]{:S(2)}) collective-permute-start(bf16[3,2,3072]{2,1,0:T(2,128)(2,1)S(1)} %fusion.7), channel_id=1, source_target_pairs={{0,64},{64,128},{128,192},{1,65},{65,129},{129,193},{2,66},{66,130... | collective-permute-start | bytes 110600 | tf_op jit(solution)/shard_map/ppermute | solution.py:17
  200.1 4.4 %copy-start.2 = (f32[128,3072]{1,0:T(8,128)S(1)}, f32[128,3072]{1,0:T(8,128)}, u32[]{:S(2)}) copy-start(f32[128,3072]{1,0:T(8,128)} %get-tuple-element.17) | copy-start | bytes 4718596
  233.6 5.0 %collective-permute-start.2 = (bf16[3,2,3072]{2,1,0:T(2,128)(2,1)S(1)}, bf16[3,2,3072]{2,1,0:T(2,128)(2,1)S(1)}, u32[]{:S(2)}, u32[]{:S(2)}) collective-permute-start(bf16[3,2,3072]{2,1,0:T(2,128)(2,1)S(1)} %fusion.11), channel_id=1, source_target_pairs={{0,64},{64,128},{128,192},{1,65},{65,129},{129,193},{2,66},{66,130... | collective-permute-start | bytes 110600 | tf_op jit(solution)/shard_map/ppermute | solution.py:17
  277.2 4.4 %copy-start.3 = (f32[128,3072]{1,0:T(8,128)S(1)}, f32[128,3072]{1,0:T(8,128)}, u32[]{:S(2)}) copy-start(f32[128,3072]{1,0:T(8,128)} %get-tuple-element.19) | copy-start | bytes 4718596

commit v16 on v15

--- a/solution.py
+++ b/solution.py
@@ -127,7 +127,8 @@
             device_id_type=pl.DeviceIdType.MESH,
         )
 
-    for step in range(1, ring_y):
+    y_order = [ring_y // 2] + [step for step in range(1, ring_y) if step != ring_y // 2]
+    for step in y_order:
         y_copy(lax.rem(y + step, ring_y), y).start()
     o_ref[0, z, y] = x_ref[y * 2 // ring_y]
     for step in range(1, ring_y):

time: 316 us -> 316 us (level)
  no operation moved by 1% of the time
where the time goes in v16:
time: 316 us; the launch traced here: 314 us
  Pallas kernels  276 us (87%)
  other arithmetic  16.3 us (5%)
  starting transfers between devices  11.6 us (4%)
  local copies, waits for them, and re-layouts  5.6 us (2%)
    pallas_call x4, Pallas kernels, ring_gather(): pl.pallas_call(functools.partial(ring_gather_kernel, ring_y, ring_z), out...  116 us
    pallas_call x4, Pallas kernels, chip_exchange(): pl.pallas_call(functools.partial(chip_exchange_kernel, ring_y, ring_z, pe...  105 us
    pallas_call x4, Pallas kernels, expert(): pl.pallas_call(functools.partial(expert_kernel, single), out_shape=(jax.S...  37.5 us
    pallas_call x4, Pallas kernels, pair_send(): pl.pallas_call(pair_send_kernel, out_shape=jax.ShapeDtypeStruct(value.sha...  17.7 us
    ppermute x3, starting transfers between devices, shifted(): lax.ppermute(value, axis, [(source, source + steps) for source in range(i...  11.6 us
  transfers between devices with their start and end apart: 3, of which 3 were waited for; matrix products, arithmetic and copies ran while one was open for 0% of the time, Pallas kernels for 0%

profile of v16, /device:TPU:1, one launch (start us, length us, event | category | flops | bytes accessed | tf_op | source)
XLA Modules:
  0.0 313.7 jit_solution(6054183514021773109)
XLA Ops:
  2.5 31.3 %shard_map.73 = bf16[2,8,4,96,128]{4,3,2,1,0:T(8,128)(2,1)} custom-call(bf16[2,96,128]{2,1,0:T(8,128)(2,1)} %pad_maximum_fusion.x_ref), custom_call_target="tpu_custom_call" | custom-call | tf_op jit(solution)/shard_map/pallas_call | solution.py:191
  33.9 9.4 %shard_map.74 = (f32[128,3072]{1,0:T(8,128)}, bf16[128,3072]{1,0:T(8,128)(2,1)}) custom-call(bf16[64,96,128]{2,1,0:T(8,128)(2,1)} %bitcast.24, bf16[3072,512]{1,0:T(8,128)(2,1)} %bitcast.12, bf16[3072,512]{1,0:T(8,128)(2,1)} %bitcast.16, bf16[512,3072]{1,0:T(8,128)(2,1)} %bitcast.20), custom_call_target="tpu_custom_call" | custom-call | flops 2415919104 | bytes 13369344 | tf_op jit(solution)/shard_map/pallas_call | solution.py:250
  43.2 4.4 %shard_map.75 = bf16[128,3072]{1,0:T(8,128)(2,1)} custom-call(bf16[128,3072]{1,0:T(8,128)(2,1)} %get-tuple-element.14.x_ref), custom_call_target="tpu_custom_call" | custom-call | tf_op jit(solution)/shard_map/pallas_call | solution.py:329
  47.7 1.3 add_convert_fusion.3
  49.0 1.2 reshape.193.x_ref
  50.2 27.1 %shard_map.76 = bf16[32,96,128]{2,1,0:T(8,128)(2,1)} custom-call(bf16[32,96,128]{2,1,0:T(8,128)(2,1)} %reshape.193.x_ref), custom_call_target="tpu_custom_call" | custom-call | tf_op jit(solution)/shard_map/pallas_call | solution.py:89
  77.3 1.2 convert_reduce_fusion.7
  79.5 3.1 collective-permute-start
  82.7 1.0 collective-permute-done
  84.7 27.8 %shard_map.77 = bf16[2,8,4,96,128]{4,3,2,1,0:T(8,128)(2,1)} custom-call(bf16[2,96,128]{2,1,0:T(8,128)(2,1)} %pad_maximum_fusion.1.x_ref), custom_call_target="tpu_custom_call" | custom-call | tf_op jit(solution)/shard_map/pallas_call | solution.py:191
  112.5 9.4 %shard_map.78 = (f32[128,3072]{1,0:T(8,128)}, bf16[128,3072]{1,0:T(8,128)(2,1)}) custom-call(bf16[64,96,128]{2,1,0:T(8,128)(2,1)} %bitcast.25, bf16[3072,512]{1,0:T(8,128)(2,1)} %bitcast.13, bf16[3072,512]{1,0:T(8,128)(2,1)} %bitcast.17, bf16[512,3072]{1,0:T(8,128)(2,1)} %bitcast.21), custom_call_target="tpu_custom_call" | custom-call | flops 2415919104 | bytes 13369344 | tf_op jit(solution)/shard_map/pallas_call | solution.py:250
  121.8 4.4 %shard_map.79 = bf16[128,3072]{1,0:T(8,128)(2,1)} custom-call(bf16[128,3072]{1,0:T(8,128)(2,1)} %get-tuple-element.16.x_ref), custom_call_target="tpu_custom_call" | custom-call | tf_op jit(solution)/shard_map/pallas_call | solution.py:329
  126.3 1.3 add_convert_fusion.2
  127.6 1.2 reshape.195.x_ref
  128.8 25.1 %shard_map.80 = bf16[32,96,128]{2,1,0:T(8,128)(2,1)} custom-call(bf16[32,96,128]{2,1,0:T(8,128)(2,1)} %reshape.195.x_ref), custom_call_target="tpu_custom_call" | custom-call | tf_op jit(solution)/shard_map/pallas_call | solution.py:89
  153.9 1.2 convert_reduce_fusion.5
  155.3 4.5 %collective-permute-start.1 = (bf16[3,2,3072]{2,1,0:T(2,128)(2,1)S(1)}, bf16[3,2,3072]{2,1,0:T(2,128)(2,1)S(1)}, u32[]{:S(2)}, u32[]{:S(2)}) collective-permute-start(bf16[3,2,3072]{2,1,0:T(2,128)(2,1)S(1)} %fusion.7), channel_id=1, source_target_pairs={{0,64},{64,128},{128,192},{1,65},{65,129},{129,193},{2,66},{66,130... | collective-permute-start | bytes 110600 | tf_op jit(solution)/shard_map/ppermute | solution.py:17
  161.7 29.2 %shard_map.81 = bf16[2,8,4,96,128]{4,3,2,1,0:T(8,128)(2,1)} custom-call(bf16[2,96,128]{2,1,0:T(8,128)(2,1)} %pad_maximum_fusion.2.x_ref), custom_call_target="tpu_custom_call" | custom-call | tf_op jit(solution)/shard_map/pallas_call | solution.py:191
  190.9 9.4 %shard_map.82 = (f32[128,3072]{1,0:T(8,128)}, bf16[128,3072]{1,0:T(8,128)(2,1)}) custom-call(bf16[64,96,128]{2,1,0:T(8,128)(2,1)} %bitcast.26, bf16[3072,512]{1,0:T(8,128)(2,1)} %bitcast.14, bf16[3072,512]{1,0:T(8,128)(2,1)} %bitcast.18, bf16[512,3072]{1,0:T(8,128)(2,1)} %bitcast.22), custom_call_target="tpu_custom_call" | custom-call | flops 2415919104 | bytes 13369344 | tf_op jit(solution)/shard_map/pallas_call | solution.py:250
  200.2 4.4 %shard_map.83 = bf16[128,3072]{1,0:T(8,128)(2,1)} custom-call(bf16[128,3072]{1,0:T(8,128)(2,1)} %get-tuple-element.18.x_ref), custom_call_target="tpu_custom_call" | custom-call | tf_op jit(solution)/shard_map/pallas_call | solution.py:329
  204.7 1.3 add_convert_fusion.1
  206.0 1.2 reshape.197.x_ref
  207.2 26.6 %shard_map.84 = bf16[32,96,128]{2,1,0:T(8,128)(2,1)} custom-call(bf16[32,96,128]{2,1,0:T(8,128)(2,1)} %reshape.197.x_ref), custom_call_target="tpu_custom_call" | custom-call | tf_op jit(solution)/shard_map/pallas_call | solution.py:89
  233.8 1.2 convert_reduce_fusion.3
  235.3 3.9 %collective-permute-start.2 = (bf16[3,2,3072]{2,1,0:T(2,128)(2,1)S(1)}, bf16[3,2,3072]{2,1,0:T(2,128)(2,1)S(1)}, u32[]{:S(2)}, u32[]{:S(2)}) collective-permute-start(bf16[3,2,3072]{2,1,0:T(2,128)(2,1)S(1)} %fusion.11), channel_id=1, source_target_pairs={{0,64},{64,128},{128,192},{1,65},{65,129},{129,193},{2,66},{66,130... | collective-permute-start | bytes 110600 | tf_op jit(solution)/shard_map/ppermute | solution.py:17
  241.2 27.7 %shard_map.85 = bf16[2,8,4,96,128]{4,3,2,1,0:T(8,128)(2,1)} custom-call(bf16[2,96,128]{2,1,0:T(8,128)(2,1)} %pad_maximum_fusion.3.x_ref), custom_call_target="tpu_custom_call" | custom-call | tf_op jit(solution)/shard_map/pallas_call | solution.py:191
  268.9 9.4 %shard_map.86 = (f32[128,3072]{1,0:T(8,128)}, bf16[128,3072]{1,0:T(8,128)(2,1)}) custom-call(bf16[64,96,128]{2,1,0:T(8,128)(2,1)} %bitcast.27, bf16[3072,512]{1,0:T(8,128)(2,1)} %bitcast.15, bf16[3072,512]{1,0:T(8,128)(2,1)} %bitcast.19, bf16[512,3072]{1,0:T(8,128)(2,1)} %bitcast.23), custom_call_target="tpu_custom_call" | custom-call | flops 2415919104 | bytes 13369344 | tf_op jit(solution)/shard_map/pallas_call | solution.py:250
  278.3 4.4 %shard_map.87 = bf16[128,3072]{1,0:T(8,128)(2,1)} custom-call(bf16[128,3072]{1,0:T(8,128)(2,1)} %get-tuple-element.20.x_ref), custom_call_target="tpu_custom_call" | custom-call | tf_op jit(solution)/shard_map/pallas_call | solution.py:329
  282.7 1.3 add_convert_fusion
  284.0 1.2 reshape.199.x_ref
  285.2 26.3 %shard_map.88 = bf16[32,96,128]{2,1,0:T(8,128)(2,1)} custom-call(bf16[32,96,128]{2,1,0:T(8,128)(2,1)} %reshape.199.x_ref), custom_call_target="tpu_custom_call" | custom-call | tf_op jit(solution)/shard_map/pallas_call | solution.py:89
  311.5 1.2 convert_reduce_fusion.1
  (65 shorter events, 8.8 us)
Async XLA Ops:
  43.2 4.4 %copy-start = (f32[128,3072]{1,0:T(8,128)S(1)}, f32[128,3072]{1,0:T(8,128)}, u32[]{:S(2)}) copy-start(f32[128,3072]{1,0:T(8,128)} %get-tuple-element.13) | copy-start | bytes 4718596
  50.2 29.1 %copy-start.6 = (f32[1,3,2]{1,2,0:T(2,128)S(1)}, f32[1,3,2]{1,2,0:T(2,128)}, u32[]{:S(2)}) copy-start(f32[1,3,2]{1,2,0:T(2,128)} %param.13) | copy-start | bytes 76
  50.2 29.2 %copy-start.4 = (bf16[3,2,3072]{2,1,0:T(2,128)(2,1)S(1)}, bf16[3,2,3072]{2,1,0:T(2,128)(2,1)}, u32[]{:S(2)}) copy-start(bf16[3,2,3072]{2,1,0:T(2,128)(2,1)} %param.7) | copy-start | bytes 110596
  50.2 33.6 %copy-start.5 = (f32[1,3072]{1,0:T(1,128)S(1)}, f32[1,3072]{1,0:T(1,128)}, u32[]{:S(2)}) copy-start(f32[1,3072]{1,0:T(1,128)} %param.8) | copy-start | bytes 36868
  79.5 4.2 %collective-permute-start = (bf16[3,2,3072]{2,1,0:T(2,128)(2,1)S(1)}, bf16[3,2,3072]{2,1,0:T(2,128)(2,1)S(1)}, u32[]{:S(2)}, u32[]{:S(2)}) collective-permute-start(bf16[3,2,3072]{2,1,0:T(2,128)(2,1)S(1)} %fusion.3), channel_id=1, source_target_pairs={{0,64},{64,128},{128,192},{1,65},{65,129},{129,193},{2,66},{66,130... | collective-permute-start | bytes 110600 | tf_op jit(solution)/shard_map/ppermute | solution.py:17
  121.8 4.4 %copy-start.1 = (f32[128,3072]{1,0:T(8,128)S(1)}, f32[128,3072]{1,0:T(8,128)}, u32[]{:S(2)}) copy-start(f32[128,3072]{1,0:T(8,128)} %get-tuple-element.15) | copy-start | bytes 4718596
  155.3 5.4 %collective-permute-start.1 = (bf16[3,2,3072]{2,1,0:T(2,128)(2,1)S(1)}, bf16[3,2,3072]{2,1,0:T(2,128)(2,1)S(1)}, u32[]{:S(2)}, u32[]{:S(2)}) collective-permute-start(bf16[3,2,3072]{2,1,0:T(2,128)(2,1)S(1)} %fusion.7), channel_id=1, source_target_pairs={{0,64},{64,128},{128,192},{1,65},{65,129},{129,193},{2,66},{66,130... | collective-permute-start | bytes 110600 | tf_op jit(solution)/shard_map/ppermute | solution.py:17
  200.2 4.4 %copy-start.2 = (f32[128,3072]{1,0:T(8,128)S(1)}, f32[128,3072]{1,0:T(8,128)}, u32[]{:S(2)}) copy-start(f32[128,3072]{1,0:T(8,128)} %get-tuple-element.17) | copy-start | bytes 4718596
  235.3 4.9 %collective-permute-start.2 = (bf16[3,2,3072]{2,1,0:T(2,128)(2,1)S(1)}, bf16[3,2,3072]{2,1,0:T(2,128)(2,1)S(1)}, u32[]{:S(2)}, u32[]{:S(2)}) collective-permute-start(bf16[3,2,3072]{2,1,0:T(2,128)(2,1)S(1)} %fusion.11), channel_id=1, source_target_pairs={{0,64},{64,128},{128,192},{1,65},{65,129},{129,193},{2,66},{66,130... | collective-permute-start | bytes 110600 | tf_op jit(solution)/shard_map/ppermute | solution.py:17
  278.3 4.4 %copy-start.3 = (f32[128,3072]{1,0:T(8,128)S(1)}, f32[128,3072]{1,0:T(8,128)}, u32[]{:S(2)}) copy-start(f32[128,3072]{1,0:T(8,128)} %get-tuple-element.19) | copy-start | bytes 4718596
